TPU v7x, 32 devices: a whole 2x2x4 slice. The times are simulated.
32 devices in a mesh: ctx: 8 (over y, x, core), wsh: 4 (over z).
Axes of the slice: x: 2, y: 2, z: 4, core: 2. Of those that a mesh axis runs over, the one named last changes fastest.
Arguments:
- tokens: bfloat16 [4, 2048, 768], P('wsh', 'ctx'), may hold values from -6 to 6
- chars: bfloat16 [4, 8192, 768], P('wsh', 'ctx'), may hold values from -6 to 6
- char_token: int32 [4, 8, 1024], P('wsh', 'ctx'), may hold values from 0 to 255, never falling along the last dimension, each value on 1 to 8 neighbouring positions
- doc_lengths: int32 [4, 8], P('wsh'), may hold values from 1 to 1024, 2048 in all within a row
- gain_attn: bfloat16 [768], P(('ctx', 'wsh')), may hold values from 0.5 to 1.5
- qkv_weight: bfloat16 [768, 2304], P(('ctx', 'wsh')), may hold values from -0.21875 to 0.21875
- out_weight: bfloat16 [768, 768], P(('ctx', 'wsh')), may hold values from -0.21875 to 0.21875
- gain_char: bfloat16 [768], P(('ctx', 'wsh')), may hold values from 0.5 to 1.5
- gru_weight: bfloat16 [768, 1536], P(('ctx', 'wsh')), may hold values from -0.21875 to 0.21875
- conv_weight: bfloat16 [768, 2304], P(('ctx', 'wsh')), may hold values from -0.21875 to 0.21875
- gain_merge: bfloat16 [768], P(('ctx', 'wsh')), may hold values from 0.5 to 1.5
- merge_weight: bfloat16 [768, 768], P(('ctx', 'wsh')), may hold values from -0.21875 to 0.21875
- up_weight: bfloat16 [768, 3072], P(('ctx', 'wsh')), may hold values from -0.21875 to 0.21875
- down_weight: bfloat16 [3072, 768], P(('ctx', 'wsh')), may hold values from -0.109375 to 0.109375
- cot_tokens: bfloat16 [4, 2048, 768], P('wsh', 'ctx'), may hold values from -6 to 6
- cot_chars: bfloat16 [4, 8192, 768], P('wsh', 'ctx'), may hold values from -6 to 6
Outputs:
- out_tokens: bfloat16 [4, 2048, 768], P('wsh', 'ctx')
- out_chars: bfloat16 [4, 8192, 768], P('wsh', 'ctx')
- grad_tokens: bfloat16 [4, 2048, 768], P('wsh', 'ctx')
- grad_chars: bfloat16 [4, 8192, 768], P('wsh', 'ctx')
- grad_gain_attn: float32 [768], P(('ctx', 'wsh'))
- grad_qkv: float32 [768, 2304], P(('ctx', 'wsh'))
- grad_out_proj: float32 [768, 768], P(('ctx', 'wsh'))
- grad_gain_char: float32 [768], P(('ctx', 'wsh'))
- grad_gru: float32 [768, 1536], P(('ctx', 'wsh'))
- grad_conv: float32 [768, 2304], P(('ctx', 'wsh'))
- grad_gain_merge: float32 [768], P(('ctx', 'wsh'))
- grad_merge: float32 [768, 768], P(('ctx', 'wsh'))
- grad_up: float32 [768, 3072], P(('ctx', 'wsh'))
- grad_down: float32 [3072, 768], P(('ctx', 'wsh'))
Inputs may be any that keep to these rules, and one draw needn't show every extreme that they name: `char_token`: each block of 1024 characters names its 256 tokens in order, each by 1 to 8 consecutive characters. `doc_lengths`: a sequence's document lengths sum to 2048.
All inputs are finite; a program needn't handle non-finite values.
Results may differ from a plain program's by a relative error of at most 0.02.
Values may be sent and summed in bfloat16 or wider, within the bound.
A program may use at most 320 MiB of HBM per device.

v0:
```python
import math

import jax
import jax.numpy as jnp
from jax import lax
from jax.sharding import PartitionSpec as P

HEADS = 12
HEAD_DIM = 64


masked_score = -1e30


def carried_in(value, axis, join, neutral, backward):
    count, mine = (lax.axis_size(axis), lax.axis_index(axis))
    pieces = jax.tree.map(lambda part: lax.all_gather(part, axis), value)
    if backward:
        pieces = jax.tree.map(lambda part: part[::-1], pieces)
        mine = count - 1 - mine
    running = jax.tree.map(
        lambda part, zero: jnp.full_like(part, 0) + jnp.asarray(zero, part.dtype), value, neutral
    )

    def turn(position, running):
        longer = join(running, jax.tree.map(lambda part: part[position], pieces))
        return jax.tree.map(lambda new, old: jnp.where(position < mine, new, old), longer, running)

    return lax.fori_loop(0, count - 1, turn, running)


def padded_2(cells, sides, width):
    for axis, dim in sides:
        count = lax.axis_size(axis)
        ends = count - 1
        head = lax.slice_in_dim(cells, 0, width, axis=dim)
        tail = lax.slice_in_dim(cells, cells.shape[dim] - width, cells.shape[dim], axis=dim)
        cells = jnp.concatenate(
            [
                lax.ppermute(tail, axis, [(i, (i + 1) % count) for i in range(ends)]),
                cells,
                lax.ppermute(head, axis, [((i + 1) % count, i) for i in range(ends)]),
            ],
            axis=dim,
        )
    return cells


def normed(values, scales):
    average = jnp.mean(values, axis=-1, keepdims=True)
    centred = values - average
    spread = jnp.mean(centred * centred, axis=-1, keepdims=True)
    return centred * lax.rsqrt(spread + 1e-05) * scales


def gelu_exact(values):
    return jax.nn.gelu(values, approximate=False)


def linear_step(former, latter):
    return (former[0] * latter[0], latter[0] * former[1] + latter[1])


def doc_index(positions, starts):
    return jnp.sum((starts[None, :] <= positions[:, None]).astype(jnp.int32), axis=1) - 1


def docs_meet(first_docs, second_docs):
    return jnp.logical_and(first_docs[0] <= second_docs[-1], second_docs[0] <= first_docs[-1])


def score_block(query_blk, key_blk, query_docs, key_docs):
    scores = jnp.einsum(
        "qhe,khe->hqk", query_blk, key_blk, preferred_element_type=jnp.float32
    ) * HEAD_DIM ** (-0.5)
    allowed = query_docs[None, :, None] == key_docs[None, None, :]
    return (scores, allowed)


def grad_block(query_blk, key_blk, value_blk, grad_blk, query_docs, key_docs, log_total, row_term):
    scores, allowed = score_block(query_blk, key_blk, query_docs, key_docs)
    probs = jnp.where(allowed, jnp.exp(scores - log_total[:, :, None]), 0.0)
    dprobs = jnp.einsum("qhe,khe->hqk", grad_blk, value_blk, preferred_element_type=jnp.float32)
    dscores = (probs * (dprobs - row_term[:, :, None])).astype(jnp.bfloat16)
    return (probs, dscores)


def body(
    tokens,
    chars,
    char_token,
    doc_lengths,
    gain_attn,
    qkv_weight,
    out_weight,
    gain_char,
    gru_weight,
    conv_weight,
    gain_merge,
    merge_weight,
    up_weight,
    down_weight,
    cot_tokens,
    cot_chars,
):
    f32 = jnp.float32
    bf16 = jnp.bfloat16
    (
        attn_gain,
        qkv_full,
        out_full,
        char_gain,
        gru_full,
        conv_full,
        merge_gain,
        merge_full,
        up_full,
        down_full,
    ) = (
        lax.all_gather(gain_attn, ("ctx", "wsh"), axis=0, tiled=True),
        lax.all_gather(qkv_weight, ("ctx", "wsh"), axis=0, tiled=True),
        lax.all_gather(out_weight, ("ctx", "wsh"), axis=0, tiled=True),
        lax.all_gather(gain_char, ("ctx", "wsh"), axis=0, tiled=True),
        lax.all_gather(gru_weight, ("ctx", "wsh"), axis=0, tiled=True),
        lax.all_gather(conv_weight, ("ctx", "wsh"), axis=0, tiled=True),
        lax.all_gather(gain_merge, ("ctx", "wsh"), axis=0, tiled=True),
        lax.all_gather(merge_weight, ("ctx", "wsh"), axis=0, tiled=True),
        lax.all_gather(up_weight, ("ctx", "wsh"), axis=0, tiled=True),
        lax.all_gather(down_weight, ("ctx", "wsh"), axis=0, tiled=True),
    )
    attn_gain_f = attn_gain.astype(f32)
    char_gain_f = char_gain.astype(f32)
    merge_gain_f = merge_gain.astype(f32)
    width = tokens.shape[2]
    tok_rows = tokens.shape[1]
    char_rows = chars.shape[1]
    half_width = width // 2
    seq_len = tok_rows * lax.axis_size("ctx")
    key_block = min(seq_len, 512)
    key_count = seq_len // key_block
    scale = HEAD_DIM ** (-0.5)
    token_in = tokens[0].astype(f32)
    char_in = chars[0].astype(f32)
    char_map = char_token[0, 0]
    lengths = doc_lengths[0]
    starts = jnp.cumsum(lengths) - lengths
    positions = lax.axis_index("ctx") * tok_rows + jnp.arange(tok_rows, dtype=jnp.int32)
    query_docs = doc_index(positions, starts)
    doc_first = jnp.any(starts[None, :] == positions[:, None], axis=1)
    doc_last = jnp.any(starts[None, :] == positions[:, None] + 1, axis=1)
    onehot = char_map[None, :] == jnp.arange(tok_rows, dtype=jnp.int32)[:, None]
    onehot_low = onehot.astype(bf16)
    counts = jnp.sum(onehot.astype(f32), axis=1)
    root_counts = jnp.sqrt(counts)
    boundary = char_map[1:] != char_map[:-1]
    first_char = jnp.concatenate([jnp.ones((1,), bool), boundary])
    last_char = jnp.concatenate([boundary, jnp.ones((1,), bool)])
    opens_doc = jnp.any(onehot & doc_first[:, None], axis=0)
    closes_doc = jnp.any(onehot & doc_last[:, None], axis=0)
    keep_fwd = 1.0 - (first_char & opens_doc).astype(f32)
    keep_bwd = 1.0 - (last_char & closes_doc).astype(f32)
    attn_in = normed(token_in, attn_gain_f).astype(bf16)
    qkv = jnp.dot(attn_in, qkv_full, preferred_element_type=f32).astype(bf16)
    queries = qkv[:, :width]
    keys = qkv[:, width : 2 * width]
    values = qkv[:, 2 * width :]
    keys_all, values_all = (
        lax.all_gather(keys, "ctx", axis=0, tiled=True),
        lax.all_gather(values, "ctx", axis=0, tiled=True),
    )
    query_heads = queries.reshape(tok_rows, HEADS, HEAD_DIM)
    key_blocks = keys_all.reshape(key_count, key_block, HEADS, HEAD_DIM)
    value_blocks = values_all.reshape(key_count, key_block, HEADS, HEAD_DIM)
    key_docs = doc_index(jnp.arange(seq_len, dtype=jnp.int32), starts).reshape(key_count, key_block)

    def forward_block(carry, inputs):
        key_blk, value_blk, docs_blk = inputs

        def forward_used(state):
            run_max, run_total, run_acc = state
            scores, allowed = score_block(query_heads, key_blk, query_docs, docs_blk)
            scores = jnp.where(allowed, scores, masked_score)
            new_max = jnp.maximum(run_max, jnp.max(scores, axis=2))
            factor = jnp.exp(run_max - new_max)
            weights = jnp.where(allowed, jnp.exp(scores - new_max[:, :, None]), 0.0)
            run_total = run_total * factor + jnp.sum(weights, axis=2)
            run_acc = run_acc * factor[:, :, None] + jnp.einsum(
                "hqk,khe->hqe", weights.astype(bf16), value_blk, preferred_element_type=f32
            )
            return (new_max, run_total, run_acc)

        def forward_skipped(state):
            return state

        return (
            lax.cond(docs_meet(query_docs, docs_blk), forward_used, forward_skipped, carry),
            None,
        )

    start_carry = (
        jnp.full((HEADS, tok_rows), masked_score, f32),
        jnp.zeros((HEADS, tok_rows), f32),
        jnp.zeros((HEADS, tok_rows, HEAD_DIM), f32),
    )
    (run_max, run_total, run_acc), _ = lax.scan(
        forward_block, start_carry, (key_blocks, value_blocks, key_docs)
    )
    log_total = run_max + jnp.log(run_total)
    attn_heads = jnp.transpose(run_acc / run_total[:, :, None], (1, 0, 2))
    attn_out = attn_heads.reshape(tok_rows, width).astype(bf16)
    proj = jnp.dot(attn_out, out_full, preferred_element_type=f32)
    sq_proj, cross_sum, sq_tok = lax.psum(
        (jnp.sum(proj * proj), jnp.sum(token_in * proj), jnp.sum(token_in * token_in)), "ctx"
    )
    elements = seq_len * width
    rms_scale = lax.rsqrt(sq_proj / elements + 1e-06)
    stream_sq = (sq_tok + 2.0 * rms_scale * cross_sum + rms_scale * rms_scale * sq_proj) / elements
    stream_scale = lax.rsqrt(stream_sq + 1e-06)
    stream = token_in + proj * rms_scale
    resid = stream * stream_scale
    char_low = normed(char_in, char_gain_f).astype(bf16)
    gates = jnp.dot(char_low, gru_full, preferred_element_type=f32)
    ramp = jnp.arange(half_width, dtype=f32) / (half_width - 1)
    shift = (1.0 + math.log(char_rows * lax.axis_size("ctx"))) * ramp
    lift = jnp.exp(0.5 * shift)
    zeta_f = jax.nn.sigmoid(gates[:, :half_width] - shift)
    cand_f = gates[:, half_width : 2 * half_width] * lift
    zeta_b = jax.nn.sigmoid(gates[:, 2 * half_width : 3 * half_width] - shift)
    cand_b = gates[:, 3 * half_width :] * lift
    identity = (jnp.ones((half_width,), f32), jnp.zeros((half_width,), f32))
    coef_f = (1.0 - zeta_f) * keep_fwd[:, None]
    cum_f, local_f = lax.associative_scan(linear_step, (coef_f, zeta_f * cand_f))
    prefix_f = carried_in((cum_f[-1], local_f[-1]), "ctx", linear_step, identity, False)
    carry_in_f = prefix_f[1]
    state_f = local_f + cum_f * carry_in_f
    coef_b = (1.0 - zeta_b) * keep_bwd[:, None]
    cum_b, local_b = lax.associative_scan(linear_step, (coef_b, zeta_b * cand_b), reverse=True)
    prefix_b = carried_in((cum_b[0], local_b[0]), "ctx", linear_step, identity, True)
    carry_in_b = prefix_b[1]
    state_b = local_b + cum_b * carry_in_b
    mixed = jnp.concatenate([state_f, state_b], axis=1).astype(bf16)
    out_chars = (char_in + mixed.astype(f32)).astype(bf16)
    pooled = (jnp.dot(onehot_low, mixed, preferred_element_type=f32) / root_counts[:, None]).astype(
        bf16
    )
    padded = padded_2(pooled, (("ctx", 0),), 1)
    conv_out = jnp.zeros((tok_rows, width), f32)
    for kernel in range(3):
        conv_out = conv_out + jnp.dot(
            padded[kernel : kernel + tok_rows],
            conv_full[:, kernel * width : (kernel + 1) * width],
            preferred_element_type=f32,
        )
    merge_in = normed(resid, merge_gain_f).astype(bf16)
    merge_pre = jnp.dot(merge_in, merge_full, preferred_element_type=f32) + conv_out
    merged = gelu_exact(merge_pre).astype(bf16)
    up_pre = jnp.dot(merged, up_full, preferred_element_type=f32)
    up_act = gelu_exact(up_pre).astype(bf16)
    out_tok = (resid + jnp.dot(up_act, down_full, preferred_element_type=f32)).astype(bf16)
    cot_tok = cot_tokens[0]
    cot_tok_f = cot_tok.astype(f32)
    cot_chr_f = cot_chars[0].astype(f32)
    grad_down = jnp.einsum("tf,td->fd", up_act, cot_tok, preferred_element_type=f32)
    grad_act = jnp.einsum("td,fd->tf", cot_tok, down_full, preferred_element_type=f32)
    _, gelu_up_back = jax.vjp(gelu_exact, up_pre)
    grad_up_pre = gelu_up_back(grad_act)[0].astype(bf16)
    grad_up = jnp.einsum("tc,tf->cf", merged, grad_up_pre, preferred_element_type=f32)
    grad_merged = jnp.einsum("tf,cf->tc", grad_up_pre, up_full, preferred_element_type=f32)
    _, gelu_merge_back = jax.vjp(gelu_exact, merge_pre)
    grad_pre = gelu_merge_back(grad_merged)[0].astype(bf16)
    grad_merge = jnp.einsum("tc,te->ce", merge_in, grad_pre, preferred_element_type=f32)
    grad_merge_in = jnp.einsum("te,ce->tc", grad_pre, merge_full, preferred_element_type=f32)
    grad_conv = jnp.concatenate(
        [
            jnp.einsum(
                "tc,te->ce",
                padded[kernel : kernel + tok_rows],
                grad_pre,
                preferred_element_type=f32,
            )
            for kernel in range(3)
        ],
        axis=1,
    )
    grad_padded = padded_2(grad_pre, (("ctx", 0),), 1)
    grad_pooled = jnp.zeros((tok_rows, width), f32)
    for kernel in range(3):
        grad_pooled = grad_pooled + jnp.einsum(
            "te,ce->tc",
            grad_padded[2 - kernel : 2 - kernel + tok_rows],
            conv_full[:, kernel * width : (kernel + 1) * width],
            preferred_element_type=f32,
        )
    _, merge_norm_back = jax.vjp(normed, resid, merge_gain_f)
    grad_resid_norm, grad_merge_gain = merge_norm_back(grad_merge_in)
    grad_resid = cot_tok_f + grad_resid_norm
    grad_mixed = cot_chr_f + jnp.take(grad_pooled / root_counts[:, None], char_map, axis=0)
    grad_state_f = grad_mixed[:, :half_width]
    grad_state_b = grad_mixed[:, half_width:]
    shifted_f = jnp.concatenate([coef_f[1:], jnp.ones((1, half_width), f32)], axis=0)
    cum_gf, local_gf = lax.associative_scan(linear_step, (shifted_f, grad_state_f), reverse=True)
    prefix_gf = carried_in(
        (coef_f[0] * cum_gf[0], coef_f[0] * local_gf[0]), "ctx", linear_step, identity, True
    )
    lam_f = local_gf + cum_gf * prefix_gf[1]
    prev_f = jnp.concatenate([carry_in_f[None, :], state_f[:-1]], axis=0)
    grad_zeta_f = lam_f * (cand_f - keep_fwd[:, None] * prev_f) * zeta_f * (1.0 - zeta_f)
    grad_cand_f = lam_f * zeta_f * lift
    shifted_b = jnp.concatenate([jnp.ones((1, half_width), f32), coef_b[:-1]], axis=0)
    cum_gb, local_gb = lax.associative_scan(linear_step, (shifted_b, grad_state_b))
    prefix_gb = carried_in(
        (coef_b[-1] * cum_gb[-1], coef_b[-1] * local_gb[-1]), "ctx", linear_step, identity, False
    )
    lam_b = local_gb + cum_gb * prefix_gb[1]
    next_b = jnp.concatenate([state_b[1:], carry_in_b[None, :]], axis=0)
    grad_zeta_b = lam_b * (cand_b - keep_bwd[:, None] * next_b) * zeta_b * (1.0 - zeta_b)
    grad_cand_b = lam_b * zeta_b * lift
    grad_gates = jnp.concatenate(
        [grad_zeta_f, grad_cand_f, grad_zeta_b, grad_cand_b], axis=1
    ).astype(bf16)
    grad_gru = jnp.einsum("tc,tg->cg", char_low, grad_gates, preferred_element_type=f32)
    grad_char_norm = jnp.einsum("tg,cg->tc", grad_gates, gru_full, preferred_element_type=f32)
    _, char_norm_back = jax.vjp(normed, char_in, char_gain_f)
    grad_char_in, grad_char_gain = char_norm_back(grad_char_norm)
    grad_chars_out = (cot_chr_f + grad_char_in).astype(bf16)
    dot_stream, dot_proj = lax.psum(
        (jnp.sum(grad_resid * stream), jnp.sum(grad_resid * proj)), "ctx"
    )
    mean_gs = dot_stream / elements
    mean_gp = dot_proj / elements
    mean_sp = (cross_sum + rms_scale * sq_proj) / elements
    grad_stream = stream_scale * grad_resid - stream_scale**3 * mean_gs * stream
    mean_gsp = stream_scale * mean_gp - stream_scale**3 * mean_gs * mean_sp
    grad_proj = (rms_scale * grad_stream - rms_scale**3 * mean_gsp * proj).astype(bf16)
    grad_out_proj = jnp.einsum("tc,te->ce", attn_out, grad_proj, preferred_element_type=f32)
    grad_attn = jnp.einsum("te,ce->tc", grad_proj, out_full, preferred_element_type=f32).astype(
        bf16
    )
    grad_heads = grad_attn.reshape(tok_rows, HEADS, HEAD_DIM)
    row_term = jnp.einsum("qhe,qhe->hq", grad_heads.astype(f32), attn_heads)

    def step_block(dq_acc, inputs):
        key_blk, value_blk, docs_blk = inputs

        def step_used(acc):
            probs, dscores = grad_block(
                query_heads,
                key_blk,
                value_blk,
                grad_heads,
                query_docs,
                docs_blk,
                log_total,
                row_term,
            )
            acc = (
                acc
                + jnp.einsum("hqk,khe->qhe", dscores, key_blk, preferred_element_type=f32) * scale
            )
            dk_blk = (
                jnp.einsum("hqk,qhe->khe", dscores, query_heads, preferred_element_type=f32) * scale
            )
            dv_blk = jnp.einsum(
                "hqk,qhe->khe", probs.astype(bf16), grad_heads, preferred_element_type=f32
            )
            return (acc, (dk_blk, dv_blk))

        def step_skipped(acc):
            zero_blk = jnp.zeros((key_blk.shape[0], HEADS, HEAD_DIM), f32)
            return (acc, (zero_blk, zero_blk))

        return lax.cond(docs_meet(query_docs, docs_blk), step_used, step_skipped, dq_acc)

    dq_heads, key_terms = lax.scan(
        step_block,
        jnp.zeros((tok_rows, HEADS, HEAD_DIM), f32),
        (key_blocks, value_blocks, key_docs),
    )
    dk_local, dv_local = (
        lax.psum_scatter(
            key_terms[0].reshape(seq_len, width).astype(jnp.bfloat16),
            "ctx",
            scatter_dimension=0,
            tiled=True,
        ).astype(jnp.float32),
        lax.psum_scatter(
            key_terms[1].reshape(seq_len, width).astype(jnp.bfloat16),
            "ctx",
            scatter_dimension=0,
            tiled=True,
        ).astype(jnp.float32),
    )
    grad_qkv_low = jnp.concatenate(
        [
            dq_heads.reshape(tok_rows, width).astype(bf16),
            dk_local.astype(bf16),
            dv_local.astype(bf16),
        ],
        axis=1,
    )
    grad_qkv = jnp.einsum("tc,tg->cg", attn_in, grad_qkv_low, preferred_element_type=f32)
    grad_attn_in = jnp.einsum("tg,cg->tc", grad_qkv_low, qkv_full, preferred_element_type=f32)
    _, attn_norm_back = jax.vjp(normed, token_in, attn_gain_f)
    grad_token_in, grad_attn_gain = attn_norm_back(grad_attn_in)
    grad_tokens_out = (grad_stream + grad_token_in).astype(bf16)
    shards = (
        lax.psum_scatter(grad_attn_gain, ("ctx", "wsh"), scatter_dimension=0, tiled=True),
        lax.psum_scatter(grad_qkv, ("ctx", "wsh"), scatter_dimension=0, tiled=True),
        lax.psum_scatter(grad_out_proj, ("ctx", "wsh"), scatter_dimension=0, tiled=True),
        lax.psum_scatter(grad_char_gain, ("ctx", "wsh"), scatter_dimension=0, tiled=True),
        lax.psum_scatter(grad_gru, ("ctx", "wsh"), scatter_dimension=0, tiled=True),
        lax.psum_scatter(grad_conv, ("ctx", "wsh"), scatter_dimension=0, tiled=True),
        lax.psum_scatter(grad_merge_gain, ("ctx", "wsh"), scatter_dimension=0, tiled=True),
        lax.psum_scatter(grad_merge, ("ctx", "wsh"), scatter_dimension=0, tiled=True),
        lax.psum_scatter(grad_up, ("ctx", "wsh"), scatter_dimension=0, tiled=True),
        lax.psum_scatter(grad_down, ("ctx", "wsh"), scatter_dimension=0, tiled=True),
    )
    return (
        out_tok[None],
        out_chars[None],
        grad_tokens_out[None],
        grad_chars_out[None],
        shards[0],
        shards[1],
        shards[2],
        shards[3],
        shards[4],
        shards[5],
        shards[6],
        shards[7],
        shards[8],
        shards[9],
    )


def solution(mesh):
    in_specs = (
        P("wsh", "ctx", None),
        P("wsh", "ctx", None),
        P("wsh", "ctx", None),
        P("wsh", None),
        P(("ctx", "wsh")),
        P(("ctx", "wsh"), None),
        P(("ctx", "wsh"), None),
        P(("ctx", "wsh")),
        P(("ctx", "wsh"), None),
        P(("ctx", "wsh"), None),
        P(("ctx", "wsh")),
        P(("ctx", "wsh"), None),
        P(("ctx", "wsh"), None),
        P(("ctx", "wsh"), None),
        P("wsh", "ctx", None),
        P("wsh", "ctx", None),
    )
    out_specs = (
        P("wsh", "ctx", None),
        P("wsh", "ctx", None),
        P("wsh", "ctx", None),
        P("wsh", "ctx", None),
        P(("ctx", "wsh")),
        P(("ctx", "wsh"), None),
        P(("ctx", "wsh"), None),
        P(("ctx", "wsh")),
        P(("ctx", "wsh"), None),
        P(("ctx", "wsh"), None),
        P(("ctx", "wsh")),
        P(("ctx", "wsh"), None),
        P(("ctx", "wsh"), None),
        P(("ctx", "wsh"), None),
    )
    return jax.shard_map(body, mesh=mesh, in_specs=in_specs, out_specs=out_specs, check_vma=False)
```

profile of v0, /device:TPU:0, one launch (start us, length us, event | category | flops | bytes accessed | tf_op | source)
XLA Modules:
  0.0 1993.1 jit_solution(18089502802214424938)
XLA Ops:
  12.0 42.1 %all-reduce.173 = (bf16[768]{0:T(1024)(128)(2,1)S(1)}, bf16[768]{0:T(1024)(128)(2,1)}, bf16[768]{0:T(1024)(128)(2,1)S(1)}) all-reduce(bf16[768]{0:T(1024)(128)(2,1)S(1)} %dynamic-update-slice, bf16[768]{0:T(1024)(128)(2,1)S(1)} %dynamic-update-slice.1, ...), channel_id=1, replica_groups=mesh['ctx'=8,'wsh'=4] {'ctx','wsh'}, use_global_device_ids=true, to_apply=%add.164 | all-reduce | flops 2304 | bytes 9216
  56.5 17.2 all-gather.18.cloned.1.call-done
  85.7 47.0 %all-gather.28.cloned.1.call-done = bf16[768,1536]{1,0:T(8,128)(2,1)} async-done(((bf16[24,1536]{1,0:T(8,128)(2,1)}), bf16[768,1536]{1,0:T(8,128)(2,1)}) %all-gather.28.cloned.1.call-update) | async-done | bytes 2359312 | tf_op jit(solution)/shard_map/all_gather | solution.py:124
  442.6 7.0 slice.1453
  449.6 7.1 slice.1531
  494.8 9.0 all-gather.1
  517.1 7.7 all-gather
  524.8 9.0 all-gather.3
  533.9 7.8 all-gather.2
  542.2 12.8 rev.29
  555.0 12.7 rev.28
  618.7 22.3 %while.87 = (s32[]{:T(128)}, f32[12,256]{1,0:T(8,128)S(1)}, f32[12,256]{1,0:T(8,128)S(1)}, f32[12,256,64]{1,2,0:T(8,128)S(1)}, s32[256]{0:T(256)S(1)}, /*index=5...) while((s32[]{:T(128)}, f32[12,256]{1,0:T(8,128)S(1)}, ...), condition=%wide.region_10.11_spmd, body=%wide.region_5.10_spmd.sunk | while | flops 423630848 | bytes 23142728 | solution.py:205
  644.9 27.1 %all-reduce.172 = (f32[]{:T(128)}, f32[]{:T(128)}, f32[]{:T(128)}) all-reduce(f32[]{:T(128)} %get-tuple-element.906, f32[]{:T(128)} %get-tuple-element.907, f32[]{:T(128)} %get-tuple-element.905), channel_id=1, replica_groups=mesh['ctx'=8,'wsh'=4] {'ctx'}, use_global_device_ids=true, to_apply=%region_12.13 | all-reduce | flops 3 | bytes 24 | tf_op jit(solution)/shard_map/psum | solution.py:212
  683.8 11.4 multiply_convert_fusion
  706.5 12.8 all-reduce.171
  728.1 39.0 %while.88 = (s32[]{:T(128)}, f32[256,12,64]{0,2,1:T(8,128)S(1)}, bf16[4,512,12,64]{1,3,2,0:T(8,128)(2,1)}, bf16[4,512,12,64]{1,3,2,0:T(8,128)(2,1)}, s32[256]{0:...) while((s32[]{:T(128)}, f32[256,12,64]{0,2,1:T(8,128)S(1)}, ...), condition=%wide.region_39.40_spmd, body=%wide.region_36.39_spmd.sunk | while | flops 1023672320 | bytes 40650168 | solution.py:374
  734.0 9.9 conditional.5
  829.2 11.3 collective-permute-start.3
  1173.0 24.9 %all-gather.7 = f32[8,1,384]{2,1,0:T(1,128)S(1)} all-gather(f32[1,1,384]{2,1,0:T(1,128)S(1)} %get-tuple-element.1054), channel_id=1, replica_groups=mesh['ctx'=8,'wsh'=4] {'ctx'}, dimensions={0}, use_global_device_ids=true | all-gather | bytes 13824 | tf_op jit(solution)/shard_map/all_gather | solution.py:17
  1197.9 7.9 all-gather.6
  1247.9 7.0 slice.1646
  1279.1 9.2 all-gather.4
  1290.9 8.0 all-gather.5
  1301.5 12.8 rev.33
  1314.3 7.7 rev.32
  1345.5 8.1 copy.108
  1393.7 47.1 %all-reduce.170 = (f32[768]{0:T(1024)S(1)}, f32[768]{0:T(1024)S(1)}, f32[768]{0:T(1024)S(1)}) all-reduce(f32[768]{0:T(1024)S(1)} %get-tuple-element.901, f32[768]{0:T(1024)S(1)} %copy-done.130, f32[768]{0:T(1024)S(1)} %copy-done.178), channel_id=4, replica_groups=mesh['ctx'=8,'wsh'=4] {'ctx','wsh'}, use_global_device_ids=true, to_apply=%region_51.52.clone | all-reduce | flops 2304 | bytes 18432
  1443.8 9.5 reduce-scatter.20.cloned.1.call-done
  1453.3 125.2 %reduce-scatter.28.cloned.1.call-done = f32[24,2304]{1,0:T(8,128)} async-done(((f32[768,2304]{1,0:T(8,128)}), f32[24,2304]{1,0:T(8,128)}) %reduce-scatter.28.cloned.1.call-update) | async-done | bytes 221200
  1578.5 141.3 %reduce-scatter.24.cloned.1.call-done = f32[24,3072]{1,0:T(8,128)} async-done(((f32[768,3072]{1,0:T(8,128)}), f32[24,3072]{1,0:T(8,128)}) %reduce-scatter.24.cloned.1.call-update) | async-done | bytes 294928 | tf_op jit(solution)/shard_map/reduce_scatter | solution.py:415
  1719.8 141.8 %reduce-scatter.26.cloned.1.call-done = f32[96,768]{1,0:T(8,128)} async-done(((f32[3072,768]{1,0:T(8,128)}), f32[96,768]{1,0:T(8,128)}) %reduce-scatter.26.cloned.1.call-update) | async-done | bytes 294928 | tf_op jit(solution)/shard_map/reduce_scatter | solution.py:416
  1861.7 124.2 %reduce-scatter.16.cloned.1.call-done = f32[24,2304]{1,0:T(8,128)} async-done(((f32[768,2304]{1,0:T(8,128)}), f32[24,2304]{1,0:T(8,128)}) %reduce-scatter.16.cloned.1.call-update) | async-done | bytes 221200 | tf_op jit(solution)/shard_map/reduce_scatter | solution.py:408
  (1338 shorter events, 1045.2 us)
Async XLA Ops:
  7.2 66.6 %all-gather.18.cloned.1.call-start = ((), (), s32[]{:S(2)}) async-start(), calls=%async_computation.9 | async-start | bytes 3649536 | tf_op jit(solution)/shard_map/all_gather | solution.py:121
  7.9 124.8 %all-gather.28.cloned.1.call-start = ((), (), s32[]{:S(2)}) async-start(), calls=%async_computation.14 | async-start | bytes 2433024 | tf_op jit(solution)/shard_map/all_gather | solution.py:124
  8.7 573.7 %all-gather.30.cloned.1.call-start = ((), (), s32[]{:S(2)}) async-start(), calls=%async_computation.15 | async-start | bytes 3649536 | tf_op jit(solution)/shard_map/all_gather | solution.py:125
  9.4 578.2 %all-gather.20.cloned.1.call-start = ((), (), s32[]{:S(2)}) async-start(), calls=%async_computation.10 | async-start | bytes 3538944 | tf_op jit(solution)/shard_map/all_gather | solution.py:168
  78.1 525.2 %all-gather.22.cloned.1.call-start = ((), (), s32[]{:S(2)}) async-start(), calls=%async_computation.11 | async-start | bytes 3538944 | tf_op jit(solution)/shard_map/all_gather | solution.py:169
  78.7 563.0 %all-gather.24.cloned.1.call-start = ((), (), s32[]{:S(2)}) async-start(), calls=%async_computation.12 | async-start | bytes 1216512 | tf_op jit(solution)/shard_map/all_gather | solution.py:122
  79.3 595.9 %all-gather.26.cloned.1.call-start = ((), (), s32[]{:S(2)}) async-start(), calls=%async_computation.13 | async-start | bytes 1216512 | tf_op jit(solution)/shard_map/all_gather | solution.py:127
  80.1 603.7 %all-gather.32.cloned.1.call-start = ((), (), s32[]{:S(2)}) async-start(), calls=%async_computation.16 | async-start | bytes 4866048 | tf_op jit(solution)/shard_map/all_gather | solution.py:128
  80.8 614.3 %all-gather.34.cloned.1.call-start = ((), (), s32[]{:S(2)}) async-start(), calls=%async_computation.17 | async-start | bytes 4866048 | tf_op jit(solution)/shard_map/all_gather | solution.py:129
  81.5 1287.9 %reduce-scatter.12.cloned.1.call-start = ((), (), s32[]{:S(2)}) async-start(), calls=%async_computation.18 | async-start | bytes 3538944 | tf_op jit(solution)/shard_map/reduce_scatter | solution.py:380
  81.8 55.3 %copy-start.117 = (f32[384]{0:T(512)}, f32[384]{0:T(512)S(1)}, u32[]{:S(2)}) copy-start(f32[384]{0:T(512)S(1)} %get-tuple-element.1243) | copy-start | bytes 4612
  81.8 55.3 %copy-start.119 = (f32[384]{0:T(512)}, f32[384]{0:T(512)S(1)}, u32[]{:S(2)}) copy-start(f32[384]{0:T(512)S(1)} %get-tuple-element.1244) | copy-start | bytes 4612
  83.0 54.1 %copy-start.107 = (f32[768]{0:T(1024)}, f32[768]{0:T(1024)S(1)}, u32[]{:S(2)}) copy-start(f32[768]{0:T(1024)S(1)} %convert_element_type.183) | copy-start | bytes 9220
  83.3 53.8 %copy-start.96 = (f32[1024]{0:T(1024)}, f32[1024]{0:T(1024)S(1)}, u32[]{:S(2)}) copy-start(f32[1024]{0:T(1024)S(1)} %broadcast_multiply_fusion) | copy-start | bytes 12292
  83.9 53.2 %copy-start.109 = (f32[1024]{0:T(1024)}, f32[1024]{0:T(1024)S(1)}, u32[]{:S(2)}) copy-start(f32[1024]{0:T(1024)S(1)} %fusion.185) | copy-start | bytes 12292
  85.7 51.5 %copy-start.103 = (f32[1024]{0:T(1024)}, f32[1024]{0:T(1024)S(1)}, u32[]{:S(2)}) copy-start(f32[1024]{0:T(1024)S(1)} %get-tuple-element.1231) | copy-start | bytes 12292
  85.7 51.5 %copy-start.105 = (f32[1024]{0:T(1024)}, f32[1024]{0:T(1024)S(1)}, u32[]{:S(2)}) copy-start(f32[1024]{0:T(1024)S(1)} %get-tuple-element.1232) | copy-start | bytes 12292
  140.8 132.4 %copy-start.5 = (f32[1024,384]{1,0:T(8,128)}, f32[1024,384]{1,0:T(8,128)S(1)}, u32[]{:S(2)}) copy-start(f32[1024,384]{1,0:T(8,128)S(1)} %get-tuple-element.1047) | copy-start | bytes 4718596
  140.8 285.4 %copy-start.2 = (f32[1024,384]{1,0:T(8,128)}, f32[1024,384]{1,0:T(8,128)S(1)}, u32[]{:S(2)}) copy-start(f32[1024,384]{1,0:T(8,128)S(1)} %get-tuple-element.1046) | copy-start | bytes 4718596
  576.6 5.7 collective-permute-start.1
  578.5 100.0 %collective-permute-start = (bf16[1,768]{1,0:T(2,128)(2,1)}, bf16[1,768]{1,0:T(2,128)(2,1)}, u32[]{:S(2)}, u32[]{:S(2)}) collective-permute-start(bf16[1,768]{1,0:T(2,128)(2,1)} %get-tuple-element.1085), channel_id=1, source_target_pairs={{0,4},{4,8},{8,12},{12,16},{16,20},{20,24},{24,28},{1,5},{5,9},{9,... | collective-permute-start | bytes 4616 | tf_op jit(solution)/shard_map/ppermute | solution.py:40
  774.2 595.3 %reduce-scatter.14.cloned.1.call-start = ((), (), s32[]{:S(2)}) async-start(), calls=%async_computation.19 | async-start | bytes 3538944 | tf_op jit(solution)/shard_map/reduce_scatter | solution.py:386
  781.3 662.5 %reduce-scatter.22.cloned.1.call-start = ((), (), s32[]{:S(2)}) async-start(), calls=%async_computation.23 | async-start | bytes 2433024 | tf_op jit(solution)/shard_map/reduce_scatter | solution.py:414
  784.3 659.5 %reduce-scatter.18.cloned.1.call-start = ((), (), s32[]{:S(2)}) async-start(), calls=%async_computation.21 | async-start | bytes 2433024 | tf_op jit(solution)/shard_map/reduce_scatter | solution.py:409
  829.2 16.5 collective-permute-start.3
  840.5 7.0 collective-permute-start.2
  843.7 609.6 %reduce-scatter.20.cloned.1.call-start = ((), (), s32[]{:S(2)}) async-start(), calls=%async_computation.22 | async-start | bytes 4866048 | tf_op jit(solution)/shard_map/reduce_scatter | solution.py:411
  1339.3 239.2 %reduce-scatter.28.cloned.1.call-start = ((), (), s32[]{:S(2)}) async-start(), calls=%async_computation.26 | async-start | bytes 7299072
  1353.7 366.1 %reduce-scatter.24.cloned.1.call-start = ((), (), s32[]{:S(2)}) async-start(), calls=%async_computation.24 | async-start | bytes 9732096 | tf_op jit(solution)/shard_map/reduce_scatter | solution.py:415
  1361.1 500.5 %reduce-scatter.26.cloned.1.call-start = ((), (), s32[]{:S(2)}) async-start(), calls=%async_computation.25 | async-start | bytes 9732096 | tf_op jit(solution)/shard_map/reduce_scatter | solution.py:416
  1368.6 617.3 %reduce-scatter.16.cloned.1.call-start = ((), (), s32[]{:S(2)}) async-start(), calls=%async_computation.20 | async-start | bytes 7299072 | tf_op jit(solution)/shard_map/reduce_scatter | solution.py:408
  1391.9 50.6 %copy-start.12 = (f32[256,768]{1,0:T(8,128)S(1)}, f32[256,768]{1,0:T(8,128)}, u32[]{:S(2)}) copy-start(f32[256,768]{1,0:T(8,128)} %copy-done.11) | copy-start | bytes 2359300
  (179 other events, 1485.1 us)
Sparse Core Ops, SparseCore 0:
  10.8 62.8 all-gather.17
  76.5 56.0 all-gather.27
  135.5 59.0 all-gather.29
  196.3 31.0 all-gather.19
  229.7 32.3 all-gather.21
  264.7 54.0 all-gather.23
  321.6 53.0 all-gather.25
  377.5 62.4 all-gather.31
  442.8 62.3 all-gather.33
  774.3 75.7 reduce-scatter.11
  853.8 46.2 reduce-scatter.13
  905.8 99.0 reduce-scatter.21
  1011.6 98.0 reduce-scatter.17
  1339.4 113.8 reduce-scatter.19
  1460.3 118.1 reduce-scatter.27
  1584.8 134.9 reduce-scatter.23
  1727.2 134.4 reduce-scatter.25
  1867.8 118.0 reduce-scatter.15
where the time goes:
time: 2030 us; the launch traced here: 1990 us
  local copies, waits for them, and re-layouts  786 us (39%)
  waiting for transfers between devices  612 us (30%)
  other arithmetic  214 us (11%)
  blocking collectives  213 us (10%)
  matrix products  105 us (5%)
  between operations  23.8 us (1%)
  loops' own time  21.5 us (1%)
    slice x74, local copies, waits for them, and re-layouts, body(): lax.associative_scan(linear_step, (coef_b, zeta_b * cand_b), reverse=True)  149 us
    slice x73, local copies, waits for them, and re-layouts, body(): lax.associative_scan(linear_step, (shifted_f, grad_state_f), reverse=True)  148 us
    reduce_scatter x1, waiting for transfers between devices, body(): lax.psum_scatter(grad_down, ('ctx', 'wsh'), scatter_dimension=0, tiled=True)  142 us
    reduce_scatter x1, waiting for transfers between devices, body(): lax.psum_scatter(grad_up, ('ctx', 'wsh'), scatter_dimension=0, tiled=True)  141 us
    unnamed x19, waiting for transfers between devices  131 us
    reduce_scatter x1, waiting for transfers between devices, body(): lax.psum_scatter(grad_qkv, ('ctx', 'wsh'), scatter_dimension=0, tiled=True)  124 us
    slice x66, local copies, waits for them, and re-layouts, body(): lax.associative_scan(linear_step, (shifted_b, grad_state_b))  117 us
    slice x68, local copies, waits for them, and re-layouts, body(): lax.associative_scan(linear_step, (coef_f, zeta_f * cand_f))  115 us
  transfers between devices with their start and end apart: 22, of which 7 were waited for; matrix products, arithmetic and copies ran while one was open for 52% of the time, Pallas kernels for 0%

commit v1 on v0

--- a/solution.py
+++ b/solution.py
@@ -1,8 +1,11 @@
+import functools
 import math
 
 import jax
 import jax.numpy as jnp
 from jax import lax
+from jax.experimental import pallas as pl
+from jax.experimental.pallas import tpu as pltpu
 from jax.sharding import PartitionSpec as P
 
 HEADS = 12
@@ -12,21 +15,145 @@
 masked_score = -1e30
 
 
-def carried_in(value, axis, join, neutral, backward):
-    count, mine = (lax.axis_size(axis), lax.axis_index(axis))
-    pieces = jax.tree.map(lambda part: lax.all_gather(part, axis), value)
-    if backward:
-        pieces = jax.tree.map(lambda part: part[::-1], pieces)
-        mine = count - 1 - mine
-    running = jax.tree.map(
-        lambda part, zero: jnp.full_like(part, 0) + jnp.asarray(zero, part.dtype), value, neutral
-    )
-
-    def turn(position, running):
-        longer = join(running, jax.tree.map(lambda part: part[position], pieces))
-        return jax.tree.map(lambda new, old: jnp.where(position < mine, new, old), longer, running)
-
-    return lax.fori_loop(0, count - 1, turn, running)
+def masks_of(axis):
+    return [1 << k for k in range(lax.axis_size(axis).bit_length() - 1)]
+
+
+def swapped(value, axis, mask):
+    count = lax.axis_size(axis)
+    return lax.ppermute(value, axis, [(i, i ^ mask) for i in range(count)])
+
+
+def bit_set(axis, mask):
+    return (lax.axis_index(axis) & mask) != 0
+
+
+def hop_order(axes, upward):
+    places, dim = {}, 0
+    for axis in axes:
+        for mask in reversed(masks_of(axis)):
+            places[axis, mask] = dim
+            dim = dim + 1
+    middle = [("ctx", mask) for mask in masks_of("ctx")[1:]]
+    hops = [("wsh", mask) for mask in masks_of("wsh")] if "wsh" in axes else []
+    hops = hops + (middle if upward else middle[::-1]) + [("ctx", 1)]
+    return [(axis, mask, places[axis, mask]) for axis, mask in hops], dim
+
+
+def gathered(shard, axes, upward):
+    hops, dims = hop_order(axes, upward)
+    block = shard.reshape((1,) * dims + shard.shape)
+    for axis, mask, dim in hops:
+        other = swapped(block, axis, mask)
+        high = bit_set(axis, mask)
+        block = jnp.concatenate(
+            [jnp.where(high, other, block), jnp.where(high, block, other)], axis=dim
+        )
+    return block.reshape((-1,) + shard.shape[1:])
+
+
+def scattered(value, axes, upward, last):
+    hops, dims = hop_order(axes, upward)
+    rows = value.shape[0] >> dims
+    block = value.reshape((2,) * dims + (rows,) + value.shape[1:])
+    for axis, mask, dim in hops[::-1]:
+        high = bit_set(axis, mask).astype(jnp.int32)
+        away = lax.dynamic_index_in_dim(block, 1 - high, dim, keepdims=True)
+        kept = lax.dynamic_index_in_dim(block, high, dim, keepdims=True)
+        other = swapped(away, axis, mask)
+        block = kept.astype(jnp.float32) + other.astype(jnp.float32)
+        if (axis, mask, dim) != hops[0]:
+            block = block.astype(jnp.bfloat16)
+    return block.reshape((rows,) + value.shape[1:]).astype(last)
+
+
+def scan_kernel(forward_first, a_ref, b_ref, local_ref, cum_ref, total_ref, coef_s, term_s):
+    rows, width = a_ref.shape
+    segments = 8
+    length = rows // segments
+    lanes = 128
+    chunks = width // lanes
+    half = chunks // 2
+    ahead = [(chunk < half) == forward_first for chunk in range(chunks)]
+    for chunk in range(chunks):
+        span = pl.ds(chunk * rows, rows)
+        coef_s[span, :] = a_ref[:, pl.ds(chunk * lanes, lanes)]
+        term_s[span, :] = b_ref[:, pl.ds(chunk * lanes, lanes)]
+
+    def step(j, carry):
+        states, prods = carry
+        new_states, new_prods = [], []
+        for chunk in range(chunks):
+            place = j if ahead[chunk] else length - 1 - j
+            where = (pl.ds(chunk * rows + place, segments, stride=length), slice(None))
+            coef = coef_s[where]
+            state = coef * states[chunk] + term_s[where]
+            prod = coef * prods[chunk]
+            term_s[where] = state
+            coef_s[where] = prod
+            new_states.append(state)
+            new_prods.append(prod)
+        return (tuple(new_states), tuple(new_prods))
+
+    zero = jnp.zeros((segments, lanes), jnp.float32)
+    one = jnp.ones((segments, lanes), jnp.float32)
+    states, prods = lax.fori_loop(
+        0, length, step, ((zero,) * chunks, (one,) * chunks), unroll=4
+    )
+    for chunk in range(chunks):
+        cols = pl.ds(chunk * lanes, lanes)
+        carry = jnp.zeros((1, lanes), jnp.float32)
+        prod = jnp.ones((1, lanes), jnp.float32)
+        order = range(segments) if ahead[chunk] else range(segments - 1, -1, -1)
+        for segment in order:
+            span = (pl.ds(segment * length, length), cols)
+            held = pl.ds(chunk * rows + segment * length, length)
+            cum = coef_s[held, :]
+            local_ref[span] = term_s[held, :] + cum * carry
+            cum_ref[span] = cum * prod
+            end_prod = prods[chunk][segment : segment + 1]
+            carry = end_prod * carry + states[chunk][segment : segment + 1]
+            prod = end_prod * prod
+        total_ref[0:1, cols] = prod
+        total_ref[1:2, cols] = carry
+
+
+def scan_both(coefs, terms, forward_first):
+    rows, width = coefs.shape
+    full = jax.ShapeDtypeStruct((rows, width), jnp.float32)
+    whole = pl.BlockSpec(memory_space=pltpu.VMEM)
+    return pl.pallas_call(
+        functools.partial(scan_kernel, forward_first),
+        out_shape=(full, full, jax.ShapeDtypeStruct((8, width), jnp.float32)),
+        in_specs=[whole, whole],
+        out_specs=(whole, whole, whole),
+        scratch_shapes=[pltpu.VMEM((rows * width // 128, 128), jnp.float32)] * 2,
+        compiler_params=pltpu.CompilerParams(vmem_limit_bytes=32 << 20),
+        cost_estimate=pl.CostEstimate(
+            flops=8 * rows * width, bytes_accessed=16 * rows * width, transcendentals=0
+        ),
+        name="scan_both",
+    )(coefs, terms)
+
+
+def carried(totals, forward_first):
+    count, mine = lax.axis_size("ctx"), lax.axis_index("ctx")
+    pieces = lax.all_gather(totals[:2], "ctx")
+    half = totals.shape[1] // 2
+    low = jnp.zeros((1, half), jnp.float32)
+    high = jnp.zeros((1, half), jnp.float32)
+    for position in range(count - 1):
+        back = count - 1 - position
+        first, second = (position, back) if forward_first else (back, position)
+        ahead_ok = (first < mine) if forward_first else (first > mine)
+        behind_ok = (second > mine) if forward_first else (second < mine)
+        low = jnp.where(
+            ahead_ok, pieces[first, 0:1, :half] * low + pieces[first, 1:2, :half], low
+        )
+        high = jnp.where(
+            behind_ok, pieces[second, 0:1, half:] * high + pieces[second, 1:2, half:], high
+        )
+    return jnp.concatenate([low, high], axis=1)
 
 
 def padded_2(cells, sides, width):
@@ -55,10 +182,6 @@
 
 def gelu_exact(values):
     return jax.nn.gelu(values, approximate=False)
-
-
-def linear_step(former, latter):
-    return (former[0] * latter[0], latter[0] * former[1] + latter[1])
 
 
 def doc_index(positions, starts):
@@ -105,33 +228,22 @@
 ):
     f32 = jnp.float32
     bf16 = jnp.bfloat16
-    (
-        attn_gain,
-        qkv_full,
-        out_full,
-        char_gain,
-        gru_full,
-        conv_full,
-        merge_gain,
-        merge_full,
-        up_full,
-        down_full,
-    ) = (
-        lax.all_gather(gain_attn, ("ctx", "wsh"), axis=0, tiled=True),
-        lax.all_gather(qkv_weight, ("ctx", "wsh"), axis=0, tiled=True),
-        lax.all_gather(out_weight, ("ctx", "wsh"), axis=0, tiled=True),
-        lax.all_gather(gain_char, ("ctx", "wsh"), axis=0, tiled=True),
-        lax.all_gather(gru_weight, ("ctx", "wsh"), axis=0, tiled=True),
-        lax.all_gather(conv_weight, ("ctx", "wsh"), axis=0, tiled=True),
-        lax.all_gather(gain_merge, ("ctx", "wsh"), axis=0, tiled=True),
-        lax.all_gather(merge_weight, ("ctx", "wsh"), axis=0, tiled=True),
-        lax.all_gather(up_weight, ("ctx", "wsh"), axis=0, tiled=True),
-        lax.all_gather(down_weight, ("ctx", "wsh"), axis=0, tiled=True),
-    )
-    attn_gain_f = attn_gain.astype(f32)
-    char_gain_f = char_gain.astype(f32)
-    merge_gain_f = merge_gain.astype(f32)
+    every = ("ctx", "wsh")
     width = tokens.shape[2]
+    lane = 128
+    gain_block = jnp.stack([gain_attn, gain_char, gain_merge], axis=1)
+    gain_block = jnp.pad(gain_block, ((0, 0), (0, lane - 3)))
+    gains_and_qkv = gathered(jnp.concatenate([qkv_weight, gain_block], axis=1), every, True)
+    qkv_full = gains_and_qkv[:, : 3 * width]
+    gains = jnp.transpose(gains_and_qkv[:, 3 * width :].astype(f32))
+    attn_gain_f, char_gain_f, merge_gain_f = gains[0], gains[1], gains[2]
+    gru_full = gathered(gru_weight, every, False)
+    out_merge = gathered(jnp.concatenate([out_weight, merge_weight], axis=1), every, False)
+    out_full = out_merge[:, :width]
+    merge_full = out_merge[:, width:]
+    conv_full = gathered(conv_weight, every, True)
+    up_full = gathered(up_weight, every, False)
+    down_full = gathered(down_weight, every, True)
     tok_rows = tokens.shape[1]
     char_rows = chars.shape[1]
     half_width = width // 2
@@ -164,10 +276,8 @@
     queries = qkv[:, :width]
     keys = qkv[:, width : 2 * width]
     values = qkv[:, 2 * width :]
-    keys_all, values_all = (
-        lax.all_gather(keys, "ctx", axis=0, tiled=True),
-        lax.all_gather(values, "ctx", axis=0, tiled=True),
-    )
+    keys_all = gathered(keys, ("ctx",), True)
+    values_all = gathered(values, ("ctx",), False)
     query_heads = queries.reshape(tok_rows, HEADS, HEAD_DIM)
     key_blocks = keys_all.reshape(key_count, key_block, HEADS, HEAD_DIM)
     value_blocks = values_all.reshape(key_count, key_block, HEADS, HEAD_DIM)
@@ -227,18 +337,18 @@
     cand_f = gates[:, half_width : 2 * half_width] * lift
     zeta_b = jax.nn.sigmoid(gates[:, 2 * half_width : 3 * half_width] - shift)
     cand_b = gates[:, 3 * half_width :] * lift
-    identity = (jnp.ones((half_width,), f32), jnp.zeros((half_width,), f32))
     coef_f = (1.0 - zeta_f) * keep_fwd[:, None]
-    cum_f, local_f = lax.associative_scan(linear_step, (coef_f, zeta_f * cand_f))
-    prefix_f = carried_in((cum_f[-1], local_f[-1]), "ctx", linear_step, identity, False)
-    carry_in_f = prefix_f[1]
-    state_f = local_f + cum_f * carry_in_f
     coef_b = (1.0 - zeta_b) * keep_bwd[:, None]
-    cum_b, local_b = lax.associative_scan(linear_step, (coef_b, zeta_b * cand_b), reverse=True)
-    prefix_b = carried_in((cum_b[0], local_b[0]), "ctx", linear_step, identity, True)
-    carry_in_b = prefix_b[1]
-    state_b = local_b + cum_b * carry_in_b
-    mixed = jnp.concatenate([state_f, state_b], axis=1).astype(bf16)
+    coefs = jnp.concatenate([coef_f, coef_b], axis=1)
+    terms = jnp.concatenate([zeta_f * cand_f, zeta_b * cand_b], axis=1)
+    local_state, cum_state, totals = scan_both(coefs, terms, True)
+    carry_in = carried(totals, True)
+    states = local_state + cum_state * carry_in
+    state_f = states[:, :half_width]
+    state_b = states[:, half_width:]
+    carry_in_f = carry_in[0, :half_width]
+    carry_in_b = carry_in[0, half_width:]
+    mixed = states.astype(bf16)
     out_chars = (char_in + mixed.astype(f32)).astype(bf16)
     pooled = (jnp.dot(onehot_low, mixed, preferred_element_type=f32) / root_counts[:, None]).astype(
         bf16
@@ -295,23 +405,18 @@
     grad_resid_norm, grad_merge_gain = merge_norm_back(grad_merge_in)
     grad_resid = cot_tok_f + grad_resid_norm
     grad_mixed = cot_chr_f + jnp.take(grad_pooled / root_counts[:, None], char_map, axis=0)
-    grad_state_f = grad_mixed[:, :half_width]
-    grad_state_b = grad_mixed[:, half_width:]
     shifted_f = jnp.concatenate([coef_f[1:], jnp.ones((1, half_width), f32)], axis=0)
-    cum_gf, local_gf = lax.associative_scan(linear_step, (shifted_f, grad_state_f), reverse=True)
-    prefix_gf = carried_in(
-        (coef_f[0] * cum_gf[0], coef_f[0] * local_gf[0]), "ctx", linear_step, identity, True
-    )
-    lam_f = local_gf + cum_gf * prefix_gf[1]
+    shifted_b = jnp.concatenate([jnp.ones((1, half_width), f32), coef_b[:-1]], axis=0)
+    local_lam, cum_lam, lam_totals = scan_both(
+        jnp.concatenate([shifted_f, shifted_b], axis=1), grad_mixed, False
+    )
+    edge = jnp.concatenate([coef_f[0], coef_b[-1]])[None, :]
+    lams = local_lam + cum_lam * carried(lam_totals[:2] * edge, False)
+    lam_f = lams[:, :half_width]
+    lam_b = lams[:, half_width:]
     prev_f = jnp.concatenate([carry_in_f[None, :], state_f[:-1]], axis=0)
     grad_zeta_f = lam_f * (cand_f - keep_fwd[:, None] * prev_f) * zeta_f * (1.0 - zeta_f)
     grad_cand_f = lam_f * zeta_f * lift
-    shifted_b = jnp.concatenate([jnp.ones((1, half_width), f32), coef_b[:-1]], axis=0)
-    cum_gb, local_gb = lax.associative_scan(linear_step, (shifted_b, grad_state_b))
-    prefix_gb = carried_in(
-        (coef_b[-1] * cum_gb[-1], coef_b[-1] * local_gb[-1]), "ctx", linear_step, identity, False
-    )
-    lam_b = local_gb + cum_gb * prefix_gb[1]
     next_b = jnp.concatenate([state_b[1:], carry_in_b[None, :]], axis=0)
     grad_zeta_b = lam_b * (cand_b - keep_bwd[:, None] * next_b) * zeta_b * (1.0 - zeta_b)
     grad_cand_b = lam_b * zeta_b * lift
@@ -376,25 +481,13 @@
         jnp.zeros((tok_rows, HEADS, HEAD_DIM), f32),
         (key_blocks, value_blocks, key_docs),
     )
-    dk_local, dv_local = (
-        lax.psum_scatter(
-            key_terms[0].reshape(seq_len, width).astype(jnp.bfloat16),
-            "ctx",
-            scatter_dimension=0,
-            tiled=True,
-        ).astype(jnp.float32),
-        lax.psum_scatter(
-            key_terms[1].reshape(seq_len, width).astype(jnp.bfloat16),
-            "ctx",
-            scatter_dimension=0,
-            tiled=True,
-        ).astype(jnp.float32),
-    )
+    dk_local = scattered(key_terms[0].reshape(seq_len, width).astype(bf16), ("ctx",), True, bf16)
+    dv_local = scattered(key_terms[1].reshape(seq_len, width).astype(bf16), ("ctx",), False, bf16)
     grad_qkv_low = jnp.concatenate(
         [
             dq_heads.reshape(tok_rows, width).astype(bf16),
-            dk_local.astype(bf16),
-            dv_local.astype(bf16),
+            dk_local,
+            dv_local,
         ],
         axis=1,
     )
@@ -403,17 +496,27 @@
     _, attn_norm_back = jax.vjp(normed, token_in, attn_gain_f)
     grad_token_in, grad_attn_gain = attn_norm_back(grad_attn_in)
     grad_tokens_out = (grad_stream + grad_token_in).astype(bf16)
+    gain_grads = jnp.stack([grad_attn_gain, grad_char_gain, grad_merge_gain], axis=1)
+    gain_grads = jnp.pad(gain_grads, ((0, 0), (0, lane - 3)))
+    down_shard = scattered(grad_down.astype(bf16), every, True, f32)
+    up_shard = scattered(grad_up.astype(bf16), every, False, f32)
+    merge_conv = jnp.concatenate([grad_merge.astype(bf16), grad_conv.astype(bf16)], axis=1)
+    merge_conv = scattered(merge_conv, every, True, f32)
+    gru_out = jnp.concatenate([grad_gru.astype(bf16), grad_out_proj.astype(bf16)], axis=1)
+    gru_out = scattered(gru_out, every, False, f32)
+    qkv_shard = scattered(grad_qkv.astype(bf16), every, True, f32)
+    gain_shard = scattered(gain_grads.astype(bf16), every, False, f32)
     shards = (
-        lax.psum_scatter(grad_attn_gain, ("ctx", "wsh"), scatter_dimension=0, tiled=True),
-        lax.psum_scatter(grad_qkv, ("ctx", "wsh"), scatter_dimension=0, tiled=True),
-        lax.psum_scatter(grad_out_proj, ("ctx", "wsh"), scatter_dimension=0, tiled=True),
-        lax.psum_scatter(grad_char_gain, ("ctx", "wsh"), scatter_dimension=0, tiled=True),
-        lax.psum_scatter(grad_gru, ("ctx", "wsh"), scatter_dimension=0, tiled=True),
-        lax.psum_scatter(grad_conv, ("ctx", "wsh"), scatter_dimension=0, tiled=True),
-        lax.psum_scatter(grad_merge_gain, ("ctx", "wsh"), scatter_dimension=0, tiled=True),
-        lax.psum_scatter(grad_merge, ("ctx", "wsh"), scatter_dimension=0, tiled=True),
-        lax.psum_scatter(grad_up, ("ctx", "wsh"), scatter_dimension=0, tiled=True),
-        lax.psum_scatter(grad_down, ("ctx", "wsh"), scatter_dimension=0, tiled=True),
+        gain_shard[:, 0],
+        qkv_shard,
+        gru_out[:, 2 * width :],
+        gain_shard[:, 1],
+        gru_out[:, : 2 * width],
+        merge_conv[:, width:],
+        gain_shard[:, 2],
+        merge_conv[:, :width],
+        up_shard,
+        down_shard,
     )
     return (
         out_tok[None],

time: 2030 us -> 892 us (0.44); the launches traced: 1990 us -> 880 us
  local copies, waits for them, and re-layouts: 786 us -> 177 us
  waiting for transfers between devices: 612 us -> 278 us
  blocking collectives: 213 us -> 85.8 us
  other arithmetic: 214 us -> 108 us
  starting transfers between devices: 18.8 us -> 87.3 us
  Pallas kernels: 0 us -> 27.3 us
    slice x284 -> x10, local copies, waits for them, and re-layouts: 535 us -> 5.97 us  [the longest x1 1.93 us: body(): prev_f = jnp.concatenate([carry_in_f[None, :], state_f[:-1]], axis=0)]
    reduce_scatter x8 -> x0, waiting for transfers between devices: 417 us -> none  [the longest x1 142 us: body(): lax.psum_scatter(grad_down, ('ctx', 'wsh'), scatter_dimension=0, tiled=True)]
    ppermute x0 -> x72, waiting for transfers between devices: none -> 278 us  [swapped(): return lax.ppermute(value, axis, [(i, i ^ mask) for i in range(count)])]
    unnamed x19 -> x0, waiting for transfers between devices: 131 us -> none
    unnamed x2 -> x0, blocking collectives: 89.2 us -> none
    pad x144 -> x1, local copies, waits for them, and re-layouts: 85.5 us -> 0.97 us  [body(): gain_grads = jnp.pad(gain_grads, ((0, 0), (0, lane - 3)))]
    ppermute x0 -> x72, starting transfers between devices: none -> 78.3 us  [swapped(): return lax.ppermute(value, axis, [(i, i ^ mask) for i in range(count)])]
    add x112 -> x1, other arithmetic: 67.9 us -> 0.4 us  [body(): lams = local_lam + cum_lam * carried(lam_totals[:2] * edge, False)]
  transfers between devices with their start and end apart: 22 -> 76, of which waited for: 7 -> 36; matrix products, arithmetic and copies ran while one was open for 52% -> 27% of each run, Pallas kernels for 0% -> 3%
where the time goes in v1:
time: 892 us; the launch traced here: 880 us
  waiting for transfers between devices  278 us (31%)
  local copies, waits for them, and re-layouts  177 us (20%)
  other arithmetic  108 us (12%)
  starting transfers between devices  87.3 us (10%)
  matrix products  86.7 us (10%)
  blocking collectives  85.8 us (10%)
  Pallas kernels  27.3 us (3%)
  loops' own time  21.1 us (2%)
  between operations  9.28 us (1%)
    ppermute x72, waiting for transfers between devices, swapped(): return lax.ppermute(value, axis, [(i, i ^ mask) for i in range(count)])  278 us
    ppermute x72, starting transfers between devices, swapped(): return lax.ppermute(value, axis, [(i, i ^ mask) for i in range(count)])  78.3 us
    all_gather x2, blocking collectives, carried(): pieces = lax.all_gather(totals[:2], 'ctx')  36.9 us
    psum x1, blocking collectives, body(): lax.psum((jnp.sum(proj * proj), jnp.sum(token_in * proj), jnp.sum(token_i...  36.3 us
    pallas_call x2, Pallas kernels, scan_both(): pl.pallas_call(functools.partial(scan_kernel, forward_first), out_shape=(...  27.3 us
    unnamed x276, local copies, waits for them, and re-layouts  23.8 us
    dynamic_slice x2, local copies, waits for them, and re-layouts, scattered(): kept = lax.dynamic_index_in_dim(block, high, dim, keepdims=True)  23.5 us
    concatenate x36, other arithmetic, gathered(): jnp.concatenate([jnp.where(high, other, block), jnp.where(high, block, ot...  22.4 us
  transfers between devices with their start and end apart: 76, of which 36 were waited for; matrix products, arithmetic and copies ran while one was open for 27% of the time, Pallas kernels for 3%

profile of v1, /device:TPU:0, one launch (start us, length us, event | category | flops | bytes accessed | tf_op | source)
XLA Modules:
  0.0 880.1 jit_solution(13386713058028667862)
XLA Ops:
  32.8 20.4 %collective-permute-done.12 = bf16[1,1,1,1,2,24,1536]{6,5,4,3,2,1,0:T(8,128)(2,1)S(1)} collective-permute-done((bf16[1,1,1,1,2,24,1536]{6,5,4,3,2,1,0:T(8,128)(2,1)S(1)}, bf16[1,1,1,1,2,24,1536]{6,5,4,3,2,1,0:T(8,128)(2,1)S(1)}, u32[]{:S(2)}, u32[]{:S(2)}) %collective-permute-start.12) | collective-permute-done | bytes 147488 | tf_op jit(solution)/shard_map/ppermute | solution.py:24
  108.9 11.0 %collective-permute-done.14 = bf16[2,1,1,2,2,24,1536]{6,5,4,3,2,1,0:T(8,128)(2,1)S(1)} collective-permute-done((bf16[2,1,1,2,2,24,1536]{6,5,4,3,2,1,0:T(8,128)(2,1)S(1)}, bf16[2,1,1,2,2,24,1536]{6,5,4,3,2,1,0:T(8,128)(2,1)S(1)}, u32[]{:S(2)}, u32[]{:S(2)}) %collective-permute-start.14) | collective-permute-done | bytes 589856 | tf_op jit(solution)/shard_map/ppermute | solution.py:24
  121.6 10.9 %collective-permute-done.19 = bf16[2,1,1,2,2,24,1536]{6,5,4,3,2,1,0:T(8,128)(2,1)S(1)} collective-permute-done((bf16[2,1,1,2,2,24,1536]{6,5,4,3,2,1,0:T(8,128)(2,1)S(1)}, bf16[2,1,1,2,2,24,1536]{6,5,4,3,2,1,0:T(8,128)(2,1)S(1)}, u32[]{:S(2)}, u32[]{:S(2)}) %collective-permute-start.19) | collective-permute-done | bytes 589856 | tf_op jit(solution)/shard_map/ppermute | solution.py:24
  139.2 15.5 %collective-permute-done.31 = bf16[2,1,1,2,2,24,3072]{6,5,4,3,2,1,0:T(8,128)(2,1)S(1)} collective-permute-done((bf16[2,1,1,2,2,24,3072]{6,5,4,3,2,1,0:T(8,128)(2,1)S(1)}, bf16[2,1,1,2,2,24,3072]{6,5,4,3,2,1,0:T(8,128)(2,1)S(1)}, u32[]{:S(2)}, u32[]{:S(2)}) %collective-permute-start.31) | collective-permute-done | bytes 1179680 | tf_op jit(solution)/shard_map/ppermute | solution.py:24
  187.2 13.6 %scan_both.2 = (f32[1024,768]{1,0:T(8,128)S(1)}, f32[1024,768]{1,0:T(8,128)S(1)}, f32[8,768]{1,0:T(8,128)S(1)}) custom-call(f32[1024,768]{1,0:T(8,128)S(1)} %pad_maximum_fusion.8.a_ref, f32[1024,768]{1,0:T(8,128)S(1)} %pad_maximum_fusion.9.b_ref), custom_call_target="tpu_custom_call" | custom-call | flops 6291456 | bytes 12582912 | tf_op jit(solution)/shard_map/scan_both/pallas_call | solution.py:125
  200.8 8.2 all-gather.2
  232.7 14.9 %collective-permute-done.6 = bf16[1,2,1,256,768]{4,3,2,1,0:T(8,128)(2,1)S(1)} collective-permute-done((bf16[1,2,1,256,768]{4,3,2,1,0:T(8,128)(2,1)S(1)}, bf16[1,2,1,256,768]{4,3,2,1,0:T(8,128)(2,1)S(1)}, u32[]{:S(2)}, u32[]{:S(2)}) %collective-permute-start.6) | collective-permute-done | bytes 786464 | tf_op jit(solution)/shard_map/ppermute | solution.py:24
  265.0 8.6 copy.149
  283.4 8.6 copy.147
  299.6 34.5 %while.31 = (s32[]{:T(128)}, f32[12,256]{1,0:T(8,128)S(1)}, f32[12,256]{1,0:T(8,128)}, f32[12,256,64]{1,2,0:T(8,128)}, s32[256]{0:T(256)}, /*index=5*/s32[4,512]...) while((s32[]{:T(128)}, f32[12,256]{1,0:T(8,128)S(1)}, ...), condition=%wide.region_10.11_spmd, body=%wide.region_5.10_spmd.sunk | while | flops 423630848 | bytes 29532600 | solution.py:315
  306.1 8.6 conditional.4
  339.4 36.3 %all-reduce.5 = (f32[]{:T(128)}, f32[]{:T(128)}, f32[]{:T(128)}) all-reduce(f32[]{:T(128)} %get-tuple-element.347, f32[]{:T(128)} %get-tuple-element.348, f32[]{:T(128)} %get-tuple-element.346), channel_id=1, replica_groups=mesh['ctx'=8,'wsh'=4] {'ctx'}, use_global_device_ids=true, to_apply=%region_12.13 | all-reduce | flops 3 | bytes 24 | tf_op jit(solution)/shard_map/psum | solution.py:322
  384.2 9.0 %multiply_convert_fusion = (bf16[256,3072]{1,0:T(8,128)(2,1)}, f32[256,3072]{1,0:T(8,128)S(1)}, f32[256,3072]{1,0:T(8,128)S(1)}) fusion(bf16[256,768]{1,0:T(8,128)(2,1)S(1)} %get-tuple-element.414, bf16[768,3072]{1,0:T(8,128)(2,1)S(1)} %bitcast.808), kind=kOutput, calls=%fused_computation.109 | convolution fusion | flops 1259077632 | bytes 12976128 | tf_op jit(solution)/shard_map/dot_general | solution.py:367
  415.8 12.6 %all-reduce.4 = (f32[]{:T(128)}, f32[]{:T(128)}) all-reduce(f32[]{:T(128)} %get-tuple-element.345, f32[]{:T(128)} %get-tuple-element.344), channel_id=1, replica_groups=mesh['ctx'=8,'wsh'=4] {'ctx'}, use_global_device_ids=true, to_apply=%region_31.32 | all-reduce | flops 2 | bytes 16 | tf_op jit(solution)/shard_map/psum | solution.py:431
  470.3 39.6 %while.32 = (s32[]{:T(128)}, f32[256,12,64]{0,2,1:T(8,128)}, bf16[4,512,12,64]{1,3,2,0:T(8,128)(2,1)}, bf16[4,512,12,64]{1,3,2,0:T(8,128)(2,1)}, s32[256]{0:T(25...) while((s32[]{:T(128)}, f32[256,12,64]{0,2,1:T(8,128)}, ...), condition=%wide.region_35.36_spmd, body=%wide.region_32.35_spmd.sunk | while | flops 1023672320 | bytes 46941680 | solution.py:479
  476.2 10.0 %conditional.5 = (f32[256,12,64]{0,2,1:T(8,128)}, bf16[1,512,12,64]{1,3,2,0:T(8,128)(2,1)S(1)}, bf16[1,512,12,64]{1,3,2,0:T(8,128)(2,1)S(1)}) conditional(s32[]{:T(128)} %convert_element_type.966, f32[256,12,64]{0,2,1:T(8,128)} %get-tuple-element.767, (s32[256]{0:T(256)}, s32[1,512]{1,0:T(1,128)S(1)}, bf16[4,512,12,64]{1,3,2,0:T(8,128)(2,1)}, ...), branch_computations={%region_33.33_spmd, %region_34.34_spmd} | conditional | flops 1023672320 | bytes 43791040 | solution.py:477
  515.7 11.0 %constant_dynamic-slice_fusion.43 = (bf16[2,2,1,256,768]{3,2,4,1,0:T(2,128)(2,1)}, bf16[2,2,1,256,768]{3,2,4,1,0:T(2,128)(2,1)S(1)}) fusion(bf16[2,2,2,256,768]{3,2,4,1,0:T(2,128)(2,1)} %convert_element_type.565, s32[]{:T(128)S(6)} %select_n.1073, s32[]{:T(128)S(6)} %select_n.1074), kind=kLoop, calls=%fused_computation.456 | loop fusion | bytes 6291464 | tf_op jit(solution)/shard_map/jit(dynamic_index_in_dim)/dynamic_slice | solution.py:62
  528.3 11.0 %collective-permute-start.38 = (bf16[2,2,1,256,768]{3,4,2,1,0:T(8,128)(2,1)}, bf16[2,2,1,256,768]{3,4,2,1,0:T(8,128)(2,1)}, u32[]{:S(2)}, u32[]{:S(2)}) collective-permute-start(bf16[2,2,1,256,768]{3,4,2,1,0:T(8,128)(2,1)} %copy.180), channel_id=1, source_target_pairs={{0,4},{4,0},{8,12},{12,8},{16,20},{20,16},{24,28},{28,24},{1,5},{5... | collective-permute-start | bytes 4718600 | tf_op jit(solution)/shard_map/ppermute | solution.py:24
  544.9 12.5 %constant_dynamic-slice_fusion.39 = (bf16[2,2,1,256,768]{3,2,4,1,0:T(2,128)(2,1)}, bf16[2,2,1,256,768]{3,2,4,1,0:T(2,128)(2,1)}) fusion(bf16[2,2,2,256,768]{3,2,4,1,0:T(2,128)(2,1)} %convert_element_type.580, s32[]{:T(128)S(6)} %select_n.1073, s32[]{:T(128)S(6)} %select_n.1074), kind=kLoop, calls=%fused_computation.452 | loop fusion | bytes 6291464 | tf_op jit(solution)/shard_map/jit(dynamic_index_in_dim)/dynamic_slice | solution.py:62
  557.4 8.2 copy.155
  565.6 8.2 copy.181
  590.8 13.6 %scan_both.3 = (f32[1024,768]{1,0:T(8,128)S(1)}, f32[1024,768]{1,0:T(8,128)S(1)}, f32[8,768]{1,0:T(8,128)S(1)}) custom-call(f32[1024,768]{1,0:T(8,128)S(1)} %select_maximum_fusion.a_ref, f32[1024,768]{1,0:T(8,128)S(1)} %convert_add_fusion.1.b_ref), custom_call_target="tpu_custom_call" | custom-call | flops 6291456 | bytes 12582912 | tf_op jit(solution)/shard_map/scan_both/pallas_call | solution.py:125
  604.5 28.7 %all-gather.3 = f32[8,2,768]{2,1,0:T(2,128)S(1)} all-gather(f32[1,2,768]{2,1,0:T(2,128)S(1)} %multiply_bitcast_fusion.1), channel_id=3, replica_groups=mesh['ctx'=8,'wsh'=4] {'ctx'}, dimensions={0}, use_global_device_ids=true | all-gather | bytes 55296 | tf_op jit(solution)/shard_map/all_gather | solution.py:141
  678.7 17.9 %collective-permute-done.57 = bf16[2,1,1,2,2,24,2304]{6,5,4,3,2,1,0:T(8,128)(2,1)S(1)} collective-permute-done((bf16[2,1,1,2,2,24,2304]{6,5,4,3,2,1,0:T(8,128)(2,1)S(1)}, bf16[2,1,1,2,2,24,2304]{6,5,4,3,2,1,0:T(8,128)(2,1)S(1)}, u32[]{:S(2)}, u32[]{:S(2)}) %collective-permute-start.57) | collective-permute-done | bytes 884768 | tf_op jit(solution)/shard_map/ppermute | solution.py:24
  699.4 33.5 %collective-permute-done.43 = bf16[1,1,1,256,768]{4,3,2,1,0:T(8,128)(2,1)S(1)} collective-permute-done((bf16[1,1,1,256,768]{4,3,2,1,0:T(8,128)(2,1)S(1)}, bf16[1,1,1,256,768]{4,3,2,1,0:T(8,128)(2,1)S(1)}, u32[]{:S(2)}, u32[]{:S(2)}) %collective-permute-start.43) | collective-permute-done | bytes 393248 | tf_op jit(solution)/shard_map/ppermute | solution.py:24
  763.0 12.3 %collective-permute-done.59 = bf16[1,1,1,1,2,24,2304]{6,5,4,3,2,1,0:T(8,128)(2,1)S(1)} collective-permute-done((bf16[1,1,1,1,2,24,2304]{6,5,4,3,2,1,0:T(8,128)(2,1)S(1)}, bf16[1,1,1,1,2,24,2304]{6,5,4,3,2,1,0:T(8,128)(2,1)S(1)}, u32[]{:S(2)}, u32[]{:S(2)}) %collective-permute-start.59) | collective-permute-done | bytes 221216 | tf_op jit(solution)/shard_map/ppermute | solution.py:24
  791.1 8.5 collective-permute-done.73
  803.1 7.3 collective-permute-done.63
  810.7 15.0 %collective-permute-done.74 = bf16[1,1,1,1,2,96,768]{6,5,4,3,2,1,0:T(8,128)(2,1)S(1)} collective-permute-done((bf16[1,1,1,1,2,96,768]{6,5,4,3,2,1,0:T(8,128)(2,1)S(1)}, bf16[1,1,1,1,2,96,768]{6,5,4,3,2,1,0:T(8,128)(2,1)S(1)}, u32[]{:S(2)}, u32[]{:S(2)}) %collective-permute-start.74) | collective-permute-done | bytes 294944 | tf_op jit(solution)/shard_map/ppermute | solution.py:24
  838.0 15.2 %collective-permute-done.52 = bf16[1,2,1,2,2,24,2304]{6,5,4,3,2,1,0:T(8,128)(2,1)S(1)} collective-permute-done((bf16[1,2,1,2,2,24,2304]{6,5,4,3,2,1,0:T(8,128)(2,1)S(1)}, bf16[1,2,1,2,2,24,2304]{6,5,4,3,2,1,0:T(8,128)(2,1)S(1)}, u32[]{:S(2)}, u32[]{:S(2)}) %collective-permute-start.52) | collective-permute-done | bytes 884768 | tf_op jit(solution)/shard_map/ppermute | solution.py:24
  856.0 7.7 collective-permute-done.53
  864.6 9.5 %collective-permute-done.54 = bf16[1,1,1,1,2,24,2304]{6,5,4,3,2,1,0:T(8,128)(2,1)S(1)} collective-permute-done((bf16[1,1,1,1,2,24,2304]{6,5,4,3,2,1,0:T(8,128)(2,1)S(1)}, bf16[1,1,1,1,2,24,2304]{6,5,4,3,2,1,0:T(8,128)(2,1)S(1)}, u32[]{:S(2)}, u32[]{:S(2)}) %collective-permute-start.54) | collective-permute-done | bytes 221216 | tf_op jit(solution)/shard_map/ppermute | solution.py:24
  (761 shorter events, 460.5 us)
Async XLA Ops:
  26.4 30.0 %collective-permute-start.17 = (bf16[1,1,1,1,2,24,1536]{6,5,4,3,2,1,0:T(8,128)(2,1)S(1)}, bf16[1,1,1,1,2,24,1536]{6,5,4,3,2,1,0:T(8,128)(2,1)S(1)}, u32[]{:S(2)}, u32[]{:S(2)}) collective-permute-start(bf16[1,1,1,1,2,24,1536]{6,5,4,3,2,1,0:T(8,128)(2,1)S(1)} %pad_maximum_fusion.55), channel_id=1, source_target_pairs={{0,2},{1,3},{2,0},{3,1},{4,6},{5,7},{6,4},{7,5},{8,10},{9,11},{10,... | collective-permute-start | bytes 442376 | tf_op jit(solution)/shard_map/ppermute | solution.py:24
  26.6 40.9 %collective-permute-start.23 = (bf16[1,1,1,1,2,24,2304]{6,5,4,3,2,1,0:T(8,128)(2,1)S(1)}, bf16[1,1,1,1,2,24,2304]{6,5,4,3,2,1,0:T(8,128)(2,1)S(1)}, u32[]{:S(2)}, u32[]{:S(2)}) collective-permute-start(bf16[1,1,1,1,2,24,2304]{6,5,4,3,2,1,0:T(8,128)(2,1)S(1)} %pad_maximum_fusion.53), channel_id=1, source_target_pairs={{0,2},{1,3},{2,0},{3,1},{4,6},{5,7},{6,4},{7,5},{8,10},{9,11},{10,... | collective-permute-start | bytes 663560 | tf_op jit(solution)/shard_map/ppermute | solution.py:24
  29.6 42.8 %collective-permute-start.1 = (bf16[1,1,1,1,2,24,2432]{6,5,4,3,2,1,0:T(8,128)(2,1)S(1)}, bf16[1,1,1,1,2,24,2432]{6,5,4,3,2,1,0:T(8,128)(2,1)S(1)}, u32[]{:S(2)}, u32[]{:S(2)}) collective-permute-start(bf16[1,1,1,1,2,24,2432]{6,5,4,3,2,1,0:T(8,128)(2,1)S(1)} %pad_maximum_fusion.52), channel_id=1, source_target_pairs={{0,2},{1,3},{2,0},{3,1},{4,6},{5,7},{6,4},{7,5},{8,10},{9,11},{10,... | collective-permute-start | bytes 700424 | tf_op jit(solution)/shard_map/ppermute | solution.py:24
  29.8 49.0 %collective-permute-start.29 = (bf16[1,1,1,1,2,24,3072]{6,5,4,3,2,1,0:T(8,128)(2,1)S(1)}, bf16[1,1,1,1,2,24,3072]{6,5,4,3,2,1,0:T(8,128)(2,1)S(1)}, u32[]{:S(2)}, u32[]{:S(2)}) collective-permute-start(bf16[1,1,1,1,2,24,3072]{6,5,4,3,2,1,0:T(8,128)(2,1)S(1)} %pad_maximum_fusion.46), channel_id=1, source_target_pairs={{0,2},{1,3},{2,0},{3,1},{4,6},{5,7},{6,4},{7,5},{8,10},{9,11},{10,... | collective-permute-start | bytes 884744 | tf_op jit(solution)/shard_map/ppermute | solution.py:24
  53.2 30.3 %collective-permute-start.34 = (bf16[1,1,1,1,2,96,768]{6,5,4,3,2,1,0:T(8,128)(2,1)S(1)}, bf16[1,1,1,1,2,96,768]{6,5,4,3,2,1,0:T(8,128)(2,1)S(1)}, u32[]{:S(2)}, u32[]{:S(2)}) collective-permute-start(bf16[1,1,1,1,2,96,768]{6,5,4,3,2,1,0:T(8,128)(2,1)S(1)} %pad_maximum_fusion.47), channel_id=1, source_target_pairs={{0,2},{1,3},{2,0},{3,1},{4,6},{5,7},{6,4},{7,5},{8,10},{9,11},{10,... | collective-permute-start | bytes 884744 | tf_op jit(solution)/shard_map/ppermute | solution.py:24
  86.8 33.0 %collective-permute-start.14 = (bf16[2,1,1,2,2,24,1536]{6,5,4,3,2,1,0:T(8,128)(2,1)S(1)}, bf16[2,1,1,2,2,24,1536]{6,5,4,3,2,1,0:T(8,128)(2,1)S(1)}, u32[]{:S(2)}, u32[]{:S(2)}) collective-permute-start(bf16[2,1,1,2,2,24,1536]{6,5,4,3,2,1,0:T(8,128)(2,1)S(1)} %pad_maximum_fusion.28), channel_id=1, source_target_pairs={{0,8},{4,12},{8,0},{12,4},{16,24},{20,28},{24,16},{28,20},{1,9},{5... | collective-permute-start | bytes 1769480 | tf_op jit(solution)/shard_map/ppermute | solution.py:24
  87.6 44.9 %collective-permute-start.19 = (bf16[2,1,1,2,2,24,1536]{6,5,4,3,2,1,0:T(8,128)(2,1)S(1)}, bf16[2,1,1,2,2,24,1536]{6,5,4,3,2,1,0:T(8,128)(2,1)S(1)}, u32[]{:S(2)}, u32[]{:S(2)}) collective-permute-start(bf16[2,1,1,2,2,24,1536]{6,5,4,3,2,1,0:T(8,128)(2,1)S(1)} %pad_maximum_fusion.29), channel_id=1, source_target_pairs={{0,8},{4,12},{8,0},{12,4},{16,24},{20,28},{24,16},{28,20},{1,9},{5... | collective-permute-start | bytes 1769480 | tf_op jit(solution)/shard_map/ppermute | solution.py:24
  94.6 38.1 %collective-permute-start.25 = (bf16[1,2,1,2,2,24,2304]{6,5,4,3,2,1,0:T(8,128)(2,1)S(1)}, bf16[1,2,1,2,2,24,2304]{6,5,4,3,2,1,0:T(8,128)(2,1)S(1)}, u32[]{:S(2)}, u32[]{:S(2)}) collective-permute-start(bf16[1,2,1,2,2,24,2304]{6,5,4,3,2,1,0:T(8,128)(2,1)S(1)} %pad_maximum_fusion.25), channel_id=1, source_target_pairs={{0,16},{4,20},{8,24},{12,28},{16,0},{20,4},{24,8},{28,12},{1,17},{... | collective-permute-start | bytes 2654216 | tf_op jit(solution)/shard_map/ppermute | solution.py:24
  99.8 39.0 %collective-permute-start.3 = (bf16[1,2,1,2,2,24,2432]{6,5,4,3,2,1,0:T(8,128)(2,1)S(1)}, bf16[1,2,1,2,2,24,2432]{6,5,4,3,2,1,0:T(8,128)(2,1)S(1)}, u32[]{:S(2)}, u32[]{:S(2)}) collective-permute-start(bf16[1,2,1,2,2,24,2432]{6,5,4,3,2,1,0:T(8,128)(2,1)S(1)} %pad_maximum_fusion.24), channel_id=1, source_target_pairs={{0,16},{4,20},{8,24},{12,28},{16,0},{20,4},{24,8},{28,12},{1,17},{... | collective-permute-start | bytes 2801672 | tf_op jit(solution)/shard_map/ppermute | solution.py:24
  107.2 47.5 %collective-permute-start.31 = (bf16[2,1,1,2,2,24,3072]{6,5,4,3,2,1,0:T(8,128)(2,1)S(1)}, bf16[2,1,1,2,2,24,3072]{6,5,4,3,2,1,0:T(8,128)(2,1)S(1)}, u32[]{:S(2)}, u32[]{:S(2)}) collective-permute-start(bf16[2,1,1,2,2,24,3072]{6,5,4,3,2,1,0:T(8,128)(2,1)S(1)} %pad_maximum_fusion.21), channel_id=1, source_target_pairs={{0,8},{4,12},{8,0},{12,4},{16,24},{20,28},{24,16},{28,20},{1,9},{5... | collective-permute-start | bytes 3538952 | tf_op jit(solution)/shard_map/ppermute | solution.py:24
  119.9 41.7 %collective-permute-start.36 = (bf16[1,2,1,2,2,96,768]{6,5,4,3,2,1,0:T(8,128)(2,1)S(1)}, bf16[1,2,1,2,2,96,768]{6,5,4,3,2,1,0:T(8,128)(2,1)S(1)}, u32[]{:S(2)}, u32[]{:S(2)}) collective-permute-start(bf16[1,2,1,2,2,96,768]{6,5,4,3,2,1,0:T(8,128)(2,1)S(1)} %pad_maximum_fusion.22), channel_id=1, source_target_pairs={{0,16},{4,20},{8,24},{12,28},{16,0},{20,4},{24,8},{28,12},{1,17},{... | collective-permute-start | bytes 3538952 | tf_op jit(solution)/shard_map/ppermute | solution.py:24
  132.5 31.4 %collective-permute-start.15 = (bf16[2,2,1,2,2,24,1536]{6,5,4,3,2,1,0:T(8,128)(2,1)S(1)}, bf16[2,2,1,2,2,24,1536]{6,5,4,3,2,1,0:T(8,128)(2,1)S(1)}, u32[]{:S(2)}, u32[]{:S(2)}) collective-permute-start(bf16[2,2,1,2,2,24,1536]{6,5,4,3,2,1,0:T(8,128)(2,1)S(1)} %pad_maximum_fusion.19), channel_id=1, source_target_pairs={{0,4},{4,0},{8,12},{12,8},{16,20},{20,16},{24,28},{28,24},{1,5},{5... | collective-permute-start | bytes 3538952 | tf_op jit(solution)/shard_map/ppermute | solution.py:24
  132.7 31.8 %collective-permute-start.20 = (bf16[2,2,1,2,2,24,1536]{6,5,4,3,2,1,0:T(8,128)(2,1)S(1)}, bf16[2,2,1,2,2,24,1536]{6,5,4,3,2,1,0:T(8,128)(2,1)S(1)}, u32[]{:S(2)}, u32[]{:S(2)}) collective-permute-start(bf16[2,2,1,2,2,24,1536]{6,5,4,3,2,1,0:T(8,128)(2,1)S(1)} %pad_maximum_fusion.20), channel_id=1, source_target_pairs={{0,4},{4,0},{8,12},{12,8},{16,20},{20,16},{24,28},{28,24},{1,5},{5... | collective-permute-start | bytes 3538952 | tf_op jit(solution)/shard_map/ppermute | solution.py:24
  161.5 94.9 %collective-permute-start.32 = (bf16[2,2,1,2,2,24,3072]{6,5,4,3,2,1,0:T(8,128)(2,1)}, bf16[2,2,1,2,2,24,3072]{6,5,4,3,2,1,0:T(8,128)(2,1)}, u32[]{:S(2)}, u32[]{:S(2)}) collective-permute-start(bf16[2,2,1,2,2,24,3072]{6,5,4,3,2,1,0:T(8,128)(2,1)} %pad_maximum_fusion.13), channel_id=1, source_target_pairs={{0,4},{4,0},{8,12},{12,8},{16,20},{20,16},{24,28},{28,24},{1,5},{5... | collective-permute-start | bytes 7077896 | tf_op jit(solution)/shard_map/ppermute | solution.py:24
  163.9 86.5 %collective-permute-start.37 = (bf16[2,2,1,2,2,96,768]{6,5,4,3,2,1,0:T(8,128)(2,1)}, bf16[2,2,1,2,2,96,768]{6,5,4,3,2,1,0:T(8,128)(2,1)}, u32[]{:S(2)}, u32[]{:S(2)}) collective-permute-start(bf16[2,2,1,2,2,96,768]{6,5,4,3,2,1,0:T(8,128)(2,1)} %pad_maximum_fusion.14), channel_id=1, source_target_pairs={{0,4},{4,0},{8,12},{12,8},{16,20},{20,16},{24,28},{28,24},{1,5},{5... | collective-permute-start | bytes 7077896 | tf_op jit(solution)/shard_map/ppermute | solution.py:24
  178.0 44.0 %collective-permute-start.5 = (bf16[1,1,1,256,768]{4,3,2,1,0:T(8,128)(2,1)}, bf16[1,1,1,256,768]{4,3,2,1,0:T(8,128)(2,1)}, u32[]{:S(2)}, u32[]{:S(2)}) collective-permute-start(bf16[1,1,1,256,768]{4,3,2,1,0:T(8,128)(2,1)} %get-tuple-element.484), channel_id=1, source_target_pairs={{0,8},{4,12},{8,0},{12,4},{16,24},{20,28},{24,16},{28,20},{1,9},{5... | collective-permute-start | bytes 1179656 | tf_op jit(solution)/shard_map/ppermute | solution.py:24
  179.5 46.0 %collective-permute-start.8 = (bf16[1,1,1,256,768]{4,3,2,1,0:T(8,128)(2,1)}, bf16[1,1,1,256,768]{4,3,2,1,0:T(8,128)(2,1)}, u32[]{:S(2)}, u32[]{:S(2)}) collective-permute-start(bf16[1,1,1,256,768]{4,3,2,1,0:T(8,128)(2,1)} %get-tuple-element.482), channel_id=1, source_target_pairs={{0,16},{4,20},{8,24},{12,28},{16,0},{20,4},{24,8},{28,12},{1,17},{... | collective-permute-start | bytes 1179656 | tf_op jit(solution)/shard_map/ppermute | solution.py:24
  444.0 214.6 %collective-permute-start.71 = (bf16[2,2,1,2,2,96,768]{6,5,4,3,2,1,0:T(8,128)(2,1)}, bf16[2,2,1,2,2,96,768]{6,5,4,3,2,1,0:T(8,128)(2,1)}, u32[]{:S(2)}, u32[]{:S(2)}) collective-permute-start(bf16[2,2,1,2,2,96,768]{6,5,4,3,2,1,0:T(8,128)(2,1)} %constant_dynamic-slice_fusion.8), channel_id=1, source_target_pairs={{0,4},{4,0},{8,12},{12,8},{16,20},{20,16},{24,28},{28,24},{1,5},{5... | collective-permute-start | bytes 7077896 | tf_op jit(solution)/shard_map/ppermute | solution.py:24
  445.8 217.8 %collective-permute-start.66 = (bf16[2,2,1,2,2,24,3072]{6,5,4,3,2,1,0:T(8,128)(2,1)}, bf16[2,2,1,2,2,24,3072]{6,5,4,3,2,1,0:T(8,128)(2,1)}, u32[]{:S(2)}, u32[]{:S(2)}) collective-permute-start(bf16[2,2,1,2,2,24,3072]{6,5,4,3,2,1,0:T(8,128)(2,1)} %constant_dynamic-slice_fusion.13), channel_id=1, source_target_pairs={{0,4},{4,0},{8,12},{12,8},{16,20},{20,16},{24,28},{28,24},{1,5},{5... | collective-permute-start | bytes 7077896 | tf_op jit(solution)/shard_map/ppermute | solution.py:24
  459.8 116.6 %collective-permute-start.45 = (bf16[1,768]{1,0:T(2,128)(2,1)}, bf16[1,768]{1,0:T(2,128)(2,1)}, u32[]{:S(2)}, u32[]{:S(2)}) collective-permute-start(bf16[1,768]{1,0:T(2,128)(2,1)} %get-tuple-element.506), channel_id=1, source_target_pairs={{0,4},{4,8},{8,12},{12,16},{16,20},{20,24},{24,28},{1,5},{5,9},{9,... | collective-permute-start | bytes 4616 | tf_op jit(solution)/shard_map/ppermute | solution.py:167
  462.8 115.5 %collective-permute-start.44 = (bf16[1,768]{1,0:T(2,128)(2,1)}, bf16[1,768]{1,0:T(2,128)(2,1)}, u32[]{:S(2)}, u32[]{:S(2)}) collective-permute-start(bf16[1,768]{1,0:T(2,128)(2,1)} %get-tuple-element.505), channel_id=1, source_target_pairs={{4,0},{8,4},{12,8},{16,12},{20,16},{24,20},{28,24},{5,1},{9,5},{13... | collective-permute-start | bytes 4616 | tf_op jit(solution)/shard_map/ppermute | solution.py:169
  528.3 122.9 %collective-permute-start.38 = (bf16[2,2,1,256,768]{3,4,2,1,0:T(8,128)(2,1)}, bf16[2,2,1,256,768]{3,4,2,1,0:T(8,128)(2,1)}, u32[]{:S(2)}, u32[]{:S(2)}) collective-permute-start(bf16[2,2,1,256,768]{3,4,2,1,0:T(8,128)(2,1)} %copy.180), channel_id=1, source_target_pairs={{0,4},{4,0},{8,12},{12,8},{16,20},{20,16},{24,28},{28,24},{1,5},{5... | collective-permute-start | bytes 4718600 | tf_op jit(solution)/shard_map/ppermute | solution.py:24
  576.5 77.5 %collective-permute-start.41 = (bf16[2,2,1,256,768]{4,3,2,1,0:T(8,128)(2,1)}, bf16[2,2,1,256,768]{4,3,2,1,0:T(8,128)(2,1)}, u32[]{:S(2)}, u32[]{:S(2)}) collective-permute-start(bf16[2,2,1,256,768]{4,3,2,1,0:T(8,128)(2,1)} %copy.155), channel_id=1, source_target_pairs={{0,4},{4,0},{8,12},{12,8},{16,20},{20,16},{24,28},{28,24},{1,5},{5... | collective-permute-start | bytes 4718600 | tf_op jit(solution)/shard_map/ppermute | solution.py:24
  658.6 38.0 %collective-permute-start.57 = (bf16[2,1,1,2,2,24,2304]{6,5,4,3,2,1,0:T(8,128)(2,1)S(1)}, bf16[2,1,1,2,2,24,2304]{6,5,4,3,2,1,0:T(8,128)(2,1)S(1)}, u32[]{:S(2)}, u32[]{:S(2)}) collective-permute-start(bf16[2,1,1,2,2,24,2304]{6,5,4,3,2,1,0:T(8,128)(2,1)S(1)} %constant_dynamic-slice_fusion.22), channel_id=1, source_target_pairs={{0,8},{4,12},{8,0},{12,4},{16,24},{20,28},{24,16},{28,20},{1,9},{5... | collective-permute-start | bytes 2654216 | tf_op jit(solution)/shard_map/ppermute | solution.py:24
  663.6 117.9 %collective-permute-start.72 = (bf16[1,2,1,2,2,96,768]{6,5,4,3,2,1,0:T(8,128)(2,1)}, bf16[1,2,1,2,2,96,768]{6,5,4,3,2,1,0:T(8,128)(2,1)}, u32[]{:S(2)}, u32[]{:S(2)}) collective-permute-start(bf16[1,2,1,2,2,96,768]{6,5,4,3,2,1,0:T(8,128)(2,1)} %constant_dynamic-slice_fusion.7), channel_id=1, source_target_pairs={{0,16},{4,20},{8,24},{12,28},{16,0},{20,4},{24,8},{28,12},{1,17},{... | collective-permute-start | bytes 3538952 | tf_op jit(solution)/shard_map/ppermute | solution.py:24
  668.2 117.0 %collective-permute-start.67 = (bf16[2,1,1,2,2,24,3072]{6,5,4,3,2,1,0:T(8,128)(2,1)}, bf16[2,1,1,2,2,24,3072]{6,5,4,3,2,1,0:T(8,128)(2,1)}, u32[]{:S(2)}, u32[]{:S(2)}) collective-permute-start(bf16[2,1,1,2,2,24,3072]{6,5,4,3,2,1,0:T(8,128)(2,1)} %constant_dynamic-slice_fusion.12), channel_id=1, source_target_pairs={{0,8},{4,12},{8,0},{12,4},{16,24},{20,28},{24,16},{28,20},{1,9},{5... | collective-permute-start | bytes 3538952 | tf_op jit(solution)/shard_map/ppermute | solution.py:24
  674.4 113.2 %collective-permute-start.62 = (bf16[1,2,1,2,2,24,3072]{6,5,4,3,2,1,0:T(8,128)(2,1)}, bf16[1,2,1,2,2,24,3072]{6,5,4,3,2,1,0:T(8,128)(2,1)}, u32[]{:S(2)}, u32[]{:S(2)}) collective-permute-start(bf16[1,2,1,2,2,24,3072]{6,5,4,3,2,1,0:T(8,128)(2,1)} %constant_dynamic-slice_fusion.17), channel_id=1, source_target_pairs={{0,16},{4,20},{8,24},{12,28},{16,0},{20,4},{24,8},{28,12},{1,17},{... | collective-permute-start | bytes 3538952 | tf_op jit(solution)/shard_map/ppermute | solution.py:24
  677.7 58.2 %collective-permute-start.40 = (bf16[1,1,1,256,768]{3,4,2,1,0:T(8,128)(2,1)}, bf16[1,1,1,256,768]{3,4,2,1,0:T(8,128)(2,1)}, u32[]{:S(2)}, u32[]{:S(2)}) collective-permute-start(bf16[1,1,1,256,768]{3,4,2,1,0:T(8,128)(2,1)} %constant_dynamic-slice_fusion.40), channel_id=1, source_target_pairs={{0,8},{4,12},{8,0},{12,4},{16,24},{20,28},{24,16},{28,20},{1,9},{5... | collective-permute-start | bytes 1179656 | tf_op jit(solution)/shard_map/ppermute | solution.py:24
  696.6 36.2 %collective-permute-start.43 = (bf16[1,1,1,256,768]{4,3,2,1,0:T(8,128)(2,1)S(1)}, bf16[1,1,1,256,768]{4,3,2,1,0:T(8,128)(2,1)S(1)}, u32[]{:S(2)}, u32[]{:S(2)}) collective-permute-start(bf16[1,1,1,256,768]{4,3,2,1,0:T(8,128)(2,1)S(1)} %constant_dynamic-slice_fusion.36), channel_id=1, source_target_pairs={{0,16},{4,20},{8,24},{12,28},{16,0},{20,4},{24,8},{28,12},{1,17},{... | collective-permute-start | bytes 1179656 | tf_op jit(solution)/shard_map/ppermute | solution.py:24
  759.2 73.0 %collective-permute-start.51 = (bf16[2,2,1,2,2,24,2304]{6,5,4,3,2,1,0:T(8,128)(2,1)S(1)}, bf16[2,2,1,2,2,24,2304]{6,5,4,3,2,1,0:T(8,128)(2,1)S(1)}, u32[]{:S(2)}, u32[]{:S(2)}) collective-permute-start(bf16[2,2,1,2,2,24,2304]{6,5,4,3,2,1,0:T(8,128)(2,1)S(1)} %constant_dynamic-slice_fusion.28), channel_id=1, source_target_pairs={{0,4},{4,0},{8,12},{12,8},{16,20},{20,16},{24,28},{28,24},{1,5},{5... | collective-permute-start | bytes 5308424 | tf_op jit(solution)/shard_map/ppermute | solution.py:24
  801.5 30.6 %collective-permute-start.69 = (bf16[1,1,1,1,2,24,3072]{6,5,4,3,2,1,0:T(8,128)(2,1)S(1)}, bf16[1,1,1,1,2,24,3072]{6,5,4,3,2,1,0:T(8,128)(2,1)S(1)}, u32[]{:S(2)}, u32[]{:S(2)}) collective-permute-start(bf16[1,1,1,1,2,24,3072]{6,5,4,3,2,1,0:T(8,128)(2,1)S(1)} %constant_dynamic-slice_fusion.10), channel_id=1, source_target_pairs={{0,2},{1,3},{2,0},{3,1},{4,6},{5,7},{6,4},{7,5},{8,10},{9,11},{10,... | collective-permute-start | bytes 884744 | tf_op jit(solution)/shard_map/ppermute | solution.py:24
  825.8 48.4 %collective-permute-start.75 = (bf16[1,1,1,1,1,96,768]{6,5,4,3,2,1,0:T(8,128)(2,1)S(1)}, bf16[1,1,1,1,1,96,768]{6,5,4,3,2,1,0:T(8,128)(2,1)S(1)}, u32[]{:S(2)}, u32[]{:S(2)}) collective-permute-start(bf16[1,1,1,1,1,96,768]{6,5,4,3,2,1,0:T(8,128)(2,1)S(1)} %constant_dynamic-slice_fusion.4), channel_id=1, source_target_pairs={{0,1},{1,0},{2,3},{3,2},{4,5},{5,4},{6,7},{7,6},{8,9},{9,8},{10,11... | collective-permute-start | bytes 442376 | tf_op jit(solution)/shard_map/ppermute | solution.py:24
  (189 other events, 3090.8 us)

commit v2 on v1

--- a/solution.py
+++ b/solution.py
@@ -19,52 +19,359 @@
     return [1 << k for k in range(lax.axis_size(axis).bit_length() - 1)]
 
 
-def swapped(value, axis, mask):
-    count = lax.axis_size(axis)
-    return lax.ppermute(value, axis, [(i, i ^ mask) for i in range(count)])
-
-
-def bit_set(axis, mask):
-    return (lax.axis_index(axis) & mask) != 0
-
-
-def hop_order(axes, upward):
-    places, dim = {}, 0
-    for axis in axes:
-        for mask in reversed(masks_of(axis)):
-            places[axis, mask] = dim
-            dim = dim + 1
-    middle = [("ctx", mask) for mask in masks_of("ctx")[1:]]
-    hops = [("wsh", mask) for mask in masks_of("wsh")] if "wsh" in axes else []
-    hops = hops + (middle if upward else middle[::-1]) + [("ctx", 1)]
-    return [(axis, mask, places[axis, mask]) for axis, mask in hops], dim
-
-
-def gathered(shard, axes, upward):
-    hops, dims = hop_order(axes, upward)
-    block = shard.reshape((1,) * dims + shard.shape)
-    for axis, mask, dim in hops:
-        other = swapped(block, axis, mask)
-        high = bit_set(axis, mask)
-        block = jnp.concatenate(
-            [jnp.where(high, other, block), jnp.where(high, block, other)], axis=dim
+def place_of(axis, partner):
+    here = {"ctx": lax.axis_index("ctx"), "wsh": lax.axis_index("wsh")}
+    here[axis] = partner
+    return (here["ctx"], here["wsh"])
+
+
+def greet(over_wsh):
+    barrier = pltpu.get_barrier_semaphore()
+    partners = [
+        place_of("ctx", lax.bitwise_xor(lax.axis_index("ctx"), mask)) for mask in masks_of("ctx")
+    ]
+    if over_wsh:
+        partners = partners + [
+            place_of("wsh", lax.bitwise_xor(lax.axis_index("wsh"), gap))
+            for gap in range(1, lax.axis_size("wsh"))
+        ]
+    for partner in partners:
+        pl.semaphore_signal(
+            barrier, inc=1, device_id=partner, device_id_type=pl.DeviceIdType.MESH
         )
-    return block.reshape((-1,) + shard.shape[1:])
-
-
-def scattered(value, axes, upward, last):
-    hops, dims = hop_order(axes, upward)
-    rows = value.shape[0] >> dims
-    block = value.reshape((2,) * dims + (rows,) + value.shape[1:])
-    for axis, mask, dim in hops[::-1]:
-        high = bit_set(axis, mask).astype(jnp.int32)
-        away = lax.dynamic_index_in_dim(block, 1 - high, dim, keepdims=True)
-        kept = lax.dynamic_index_in_dim(block, high, dim, keepdims=True)
-        other = swapped(away, axis, mask)
-        block = kept.astype(jnp.float32) + other.astype(jnp.float32)
-        if (axis, mask, dim) != hops[0]:
-            block = block.astype(jnp.bfloat16)
-    return block.reshape((rows,) + value.shape[1:]).astype(last)
+    pl.semaphore_wait(barrier, len(partners))
+
+
+def ctx_bits(upward):
+    masks = masks_of("ctx")
+    middle = masks[1:]
+    return (middle if upward else middle[::-1]) + masks[:1]
+
+
+def ctx_bit(mask):
+    return lax.rem(lax.div(lax.axis_index("ctx"), mask), 2)
+
+
+def ctx_index(fixed):
+    return tuple(
+        fixed[mask] if mask in fixed else slice(None) for mask in reversed(masks_of("ctx"))
+    )
+
+
+def remote(src, dst, sems, number, partner):
+    return pltpu.make_async_remote_copy(
+        src_ref=src,
+        dst_ref=dst,
+        send_sem=sems[0].at[number],
+        recv_sem=sems[1].at[number],
+        device_id=partner,
+        device_id_type=pl.DeviceIdType.MESH,
+    )
+
+
+def gather_kernel(slots, count, over_wsh, *refs):
+    shards, outs = refs[:count], refs[count : 2 * count]
+    sems, local_sems = refs[2 * count : 2 * count + 2], refs[2 * count + 2]
+    width_w = lax.axis_size("wsh") if over_wsh else 1
+    mine_w = lax.axis_index("wsh") if over_wsh else 0
+    bits = len(masks_of("ctx"))
+    per_stream = width_w - 1 + bits
+    greet(over_wsh)
+    streams = [stream for slot in slots for stream in slot]
+    number_of = {stream: position for position, stream in enumerate(streams)}
+    started = {}
+
+    def start(stream, step):
+        array, first, cols, upward = stream
+        base = number_of[stream] * per_stream
+        span = pl.ds(first, cols)
+        out = outs[array]
+        every = {mask: ctx_bit(mask) for mask in masks_of("ctx")}
+        copies = []
+        if step == 0:
+            own = ctx_index(every) + (mine_w, slice(None), span)
+            copy = pltpu.make_async_copy(
+                shards[array].at[:, span], out.at[own], local_sems.at[number_of[stream]]
+            )
+            copies.append(copy)
+            for gap in range(1, width_w):
+                copies.append(
+                    remote(
+                        shards[array].at[:, span],
+                        out.at[own],
+                        sems,
+                        base + gap - 1,
+                        place_of("wsh", lax.bitwise_xor(mine_w, gap)),
+                    )
+                )
+        else:
+            order = ctx_bits(upward)
+            held = {mask: every[mask] for mask in order[step - 1 :]}
+            part = ctx_index(held) + (slice(None), slice(None), span)
+            partner = place_of("ctx", lax.bitwise_xor(lax.axis_index("ctx"), order[step - 1]))
+            copies.append(
+                remote(out.at[part], out.at[part], sems, base + width_w - 1 + step - 1, partner)
+            )
+        for copy in copies:
+            copy.start()
+        started[stream, step] = copies
+
+    def finish(stream, step):
+        for position, copy in enumerate(started[stream, step]):
+            if step == 0 and position == 0:
+                copy.wait()
+            else:
+                copy.wait_recv()
+
+    for tick in range(len(slots) + bits + 1):
+        for number, slot in reversed(list(enumerate(slots))):
+            step = tick - number
+            for stream in slot:
+                if 1 <= step <= bits + 1:
+                    finish(stream, step - 1)
+                if 0 <= step <= bits:
+                    start(stream, step)
+    for (stream, step), copies in started.items():
+        for copy in copies[1:] if step == 0 else copies:
+            copy.wait_send()
+
+
+def gather_all(arrays, slots, over_wsh, collective):
+    bits = len(masks_of("ctx"))
+    width_w = lax.axis_size("wsh") if over_wsh else 1
+    count = len(arrays)
+    streams = sum(len(slot) for slot in slots)
+    copies = streams * (width_w - 1 + bits)
+    hbm = pl.BlockSpec(memory_space=pl.ANY)
+    outs = pl.pallas_call(
+        functools.partial(gather_kernel, slots, count, over_wsh),
+        out_shape=tuple(
+            jax.ShapeDtypeStruct((2,) * bits + (width_w,) + array.shape, array.dtype)
+            for array in arrays
+        ),
+        in_specs=[hbm] * count,
+        out_specs=(hbm,) * count,
+        scratch_shapes=[
+            pltpu.SemaphoreType.DMA((copies,)),
+            pltpu.SemaphoreType.DMA((copies,)),
+            pltpu.SemaphoreType.DMA((streams,)),
+        ],
+        compiler_params=pltpu.CompilerParams(
+            collective_id=collective, has_side_effects=True, vmem_limit_bytes=4 << 20
+        ),
+        name="gather_all",
+    )(*arrays)
+    return [out.reshape((-1, out.shape[-1])) for out in outs]
+
+
+def add_into(total_ref, extra_ref, fixed_total, fixed_extra, shape, rows, block_rows, span):
+    steps = math.prod(shape) * (rows // block_rows)
+
+    def step(position, carry):
+        rest = position
+        chunk = lax.rem(rest, rows // block_rows)
+        rest = lax.div(rest, rows // block_rows)
+        free = []
+        for size in reversed(shape):
+            free.append(lax.rem(rest, size))
+            rest = lax.div(rest, size)
+        free = free[::-1]
+        take = iter(free)
+        into = tuple(next(take) if entry is None else entry for entry in fixed_total)
+        take = iter(free)
+        source = tuple(next(take) if entry is None else entry for entry in fixed_extra)
+        down = pl.ds(pl.multiple_of(chunk * block_rows, block_rows), block_rows)
+        total_ref[into + (down, span)] = (
+            total_ref[into + (down, span)] + extra_ref[source + (down, slice(None))]
+        )
+        return carry
+
+    lax.fori_loop(0, steps, step, 0)
+
+
+def scatter_kernel(slots, count, over_wsh, *refs):
+    streams = [stream for slot in slots for stream in slot]
+    grads, outs = refs[:count], refs[count : 2 * count]
+    bits = len(masks_of("ctx"))
+    held = refs[2 * count : 3 * count]
+    rest = refs[3 * count :]
+    per_stream_bufs = bits + (1 if over_wsh else 0)
+    landing = {}
+    for number, stream in enumerate(streams):
+        landing[stream] = rest[number * per_stream_bufs : (number + 1) * per_stream_bufs]
+    sems = rest[len(streams) * per_stream_bufs : len(streams) * per_stream_bufs + 2]
+    local_sems = rest[len(streams) * per_stream_bufs + 2]
+    width_w = lax.axis_size("wsh") if over_wsh else 1
+    mine_w = lax.axis_index("wsh") if over_wsh else 0
+    per_stream = width_w - 1 + bits
+    number_of = {stream: position for position, stream in enumerate(streams)}
+    every = {mask: ctx_bit(mask) for mask in masks_of("ctx")}
+    low = masks_of("ctx")[0]
+    started = {}
+    greet(over_wsh)
+
+    def start(stream, step):
+        array, first, cols, upward = stream
+        base = number_of[stream] * per_stream
+        span = pl.ds(first, cols)
+        order = ctx_bits(upward)[::-1]
+        copies = []
+        if step == 0:
+            kept = ctx_index({low: every[low]}) + (slice(None), slice(None), span)
+            copies.append(
+                pltpu.make_async_copy(
+                    grads[array].at[kept],
+                    held[array].at[(slice(None),) * bits + (slice(None), span)],
+                    local_sems.at[number_of[stream]],
+                )
+            )
+            away = ctx_index({low: 1 - every[low]}) + (slice(None), slice(None), span)
+            copies.append(
+                remote(
+                    grads[array].at[away],
+                    landing[stream][0],
+                    sems,
+                    base,
+                    place_of("ctx", lax.bitwise_xor(lax.axis_index("ctx"), low)),
+                )
+            )
+        elif step < bits:
+            fixed = {mask: every[mask] for mask in order[:step]}
+            fixed[order[step]] = 1 - every[order[step]]
+            away = ctx_index(fixed)[:-1] + (slice(None), slice(None), span)
+            copies.append(
+                remote(
+                    held[array].at[away],
+                    landing[stream][step],
+                    sems,
+                    base + step,
+                    place_of("ctx", lax.bitwise_xor(lax.axis_index("ctx"), order[step])),
+                )
+            )
+        elif over_wsh:
+            here = ctx_index(every)[:-1]
+            for gap in range(1, width_w):
+                other = lax.bitwise_xor(mine_w, gap)
+                copies.append(
+                    remote(
+                        held[array].at[here + (other, slice(None), span)],
+                        landing[stream][bits].at[gap - 1],
+                        sems,
+                        base + bits + gap - 1,
+                        place_of("wsh", other),
+                    )
+                )
+        for copy in copies:
+            copy.start()
+        started[stream, step] = copies
+
+    def finish(stream, step):
+        array, first, cols, upward = stream
+        span = pl.ds(first, cols)
+        order = ctx_bits(upward)[::-1]
+        for position, copy in enumerate(started[stream, step]):
+            if step == 0 and position == 0:
+                copy.wait()
+            else:
+                copy.wait_recv()
+        rows = held[array].shape[-2]
+        block_rows = rows if rows <= 24 else 32
+        if step < bits:
+            fixed = {mask: every[mask] for mask in order[: step + 1]}
+            lead = ctx_index(fixed)[:-1]
+            into = tuple(None if isinstance(entry, slice) else entry for entry in lead) + (None,)
+            free = (2,) * (bits - 1 - step)
+            add_into(
+                held[array],
+                landing[stream][step],
+                into,
+                (None,) * (len(free) + 1),
+                free + (width_w,),
+                rows,
+                block_rows,
+                span,
+            )
+        if step == bits or (step == bits - 1 and not over_wsh):
+            here = ctx_index(every)[:-1] + (mine_w,)
+            for chunk in range(0, rows, block_rows):
+                down = pl.ds(chunk, block_rows)
+                total = held[array][here + (down, span)].astype(jnp.float32)
+                for gap in range(1, width_w):
+                    total = total + landing[stream][bits][gap - 1, down, :].astype(jnp.float32)
+                outs[array][down, span] = total.astype(outs[array].dtype)
+
+    steps = bits + (1 if over_wsh else 0)
+    for tick in range(len(slots) + steps):
+        for number, slot in reversed(list(enumerate(slots))):
+            step = tick - number
+            for stream in slot:
+                if 1 <= step <= steps:
+                    finish(stream, step - 1)
+                if 0 <= step < steps:
+                    start(stream, step)
+    for (stream, step), copies in started.items():
+        for copy in copies[1:] if step == 0 else copies:
+            copy.wait_send()
+
+
+def scatter_sums(arrays, slots, over_wsh, collective, dtype):
+    bits = len(masks_of("ctx"))
+    width_w = lax.axis_size("wsh") if over_wsh else 1
+    count = len(arrays)
+    parts = width_w << bits
+    rows = [array.shape[0] // parts for array in arrays]
+    shaped = [
+        array.reshape((2,) * bits + (width_w, row, array.shape[1]))
+        for array, row in zip(arrays, rows)
+    ]
+    streams = [stream for slot in slots for stream in slot]
+    copies = len(streams) * (width_w - 1 + bits)
+    buffers = [
+        pltpu.VMEM((2,) * (bits - 1) + (width_w, row, array.shape[1]), array.dtype)
+        for array, row in zip(arrays, rows)
+    ]
+    for array, first, cols, upward in streams:
+        kind = arrays[array].dtype
+        for step in range(bits):
+            buffers.append(
+                pltpu.VMEM((2,) * (bits - 1 - step) + (width_w, rows[array], cols), kind)
+            )
+        if over_wsh:
+            buffers.append(pltpu.VMEM((width_w - 1, rows[array], cols), kind))
+    return pl.pallas_call(
+        functools.partial(scatter_kernel, slots, count, over_wsh),
+        out_shape=tuple(
+            jax.ShapeDtypeStruct((row, array.shape[1]), dtype) for array, row in zip(arrays, rows)
+        ),
+        in_specs=[pl.BlockSpec(memory_space=pl.ANY)] * count,
+        out_specs=(pl.BlockSpec(memory_space=pltpu.VMEM),) * count,
+        scratch_shapes=buffers
+        + [
+            pltpu.SemaphoreType.DMA((copies,)),
+            pltpu.SemaphoreType.DMA((copies,)),
+            pltpu.SemaphoreType.DMA((len(streams),)),
+        ],
+        compiler_params=pltpu.CompilerParams(
+            collective_id=collective, has_side_effects=True, vmem_limit_bytes=56 << 20
+        ),
+        name="scatter_sums",
+    )(*shaped)
+
+
+def halves(number, cols):
+    pieces = 2 if cols < 2304 else 4
+    cuts = [cols * piece // pieces // 128 * 128 for piece in range(pieces)] + [cols]
+    streams = [
+        (number, cuts[piece], cuts[piece + 1] - cuts[piece], piece % 2 == 0)
+        for piece in range(pieces)
+    ]
+    return [tuple(streams[piece : piece + 2]) for piece in range(0, pieces, 2)]
+
+
+def slots_of(arrays):
+    return [
+        slot for number, part in enumerate(arrays) for slot in halves(number, part.shape[1])
+    ]
 
 
 def scan_kernel(forward_first, a_ref, b_ref, local_ref, cum_ref, total_ref, coef_s, term_s):
@@ -233,17 +540,23 @@
     lane = 128
     gain_block = jnp.stack([gain_attn, gain_char, gain_merge], axis=1)
     gain_block = jnp.pad(gain_block, ((0, 0), (0, lane - 3)))
-    gains_and_qkv = gathered(jnp.concatenate([qkv_weight, gain_block], axis=1), every, True)
+    first_needed = [gru_weight, jnp.concatenate([qkv_weight, gain_block], axis=1)]
+    gru_full, gains_and_qkv = gather_all(
+        first_needed,
+        slots_of(first_needed),
+        True,
+        0,
+    )
     qkv_full = gains_and_qkv[:, : 3 * width]
     gains = jnp.transpose(gains_and_qkv[:, 3 * width :].astype(f32))
     attn_gain_f, char_gain_f, merge_gain_f = gains[0], gains[1], gains[2]
-    gru_full = gathered(gru_weight, every, False)
-    out_merge = gathered(jnp.concatenate([out_weight, merge_weight], axis=1), every, False)
-    out_full = out_merge[:, :width]
-    merge_full = out_merge[:, width:]
-    conv_full = gathered(conv_weight, every, True)
-    up_full = gathered(up_weight, every, False)
-    down_full = gathered(down_weight, every, True)
+    later = [conv_weight, out_weight, merge_weight, up_weight, down_weight]
+    conv_full, out_full, merge_full, up_full, down_full = gather_all(
+        later,
+        slots_of(later),
+        True,
+        1,
+    )
     tok_rows = tokens.shape[1]
     char_rows = chars.shape[1]
     half_width = width // 2
@@ -276,8 +589,9 @@
     queries = qkv[:, :width]
     keys = qkv[:, width : 2 * width]
     values = qkv[:, 2 * width :]
-    keys_all = gathered(keys, ("ctx",), True)
-    values_all = gathered(values, ("ctx",), False)
+    keys_all, values_all = gather_all(
+        [keys, values], [((0, 0, width, True), (1, 0, width, False))], False, 2
+    )
     query_heads = queries.reshape(tok_rows, HEADS, HEAD_DIM)
     key_blocks = keys_all.reshape(key_count, key_block, HEADS, HEAD_DIM)
     value_blocks = values_all.reshape(key_count, key_block, HEADS, HEAD_DIM)
@@ -481,8 +795,13 @@
         jnp.zeros((tok_rows, HEADS, HEAD_DIM), f32),
         (key_blocks, value_blocks, key_docs),
     )
-    dk_local = scattered(key_terms[0].reshape(seq_len, width).astype(bf16), ("ctx",), True, bf16)
-    dv_local = scattered(key_terms[1].reshape(seq_len, width).astype(bf16), ("ctx",), False, bf16)
+    dk_local, dv_local = scatter_sums(
+        [term.reshape(seq_len, width).astype(bf16) for term in key_terms],
+        [((0, 0, width, True), (1, 0, width, False))],
+        False,
+        3,
+        bf16,
+    )
     grad_qkv_low = jnp.concatenate(
         [
             dq_heads.reshape(tok_rows, width).astype(bf16),
@@ -498,23 +817,34 @@
     grad_tokens_out = (grad_stream + grad_token_in).astype(bf16)
     gain_grads = jnp.stack([grad_attn_gain, grad_char_gain, grad_merge_gain], axis=1)
     gain_grads = jnp.pad(gain_grads, ((0, 0), (0, lane - 3)))
-    down_shard = scattered(grad_down.astype(bf16), every, True, f32)
-    up_shard = scattered(grad_up.astype(bf16), every, False, f32)
-    merge_conv = jnp.concatenate([grad_merge.astype(bf16), grad_conv.astype(bf16)], axis=1)
-    merge_conv = scattered(merge_conv, every, True, f32)
-    gru_out = jnp.concatenate([grad_gru.astype(bf16), grad_out_proj.astype(bf16)], axis=1)
-    gru_out = scattered(gru_out, every, False, f32)
-    qkv_shard = scattered(grad_qkv.astype(bf16), every, True, f32)
-    gain_shard = scattered(gain_grads.astype(bf16), every, False, f32)
+    early = [grad_down, grad_up, grad_merge, grad_conv]
+    early = [part.astype(bf16) for part in early]
+    down_shard, up_shard, merge_shard, conv_shard = scatter_sums(
+        early,
+        slots_of(early),
+        True,
+        4,
+        f32,
+    )
+    late = [grad_gru, grad_out_proj, jnp.concatenate([grad_qkv, gain_grads], axis=1)]
+    late = [part.astype(bf16) for part in late]
+    gru_shard, out_shard, qkv_shard = scatter_sums(
+        late,
+        slots_of(late),
+        True,
+        5,
+        f32,
+    )
+    gain_shard = qkv_shard[:, 3 * width :]
     shards = (
         gain_shard[:, 0],
-        qkv_shard,
-        gru_out[:, 2 * width :],
+        qkv_shard[:, : 3 * width],
+        out_shard,
         gain_shard[:, 1],
-        gru_out[:, : 2 * width],
-        merge_conv[:, width:],
+        gru_shard,
+        conv_shard,
         gain_shard[:, 2],
-        merge_conv[:, :width],
+        merge_shard,
         up_shard,
         down_shard,
     )

time: 892 us -> 758 us (0.85)
  Pallas kernels: 27.3 us -> 395 us
  waiting for transfers between devices: 278 us -> 1.18 us
  starting transfers between devices: 87.3 us -> 8.43 us
  other arithmetic: 108 us -> 47.2 us
  local copies, waits for them, and re-layouts: 177 us -> 130 us
  blocking collectives: 85.8 us -> 58.1 us
    pallas_call x0 -> x6, Pallas kernels: none -> 368 us  [the longest x3 206 us: scatter_sums(): pl.pallas_call(functools.partial(scatter_kernel, slots, count, over_wsh),...]
    ppermute x72 -> x0, waiting for transfers between devices: 278 us -> none  [swapped(): return lax.ppermute(value, axis, [(i, i ^ mask) for i in range(count)])]
    ppermute x72 -> x0, starting transfers between devices: 78.3 us -> none  [swapped(): return lax.ppermute(value, axis, [(i, i ^ mask) for i in range(count)])]
    dynamic_slice x37 -> x0, local copies, waits for them, and re-layouts: 44.9 us -> none  [the longest x2 23.5 us: scattered(): kept = lax.dynamic_index_in_dim(block, high, dim, keepdims=True)]
    concatenate x3 -> x0, local copies, waits for them, and re-layouts: 23.9 us -> none  [the longest x2 17.2 us: gathered(): jnp.concatenate([jnp.where(high, other, block), jnp.where(high, block, ot...]
    convert_element_type x30 -> x1, other arithmetic: 20.7 us -> 0.33 us  [body(): grad_pre = gelu_merge_back(grad_merged)[0].astype(bf16)]
    concatenate x38 -> x3, other arithmetic: 25.1 us -> 7.21 us  [the longest x1 4.11 us: body(): jnp.concatenate([grad_qkv, gain_grads], axis=1)]
    convert_element_type x3 -> x5, local copies, waits for them, and re-layouts: 13.5 us -> 29.4 us  [the longest x4 28.4 us: body(): term.reshape(seq_len, width).astype(bf16)]
  transfers between devices with their start and end apart: 76 -> 4, of which waited for: 36 -> 1; matrix products, arithmetic and copies ran while one was open for 27% -> 9% of each run, Pallas kernels for 3% -> 31%
where the time goes in v2:
time: 758 us; the launch traced here: 750 us
  Pallas kernels  395 us (52%)
  local copies, waits for them, and re-layouts  130 us (17%)
  matrix products  80.5 us (11%)
  blocking collectives  58.1 us (8%)
  other arithmetic  47.2 us (6%)
  loops' own time  21.2 us (3%)
  starting transfers between devices  8.43 us (1%)
  between operations  8.06 us (1%)
    pallas_call x3, Pallas kernels, scatter_sums(): pl.pallas_call(functools.partial(scatter_kernel, slots, count, over_wsh),...  206 us
    pallas_call x3, Pallas kernels, gather_all(): pl.pallas_call(functools.partial(gather_kernel, slots, count, over_wsh),...  162 us
    convert_element_type x4, local copies, waits for them, and re-layouts, body(): term.reshape(seq_len, width).astype(bf16)  28.4 us
    pallas_call x2, Pallas kernels, scan_both(): pl.pallas_call(functools.partial(scan_kernel, forward_first), out_shape=(...  27.3 us
    unnamed x257, local copies, waits for them, and re-layouts  27 us
    all_gather x2, blocking collectives, carried(): pieces = lax.all_gather(totals[:2], 'ctx')  24.3 us
    psum x1, blocking collectives, body(): lax.psum((jnp.sum(proj * proj), jnp.sum(token_in * proj), jnp.sum(token_i...  21.2 us
  transfers between devices with their start and end apart: 4, of which 1 were waited for; matrix products, arithmetic and copies ran while one was open for 9% of the time, Pallas kernels for 31%

profile of v2, /device:TPU:0, one launch (start us, length us, event | category | flops | bytes accessed | tf_op | source)
XLA Modules:
  0.0 749.5 jit_solution(12310846628140226485)
XLA Ops:
  5.7 42.5 %gather_all.3 = (bf16[2,2,2,4,24,1536]{5,4,3,2,1,0:T(8,128)(2,1)S(1)}, bf16[2,2,2,4,24,2432]{5,4,3,2,1,0:T(8,128)(2,1)S(1)}) custom-call(bf16[24,1536]{1,0:T(8,128)(2,1)S(1)} %copy-done.13, bf16[24,2432]{1,0:T(8,128)(2,1)S(1)} %fusion.156.refs_1_), custom_call_target="tpu_custom_call" | custom-call | tf_op jit(solution)/shard_map/gather_all/pallas_call | solution.py:146
  61.1 13.6 %scan_both.2 = (f32[1024,768]{1,0:T(8,128)S(1)}, f32[1024,768]{1,0:T(8,128)S(1)}, f32[8,768]{1,0:T(8,128)S(1)}) custom-call(f32[1024,768]{1,0:T(8,128)S(1)} %pad_maximum_fusion.2.a_ref, f32[1024,768]{1,0:T(8,128)S(1)} %pad_maximum_fusion.3.b_ref), custom_call_target="tpu_custom_call" | custom-call | flops 6291456 | bytes 12582912 | tf_op jit(solution)/shard_map/scan_both/pallas_call | solution.py:432
  76.5 9.6 %all-gather.2 = f32[8,2,768]{2,1,0:T(2,128)S(1)} all-gather(f32[1,2,768]{2,1,0:T(2,128)S(1)} %slice_bitcast_fusion), channel_id=2, replica_groups=mesh['ctx'=8,'wsh'=4] {'ctx'}, dimensions={0}, use_global_device_ids=true | all-gather | bytes 55296 | tf_op jit(solution)/shard_map/all_gather | solution.py:448
  86.8 4.1 fusion.73
  95.1 3.8 collective-permute-start
  105.3 84.3 %gather_all.5 = (bf16[2,2,2,4,24,2304]{5,4,3,2,1,0:T(8,128)(2,1)S(1)}, bf16[2,2,2,4,24,768]{5,4,3,2,1,0:T(8,128)(2,1)S(1)}, bf16[2,2,2,4,24,768]{5,4,3,2,1,0:T(8...) custom-call(bf16[24,2304]{1,0:T(8,128)(2,1)S(1)} %copy-done.12, ...), custom_call_target="tpu_custom_call" | custom-call | tf_op jit(solution)/shard_map/gather_all/pallas_call | solution.py:146
  200.7 35.4 %gather_all.4 = (bf16[2,2,2,1,256,768]{5,4,3,2,1,0:T(8,128)(2,1)S(1)}, bf16[2,2,2,1,256,768]{5,4,3,2,1,0:T(8,128)(2,1)S(1)}) custom-call(bf16[256,768]{1,0:T(8,128)(2,1)S(1)} %get-tuple-element.478.refs_0_, bf16[256,768]{1,0:T(8,128)(2,1)S(1)} %get-tuple-element.477.refs_1_), custom_call_target="tpu_custom_call" | custom-call | tf_op jit(solution)/shard_map/gather_all/pallas_call | solution.py:146
  237.9 8.6 %copy.95 = bf16[2,2,2,1,256,768]{4,2,5,1,0,3:T(2,128)(2,1)} copy(bf16[2,2,2,1,256,768]{5,4,3,2,1,0:T(8,128)(2,1)} %copy-done) | data formatting | bytes 6291456 | tf_op jit(solution)/shard_map/gather_all/pallas_call | solution.py:146
  246.5 6.0 reshape_reshape.6
  252.5 5.5 copy.97
  258.1 6.1 reshape_reshape.7
  264.5 22.3 %while.31 = (s32[]{:T(128)}, f32[12,256]{1,0:T(8,128)S(1)}, f32[12,256]{1,0:T(8,128)S(1)}, f32[12,256,64]{1,2,0:T(8,128)S(1)}, s32[256]{0:T(256)S(1)}, /*index=5...) while((s32[]{:T(128)}, f32[12,256]{1,0:T(8,128)S(1)}, ...), condition=%wide.region_10.11_spmd, body=%wide.region_5.10_spmd.sunk | while | flops 423630848 | bytes 23142728 | solution.py:629
  268.3 7.0 conditional.4
  289.5 21.2 %all-reduce.5 = (f32[]{:T(128)}, f32[]{:T(128)}, f32[]{:T(128)}) all-reduce(f32[]{:T(128)} %get-tuple-element.383, f32[]{:T(128)} %get-tuple-element.387, f32[]{:T(128)} %get-tuple-element.382), channel_id=1, replica_groups=mesh['ctx'=8,'wsh'=4] {'ctx'}, use_global_device_ids=true, to_apply=%region_12.13 | all-reduce | flops 3 | bytes 24 | tf_op jit(solution)/shard_map/psum | solution.py:636
  324.0 4.0 multiply_convert_fusion.3
  328.1 9.1 %multiply_convert_fusion = (bf16[256,3072]{1,0:T(8,128)(2,1)S(1)}, f32[256,3072]{1,0:T(8,128)S(1)}, f32[256,3072]{1,0:T(8,128)S(1)}) fusion(bf16[256,768]{1,0:T(8,128)(2,1)S(1)} %get-tuple-element.450, bf16[768,3072]{1,0:T(8,128)(2,1)S(1)} %bitcast.761), kind=kOutput, calls=%fused_computation.96 | convolution fusion | flops 1259077632 | bytes 12976128 | tf_op jit(solution)/shard_map/dot_general | solution.py:681
  359.5 12.6 %all-reduce.4 = (f32[]{:T(128)}, f32[]{:T(128)}) all-reduce(f32[]{:T(128)} %get-tuple-element.381, f32[]{:T(128)} %get-tuple-element.380), channel_id=1, replica_groups=mesh['ctx'=8,'wsh'=4] {'ctx'}, use_global_device_ids=true, to_apply=%region_31.32 | all-reduce | flops 2 | bytes 16 | tf_op jit(solution)/shard_map/psum | solution.py:745
  382.5 39.5 %while.32 = (s32[]{:T(128)}, f32[256,12,64]{0,2,1:T(8,128)}, bf16[4,512,12,64]{1,3,2,0:T(8,128)(2,1)}, bf16[4,512,12,64]{1,3,2,0:T(8,128)(2,1)}, s32[256]{0:T(25...) while((s32[]{:T(128)}, f32[256,12,64]{0,2,1:T(8,128)}, ...), condition=%wide.region_35.36_spmd, body=%wide.region_32.35_spmd.sunk | while | flops 1023672320 | bytes 46941680 | solution.py:793
  388.4 10.0 %conditional.5 = (f32[256,12,64]{0,2,1:T(8,128)}, bf16[1,512,12,64]{1,3,2,0:T(8,128)(2,1)S(1)}, bf16[1,512,12,64]{1,3,2,0:T(8,128)(2,1)S(1)}) conditional(s32[]{:T(128)} %convert_element_type.395, f32[256,12,64]{0,2,1:T(8,128)} %get-tuple-element.723, (s32[256]{0:T(256)}, s32[1,512]{1,0:T(1,128)S(1)}, bf16[4,512,12,64]{1,3,2,0:T(8,128)(2,1)}, ...), branch_computations={%region_33.33_spmd, %region_34.34_spmd} | conditional | flops 1023672320 | bytes 43791040 | solution.py:791
  422.0 5.5 convert_element_type.219
  427.5 8.7 %copy.100.refs_0_ = bf16[2,2,2,1,256,768]{5,4,3,2,1,0:T(8,128)(2,1)} copy(bf16[2,2,2,1,256,768]{4,2,5,1,0,3:T(2,128)(2,1)} %convert_element_type.219) | data formatting | bytes 6291456 | tf_op jit(solution)/shard_map/convert_element_type | solution.py:799
  436.2 5.5 convert_element_type.221
  441.7 8.7 %copy.101.refs_1_ = bf16[2,2,2,1,256,768]{5,4,3,2,1,0:T(8,128)(2,1)} copy(bf16[2,2,2,1,256,768]{4,2,5,1,0,3:T(2,128)(2,1)} %convert_element_type.221) | data formatting | bytes 6291456 | tf_op jit(solution)/shard_map/convert_element_type | solution.py:799
  452.6 47.1 %scatter_sums.3 = (bf16[256,768]{1,0:T(8,128)(2,1)}, bf16[256,768]{1,0:T(8,128)(2,1)}) custom-call(bf16[2,2,2,1,256,768]{5,4,3,2,1,0:T(8,128)(2,1)} %copy.100.refs_0_, bf16[2,2,2,1,256,768]{5,4,3,2,1,0:T(8,128)(2,1)} %copy.101.refs_1_), custom_call_target="tpu_custom_call" | custom-call | tf_op jit(solution)/shard_map/scatter_sums/pallas_call | solution.py:341
  506.2 4.3 convolution_convert_fusion.2
  518.7 110.8 %scatter_sums.5 = (f32[96,768]{1,0:T(8,128)}, f32[24,3072]{1,0:T(8,128)}, f32[24,768]{1,0:T(8,128)}, f32[24,2304]{1,0:T(8,128)}) custom-call(bf16[2,2,2,4,96,768]{5,4,3,2,1,0:T(8,128)(2,1)} %bitcast.766, bf16[2,2,2,4,24,3072]{5,4,3,2,1,0:T(8,128)(2,1)} %bitcast.767, bf16[2,2,2,4,24,768]{5,4,3,2,1,0:T(8,128)(2,1)} %bitcast.771, ...), custom_call_target="tpu_custom_call" | custom-call | tf_op jit(solution)/shard_map/scatter_sums/pallas_call | solution.py:341
  634.1 7.0 gather_fusion
  643.9 13.6 %scan_both.3 = (f32[1024,768]{1,0:T(8,128)S(1)}, f32[1024,768]{1,0:T(8,128)S(1)}, f32[8,768]{1,0:T(8,128)S(1)}) custom-call(f32[1024,768]{1,0:T(8,128)S(1)} %select_maximum_fusion.a_ref, f32[1024,768]{1,0:T(8,128)S(1)} %convert_add_fusion.1.b_ref), custom_call_target="tpu_custom_call" | custom-call | flops 6291456 | bytes 12582912 | tf_op jit(solution)/shard_map/scan_both/pallas_call | solution.py:432
  657.6 14.7 %all-gather.3 = f32[8,2,768]{2,1,0:T(2,128)S(1)} all-gather(f32[1,2,768]{2,1,0:T(2,128)S(1)} %multiply_bitcast_fusion.1), channel_id=3, replica_groups=mesh['ctx'=8,'wsh'=4] {'ctx'}, dimensions={0}, use_global_device_ids=true | all-gather | bytes 55296 | tf_op jit(solution)/shard_map/all_gather | solution.py:448
  681.5 4.4 convolution_convert_fusion.4
  687.9 4.1 pad_maximum_fusion.refs_2_
  692.0 47.7 %scatter_sums.4 = (f32[24,1536]{1,0:T(8,128)}, f32[24,768]{1,0:T(8,128)}, f32[24,2432]{1,0:T(8,128)}) custom-call(bf16[2,2,2,4,24,1536]{5,4,3,2,1,0:T(8,128)(2,1)} %bitcast.776, bf16[2,2,2,4,24,768]{5,4,3,2,1,0:T(8,128)(2,1)} %bitcast.773, bf16[2,2,2,4,24,2432]{5,4,3,2,1,0:T(8,128)(2,1)} %pad_maximum_fusion.refs_2_), custom_call_target="tpu_custom_call" | custom-call | tf_op jit(solution)/shard_map/scatter_sums/pallas_call | solution.py:341
  (450 shorter events, 172.1 us)
Async XLA Ops:
  0.6 52.5 %copy-start.69 = (s32[1,1,1024]{2,1,0:T(1,128)S(1)}, s32[1,1,1024]{2,1,0:T(1,128)}, u32[]{:S(2)}) copy-start(s32[1,1,1024]{2,1,0:T(1,128)} %param.26) | copy-start | bytes 12292
  0.7 56.0 %copy-start.91 = (f32[384]{0:T(512)}, f32[384]{0:T(512)S(1)}, u32[]{:S(2)}) copy-start(f32[384]{0:T(512)S(1)} %get-tuple-element.497) | copy-start | bytes 4612
  0.7 56.0 %copy-start.93 = (f32[384]{0:T(512)}, f32[384]{0:T(512)S(1)}, u32[]{:S(2)}) copy-start(f32[384]{0:T(512)S(1)} %get-tuple-element.498) | copy-start | bytes 4612
  50.8 147.9 %copy-start.85 = (f32[768]{0:T(1024)}, f32[768]{0:T(1024)S(1)}, u32[]{:S(2)}) copy-start(f32[768]{0:T(1024)S(1)} %get-tuple-element.386) | copy-start | bytes 9220
  90.8 9.4 %copy-start.35 = (f32[1024,384]{1,0:T(8,128)S(1)}, f32[1024,384]{1,0:T(8,128)}, u32[]{:S(2)}) copy-start(f32[1024,384]{1,0:T(8,128)} %copy-done.34) | copy-start | bytes 4718596
  93.2 101.9 %copy-start.47 = (bf16[256,768]{1,0:T(8,128)(2,1)}, bf16[256,768]{1,0:T(8,128)(2,1)S(1)}, u32[]{:S(2)}) copy-start(bf16[256,768]{1,0:T(8,128)(2,1)S(1)} %fusion.107) | copy-start | bytes 1179652
  93.8 228.1 %collective-permute-start.1 = (bf16[1,768]{1,0:T(2,128)(2,1)}, bf16[1,768]{1,0:T(2,128)(2,1)}, u32[]{:S(2)}, u32[]{:S(2)}) collective-permute-start(bf16[1,768]{1,0:T(2,128)(2,1)} %get-tuple-element.484), channel_id=1, source_target_pairs={{4,0},{8,4},{12,8},{16,12},{20,16},{24,20},{28,24},{5,1},{9,5},{13... | collective-permute-start | bytes 4616 | tf_op jit(solution)/shard_map/ppermute | solution.py:476
  95.1 228.9 %collective-permute-start = (bf16[1,768]{1,0:T(2,128)(2,1)}, bf16[1,768]{1,0:T(2,128)(2,1)}, u32[]{:S(2)}, u32[]{:S(2)}) collective-permute-start(bf16[1,768]{1,0:T(2,128)(2,1)} %get-tuple-element.483), channel_id=1, source_target_pairs={{0,4},{4,8},{8,12},{12,16},{16,20},{20,24},{24,28},{1,5},{5,9},{9,... | collective-permute-start | bytes 4616 | tf_op jit(solution)/shard_map/ppermute | solution.py:474
  103.4 94.8 %copy-start.42 = (bf16[1,256,768]{2,1,0:T(8,128)(2,1)S(1)}, bf16[1,256,768]{2,1,0:T(8,128)(2,1)}, u32[]{:S(2)}) copy-start(bf16[1,256,768]{2,1,0:T(8,128)(2,1)} %param.24) | copy-start | bytes 1179652
  103.4 95.3 %copy-start.17 = (bf16[2,2,2,4,24,2432]{5,4,3,2,1,0:T(8,128)(2,1)S(1)}, bf16[2,2,2,4,24,2432]{5,4,3,2,1,0:T(8,128)(2,1)}, u32[]{:S(2)}) copy-start(bf16[2,2,2,4,24,2432]{5,4,3,2,1,0:T(8,128)(2,1)} %copy-done.16) | copy-start | bytes 11206660
  264.5 23.0 %copy-start.8 = (bf16[2,2,2,4,24,768]{5,4,3,2,1,0:T(8,128)(2,1)S(1)}, bf16[2,2,2,4,24,768]{5,4,3,2,1,0:T(8,128)(2,1)}, u32[]{:S(2)}) copy-start(bf16[2,2,2,4,24,768]{5,4,3,2,1,0:T(8,128)(2,1)} %copy-done.7) | copy-start | bytes 3538948
  264.5 23.0 %copy-start.43 = (bf16[1,256,768]{2,1,0:T(8,128)(2,1)S(1)}, bf16[1,256,768]{2,1,0:T(8,128)(2,1)}, u32[]{:S(2)}) copy-start(bf16[1,256,768]{2,1,0:T(8,128)(2,1)} %param.24) | copy-start | bytes 1179652
  286.8 28.0 %copy-start.45 = (f32[12,256,64]{1,2,0:T(8,128)}, f32[12,256,64]{1,2,0:T(8,128)S(1)}, u32[]{:S(2)}) copy-start(f32[12,256,64]{1,2,0:T(8,128)S(1)} %get-tuple-element.326) | copy-start | bytes 2359300
  287.5 28.8 %copy-start.60 = (bf16[256,12,64]{0,2,1:T(8,128)(2,1)}, bf16[256,12,64]{0,2,1:T(8,128)(2,1)S(1)}, u32[]{:S(2)}) copy-start(bf16[256,12,64]{0,2,1:T(8,128)(2,1)S(1)} %bitcast_convert_fusion) | copy-start | bytes 1179652
  287.5 28.2 %copy-start.103 = (s32[1024,1]{0,1:T(1,128)S(1)}, s32[1024,1]{0,1:T(1,128)}, u32[]{:S(2)}) copy-start(s32[1024,1]{0,1:T(1,128)} %compare_select_fusion) | copy-start | bytes 12292
  324.0 13.3 %slice-start = ((s8[4718592]{0:T(1024)(128)(4,1)}), s8[4194304]{0:T(1024)(128)(4,1)S(1)}, s32[]{:S(2)}) async-start(s8[4718592]{0:T(1024)(128)(4,1)} %bitcast.755), calls=%async_computation | async-start | bytes 8388608
  328.1 9.2 %slice-start.1 = ((s8[4718592]{0:T(1024)(128)(4,1)}), s8[524288]{0:T(1024)(128)(4,1)S(1)}, s32[]{:S(2)}) async-start(s8[4718592]{0:T(1024)(128)(4,1)} %bitcast.755), calls=%async_computation.1 | async-start | bytes 1048576
  452.6 47.1 %copy-start.18 = (bf16[2,2,2,4,24,2432]{5,4,3,2,1,0:T(8,128)(2,1)S(1)}, bf16[2,2,2,4,24,2432]{5,4,3,2,1,0:T(8,128)(2,1)}, u32[]{:S(2)}) copy-start(bf16[2,2,2,4,24,2432]{5,4,3,2,1,0:T(8,128)(2,1)} %copy-done.16) | copy-start | bytes 11206660
  452.6 47.1 %copy-start.44 = (bf16[1,256,768]{2,1,0:T(8,128)(2,1)S(1)}, bf16[1,256,768]{2,1,0:T(8,128)(2,1)}, u32[]{:S(2)}) copy-start(bf16[1,256,768]{2,1,0:T(8,128)(2,1)} %param.24) | copy-start | bytes 1179652
  452.6 47.1 %copy-start.86 = (f32[768]{0:T(1024)S(1)}, f32[768]{0:T(1024)}, u32[]{:S(2)}) copy-start(f32[768]{0:T(1024)} %copy-done.85) | copy-start | bytes 9220
  452.6 47.1 %copy-start.99 = (f32[256]{0:T(256)S(1)}, f32[256]{0:T(256)}, u32[]{:S(2)}) copy-start(f32[256]{0:T(256)} %copy-done.98) | copy-start | bytes 3076
  510.5 120.5 %collective-permute-start.3 = (bf16[1,768]{1,0:T(2,128)(2,1)S(1)}, bf16[1,768]{1,0:T(2,128)(2,1)S(1)}, u32[]{:S(2)}, u32[]{:S(2)}) collective-permute-start(bf16[1,768]{1,0:T(2,128)(2,1)S(1)} %copy-done.120), channel_id=1, source_target_pairs={{0,4},{4,8},{8,12},{12,16},{16,20},{20,24},{24,28},{1,5},{5,9},{9,... | collective-permute-start | bytes 4616 | tf_op jit(solution)/shard_map/ppermute | solution.py:474
  518.7 110.9 %copy-start.119 = (bf16[1,768]{1,0:T(2,128)(2,1)S(1)}, bf16[1,768]{1,0:T(2,128)(2,1)}, u32[]{:S(2)}) copy-start(bf16[1,768]{1,0:T(2,128)(2,1)} %get-tuple-element.481) | copy-start | bytes 4612
  518.7 112.2 %copy-start.121 = (bf16[768]{0:T(1024)(128)(2,1)S(1)}, bf16[768]{0:T(1024)(128)(2,1)}, u32[]{:S(2)}) copy-start(bf16[768]{0:T(1024)(128)(2,1)} %get-tuple-element.376) | copy-start | bytes 4612
  518.7 112.2 %copy-start.3 = (bf16[2,2,2,4,24,2304]{5,4,3,2,1,0:T(8,128)(2,1)S(1)}, bf16[2,2,2,4,24,2304]{5,4,3,2,1,0:T(8,128)(2,1)}, u32[]{:S(2)}) copy-start(bf16[2,2,2,4,24,2304]{5,4,3,2,1,0:T(8,128)(2,1)} %copy-done.2) | copy-start | bytes 10616836
  518.7 113.9 %copy-start.62 = (f32[256,768]{1,0:T(8,128)S(1)}, f32[256,768]{1,0:T(8,128)}, u32[]{:S(2)}) copy-start(f32[256,768]{1,0:T(8,128)} %fusion.118) | copy-start | bytes 2359300
  518.7 113.9 %copy-start.123 = (f32[256]{0:T(256)S(1)}, f32[256]{0:T(256)}, u32[]{:S(2)}) copy-start(f32[256]{0:T(256)} %copy-done.122) | copy-start | bytes 3076
  629.6 3.1 collective-permute-start.2
  643.9 13.7 %copy-start.104 = (f32[768]{0:T(1024)S(1)}, f32[768]{0:T(1024)}, u32[]{:S(2)}) copy-start(f32[768]{0:T(1024)} %pad_maximum_fusion.21) | copy-start | bytes 9220
  643.9 28.9 %slice-start.4 = ((s8[6291456]{0:T(1024)(128)(4,1)}), s8[2097152]{0:T(1024)(128)(4,1)S(1)}, s32[]{:S(2)}) async-start(s8[6291456]{0:T(1024)(128)(4,1)} %bitcast.768), calls=%async_computation.4 | async-start | bytes 4194304
  692.0 50.9 %copy-start.37 = (f32[1024,768]{1,0:T(8,128)S(1)}, f32[1024,768]{1,0:T(8,128)}, u32[]{:S(2)}) copy-start(f32[1024,768]{1,0:T(8,128)} %copy-done.36) | copy-start | bytes 9437188
  692.0 50.9 %copy-start.52 = (bf16[1,1024,768]{2,1,0:T(8,128)(2,1)S(1)}, bf16[1,1024,768]{2,1,0:T(8,128)(2,1)}, u32[]{:S(2)}) copy-start(bf16[1,1024,768]{2,1,0:T(8,128)(2,1)} %param.39) | copy-start | bytes 4718596
  (102 other events, 309.3 us)

commit v3 on v2

--- a/solution.py
+++ b/solution.py
@@ -374,6 +374,595 @@
     ]
 
 
+HEAD_GROUPS = 4
+
+
+def groups():
+    apart = lax.axis_size("ctx") // HEAD_GROUPS
+    mine = lax.axis_index("ctx")
+    return apart, lax.div(mine, apart), lax.rem(mine, apart)
+
+
+def ctx_partner(gap):
+    return place_of("ctx", lax.bitwise_xor(lax.axis_index("ctx"), gap))
+
+
+def greet_ctx(gaps):
+    barrier = pltpu.get_barrier_semaphore()
+    for gap in gaps:
+        pl.semaphore_signal(
+            barrier, inc=1, device_id=ctx_partner(gap), device_id_type=pl.DeviceIdType.MESH
+        )
+    pl.semaphore_wait(barrier, len(gaps))
+
+
+def spread_kernel(qkv_ref, q_out, kv_out, send_q, send_kv, send_sem, recv_sem, local_sem):
+    apart, group, inner = groups()
+    width = qkv_ref.shape[1] // 3
+    cols = width // HEAD_GROUPS
+    mine = lax.axis_index("ctx")
+    sems = (send_sem, recv_sem)
+    gaps = [gap * apart for gap in range(1, HEAD_GROUPS)] + list(range(1, apart))
+    for other in range(HEAD_GROUPS):
+        send_q[other] = qkv_ref[:, other * cols : (other + 1) * cols]
+        for part in range(2):
+            first = (part + 1) * width + other * cols
+            send_kv[other, :, part * cols : (part + 1) * cols] = qkv_ref[:, first : first + cols]
+    greet_ctx(gaps)
+    kv_copies, q_copies = [], []
+    for gap in range(1, HEAD_GROUPS):
+        other = lax.bitwise_xor(group, gap)
+        partner = ctx_partner(gap * apart)
+        copy = remote(send_kv.at[other], kv_out.at[mine], sems, gap - 1, partner)
+        copy.start()
+        kv_copies.append(copy)
+    for gap in range(1, HEAD_GROUPS):
+        other = lax.bitwise_xor(group, gap)
+        partner = ctx_partner(gap * apart)
+        copy = remote(send_q.at[other], q_out.at[group], sems, HEAD_GROUPS - 2 + gap, partner)
+        copy.start()
+        q_copies.append(copy)
+    own = [
+        pltpu.make_async_copy(send_kv.at[group], kv_out.at[mine], local_sem.at[0]),
+        pltpu.make_async_copy(send_q.at[group], q_out.at[group], local_sem.at[1]),
+    ]
+    for copy in own:
+        copy.start()
+    own[0].wait()
+    number = 2 * (HEAD_GROUPS - 1)
+    passed = []
+    for gap in range(HEAD_GROUPS):
+        if gap:
+            kv_copies[gap - 1].wait_recv()
+        slot = lax.bitwise_xor(mine, gap * apart)
+        for near in range(1, apart):
+            copy = remote(kv_out.at[slot], kv_out.at[slot], sems, number, ctx_partner(near))
+            copy.start()
+            passed.append(copy)
+            number = number + 1
+    own[1].wait()
+    for copy in q_copies:
+        copy.wait_recv()
+    for copy in passed:
+        copy.wait_recv()
+    for copy in kv_copies + q_copies + passed:
+        copy.wait_send()
+
+
+def spread_heads(qkv, collective):
+    rows = qkv.shape[0]
+    count = lax.axis_size("ctx")
+    apart = count // HEAD_GROUPS
+    cols = qkv.shape[1] // 3 // HEAD_GROUPS
+    copies = 2 * (HEAD_GROUPS - 1) + HEAD_GROUPS * (apart - 1)
+    hbm = pl.BlockSpec(memory_space=pl.ANY)
+    return pl.pallas_call(
+        spread_kernel,
+        out_shape=(
+            jax.ShapeDtypeStruct((HEAD_GROUPS, rows, cols), qkv.dtype),
+            jax.ShapeDtypeStruct((count, rows, 2 * cols), qkv.dtype),
+        ),
+        in_specs=[pl.BlockSpec(memory_space=pltpu.VMEM)],
+        out_specs=(hbm, hbm),
+        scratch_shapes=[
+            pltpu.VMEM((HEAD_GROUPS, rows, cols), qkv.dtype),
+            pltpu.VMEM((HEAD_GROUPS, rows, 2 * cols), qkv.dtype),
+            pltpu.SemaphoreType.DMA((copies,)),
+            pltpu.SemaphoreType.DMA((copies,)),
+            pltpu.SemaphoreType.DMA((2,)),
+        ],
+        compiler_params=pltpu.CompilerParams(
+            collective_id=collective, has_side_effects=True, vmem_limit_bytes=16 << 20
+        ),
+        name="spread_heads",
+    )(qkv)
+
+
+def head_rows(value, head):
+    rows = lax.broadcasted_iota(jnp.int32, value.shape, 0)
+    inside = (rows >= head * HEAD_DIM) & (rows < (head + 1) * HEAD_DIM)
+    return jnp.where(inside, value, jnp.zeros_like(value))
+
+
+def head_cols(value, head):
+    cols = lax.broadcasted_iota(jnp.int32, value.shape, 1)
+    inside = (cols >= head * HEAD_DIM) & (cols < (head + 1) * HEAD_DIM)
+    return jnp.where(inside, value, jnp.zeros_like(value))
+
+
+def turned(value):
+    return jnp.transpose(value.astype(jnp.float32))
+
+
+def dot32(left, right):
+    return jnp.dot(left, right, preferred_element_type=jnp.float32)
+
+
+def key_mask(key_block, size, spans_ref, slot):
+    keys = key_block * size + lax.broadcasted_iota(jnp.int32, (size, size), 0)
+    return (keys >= spans_ref[slot, 0:1, :]) & (keys < spans_ref[slot, 1:2, :])
+
+
+def attend_kernel(bounds, q_ref, kv_ref, spans_ref, o_ref, exact_ref, log_ref, vt_s, qt_s, ot_s, stat_s):
+    blocks, size, both = kv_ref.shape
+    cols = both // 2
+    heads = cols // HEAD_DIM
+
+    def turn_values(block, carry):
+        vt_s[block] = turned(kv_ref[block, :, cols:]).astype(jnp.bfloat16)
+        return carry
+
+    lax.fori_loop(0, blocks, turn_values, 0)
+
+    def query_block(slot, carry):
+        qt = (turned(q_ref[slot]) * HEAD_DIM ** (-0.5)).astype(jnp.bfloat16)
+        for head in range(heads):
+            qt_s[head] = head_rows(qt, head)
+        ot_s[...] = jnp.zeros_like(ot_s)
+        stat_s[0] = jnp.full_like(stat_s[0], masked_score)
+        stat_s[1] = jnp.zeros_like(stat_s[1])
+
+        def key_step(block, carry):
+            allowed = key_mask(block, size, spans_ref, slot)
+            keys = kv_ref[block, :, :cols]
+            for head in range(heads):
+                row = slice(head, head + 1)
+                part = slice(head * HEAD_DIM, (head + 1) * HEAD_DIM)
+                scores = jnp.where(allowed, dot32(keys, qt_s[head]), masked_score)
+                old = stat_s[0, row, :]
+                top = jnp.maximum(old, jnp.max(scores, axis=0, keepdims=True))
+                factor = jnp.exp(old - top)
+                weights = jnp.exp(scores - top)
+                stat_s[0, row, :] = top
+                stat_s[1, row, :] = stat_s[1, row, :] * factor + jnp.sum(
+                    weights, axis=0, keepdims=True
+                )
+                ot_s[part, :] = ot_s[part, :] * factor + dot32(
+                    vt_s[block, part, :], weights.astype(jnp.bfloat16)
+                )
+            return carry
+
+        lax.fori_loop(bounds[slot, 0], bounds[slot, 1], key_step, 0)
+        for head in range(heads):
+            row = slice(head, head + 1)
+            part = slice(head * HEAD_DIM, (head + 1) * HEAD_DIM)
+            ot_s[part, :] = ot_s[part, :] / stat_s[1, row, :]
+            log_ref[slot, row, :] = stat_s[0, row, :] + jnp.log(stat_s[1, row, :])
+        exact = jnp.transpose(ot_s[...])
+        exact_ref[slot] = exact
+        o_ref[slot] = exact.astype(jnp.bfloat16)
+        return carry
+
+    lax.fori_loop(0, q_ref.shape[0], query_block, 0)
+
+
+def attend_back_kernel(
+    bounds, q_ref, kv_ref, g_ref, exact_ref, log_ref, spans_ref, dq_ref, dkv_ref, v_s, kt_s, qt_s, gt_s,
+    qn_s, gn_s, dqt_s, row_s, dk_s, dv_s
+):
+    blocks, size, both = kv_ref.shape
+    cols = both // 2
+    heads = cols // HEAD_DIM
+    scale = HEAD_DIM ** (-0.5)
+    bf16 = jnp.bfloat16
+
+    def turn_keys(block, carry):
+        kt_s[block] = turned(kv_ref[block, :, :cols]).astype(bf16)
+        v_s[block] = kv_ref[block, :, cols:]
+        dk_s[block] = jnp.zeros(dk_s.shape[1:], jnp.float32)
+        dv_s[block] = jnp.zeros(dv_s.shape[1:], jnp.float32)
+        return carry
+
+    lax.fori_loop(0, blocks, turn_keys, 0)
+
+    def query_block(slot, carry):
+        qn = (q_ref[slot].astype(jnp.float32) * scale).astype(bf16)
+        gn = g_ref[slot]
+        qt = turned(qn).astype(bf16)
+        gt32 = turned(gn)
+        products = gt32 * jnp.transpose(exact_ref[slot])
+        gt = gt32.astype(bf16)
+        for head in range(heads):
+            part = slice(head * HEAD_DIM, (head + 1) * HEAD_DIM)
+            qt_s[head] = head_rows(qt, head)
+            gt_s[head] = head_rows(gt, head)
+            qn_s[head] = head_cols(qn, head)
+            gn_s[head] = head_cols(gn, head)
+            row_s[head : head + 1, :] = jnp.sum(products[part], axis=0, keepdims=True)
+        dqt_s[...] = jnp.zeros_like(dqt_s)
+
+        def key_step(block, carry):
+            allowed = key_mask(block, size, spans_ref, slot)
+            keys = kv_ref[block, :, :cols]
+            values = v_s[block]
+            dk = jnp.zeros(dk_s.shape[1:], jnp.float32)
+            dv = jnp.zeros(dv_s.shape[1:], jnp.float32)
+            for head in range(heads):
+                row = slice(head, head + 1)
+                part = slice(head * HEAD_DIM, (head + 1) * HEAD_DIM)
+                scores = jnp.where(allowed, dot32(keys, qt_s[head]), masked_score)
+                weights = jnp.exp(scores - log_ref[slot, row, :])
+                slopes = dot32(values, gt_s[head])
+                ds = (weights * (slopes - row_s[row, :])).astype(bf16)
+                dqt_s[part, :] = dqt_s[part, :] + dot32(kt_s[block, part, :], ds)
+                dk = dk + dot32(ds, qn_s[head])
+                dv = dv + dot32(weights.astype(bf16), gn_s[head])
+            dk_s[block] = dk_s[block] + dk
+            dv_s[block] = dv_s[block] + dv
+            return carry
+
+        lax.fori_loop(bounds[slot, 0], bounds[slot, 1], key_step, 0)
+        dq_ref[slot] = (jnp.transpose(dqt_s[...]) * scale).astype(bf16)
+        return carry
+
+    lax.fori_loop(0, q_ref.shape[0], query_block, 0)
+
+    def write(block, carry):
+        dkv_ref[block, :, :cols] = dk_s[block].astype(bf16)
+        dkv_ref[block, :, cols:] = dv_s[block].astype(bf16)
+        return carry
+
+    lax.fori_loop(0, blocks, write, 0)
+
+
+def attend(bounds, q, kv, spans):
+    slots, size, cols = q.shape
+    blocks = kv.shape[0]
+    heads = cols // HEAD_DIM
+    whole = pl.BlockSpec(memory_space=pltpu.VMEM)
+    f32, bf16 = jnp.float32, jnp.bfloat16
+    return pl.pallas_call(
+        attend_kernel,
+        out_shape=(
+            jax.ShapeDtypeStruct(q.shape, bf16),
+            jax.ShapeDtypeStruct(q.shape, f32),
+            jax.ShapeDtypeStruct((slots, 8, size), f32),
+        ),
+        in_specs=[pl.BlockSpec(memory_space=pltpu.SMEM), whole, whole, whole],
+        out_specs=(whole, whole, whole),
+        scratch_shapes=[
+            pltpu.VMEM((blocks, cols, size), bf16),
+            pltpu.VMEM((heads, cols, size), bf16),
+            pltpu.VMEM((cols, size), f32),
+            pltpu.VMEM((2, 8, size), f32),
+        ],
+        compiler_params=pltpu.CompilerParams(vmem_limit_bytes=32 << 20),
+        name="attend",
+    )(bounds, q, kv, spans)
+
+
+def attend_back(bounds, q, kv, g, exact, log, spans):
+    slots, size, cols = q.shape
+    blocks = kv.shape[0]
+    heads = cols // HEAD_DIM
+    whole = pl.BlockSpec(memory_space=pltpu.VMEM)
+    f32, bf16 = jnp.float32, jnp.bfloat16
+    return pl.pallas_call(
+        attend_back_kernel,
+        out_shape=(
+            jax.ShapeDtypeStruct(q.shape, bf16),
+            jax.ShapeDtypeStruct(kv.shape, bf16),
+        ),
+        in_specs=[pl.BlockSpec(memory_space=pltpu.SMEM)] + [whole] * 6,
+        out_specs=(whole, whole),
+        scratch_shapes=[
+            pltpu.VMEM((blocks, size, cols), bf16),
+            pltpu.VMEM((blocks, cols, size), bf16),
+            pltpu.VMEM((heads, cols, size), bf16),
+            pltpu.VMEM((heads, cols, size), bf16),
+            pltpu.VMEM((heads, size, cols), bf16),
+            pltpu.VMEM((heads, size, cols), bf16),
+            pltpu.VMEM((cols, size), f32),
+            pltpu.VMEM((8, size), f32),
+            pltpu.VMEM((blocks, size, cols), f32),
+            pltpu.VMEM((blocks, size, cols), f32),
+        ],
+        compiler_params=pltpu.CompilerParams(vmem_limit_bytes=48 << 20),
+        name="attend_back",
+    )(bounds, q, kv, g, exact, log, spans)
+
+
+def exchange_sums(sums_ref, sems, base):
+    mine = lax.axis_index("ctx")
+    copies = []
+    for gap in range(1, lax.axis_size("ctx")):
+        copy = remote(sums_ref.at[mine], sums_ref.at[mine], sems, base + gap - 1, ctx_partner(gap))
+        copy.start()
+        copies.append(copy)
+    return copies
+
+
+def total_of(sums_ref):
+    total = sums_ref[0]
+    for slot in range(1, sums_ref.shape[0]):
+        total = total + sums_ref[slot]
+    return total
+
+
+def summed(value):
+    return jnp.sum(jnp.sum(value, axis=0, keepdims=True), axis=1, keepdims=True)
+
+
+def join_kernel(
+    elements, o_ref, tokens_ref, weight_ref, attn_ref, proj_ref, resid_ref, stat_ref, land, sums, send_sem,
+    recv_sem, local_sem
+):
+    apart, group, inner = groups()
+    cols = o_ref.shape[2]
+    sems = (send_sem, recv_sem)
+    greet_ctx(list(range(1, lax.axis_size("ctx"))))
+    copies = []
+    for gap in range(1, HEAD_GROUPS):
+        other = lax.bitwise_xor(group, gap)
+        copy = remote(o_ref.at[other], land.at[group], sems, gap - 1, ctx_partner(gap * apart))
+        copy.start()
+        copies.append(copy)
+    own = pltpu.make_async_copy(o_ref.at[group], land.at[group], local_sem.at[0])
+    own.start()
+    tokens = tokens_ref[...].astype(jnp.float32)
+    square = summed(tokens * tokens)
+    own.wait()
+    for copy in copies:
+        copy.wait_recv()
+    proj = jnp.zeros(proj_ref.shape, jnp.float32)
+    for other in range(HEAD_GROUPS):
+        part = land[other]
+        attn_ref[:, other * cols : (other + 1) * cols] = part
+        proj = proj + dot32(part, weight_ref[other * cols : (other + 1) * cols, :])
+    proj_ref[...] = proj
+    row = lax.broadcasted_iota(jnp.int32, sums.shape[1:], 0)
+    mine = lax.axis_index("ctx")
+    sums[mine] = jnp.where(
+        row == 0,
+        summed(proj * proj),
+        jnp.where(row == 1, summed(tokens * proj), jnp.where(row == 2, square, 0.0)),
+    )
+    small = exchange_sums(sums, sems, HEAD_GROUPS - 1)
+    for copy in small:
+        copy.wait_recv()
+    total = total_of(sums)
+    stat_ref[...] = total
+    sq_proj, cross, sq_tok = total[0:1, 0:1], total[1:2, 0:1], total[2:3, 0:1]
+    rms_scale = lax.rsqrt(sq_proj / elements + 1e-06)
+    stream_sq = (sq_tok + 2.0 * rms_scale * cross + rms_scale * rms_scale * sq_proj) / elements
+    stream_scale = lax.rsqrt(stream_sq + 1e-06)
+    resid_ref[...] = (tokens + proj_ref[...] * rms_scale) * stream_scale
+    for copy in copies + small:
+        copy.wait_send()
+
+
+def join_heads(o, tokens, weight, elements, collective):
+    rows, width = tokens.shape
+    count = lax.axis_size("ctx")
+    copies = HEAD_GROUPS - 1 + count - 1
+    whole = pl.BlockSpec(memory_space=pltpu.VMEM)
+    f32, bf16 = jnp.float32, jnp.bfloat16
+    return pl.pallas_call(
+        functools.partial(join_kernel, elements),
+        out_shape=(
+            jax.ShapeDtypeStruct((rows, width), bf16),
+            jax.ShapeDtypeStruct((rows, width), f32),
+            jax.ShapeDtypeStruct((rows, width), f32),
+            jax.ShapeDtypeStruct((8, 128), f32),
+        ),
+        in_specs=[whole] * 3,
+        out_specs=(whole,) * 4,
+        scratch_shapes=[
+            pltpu.VMEM(o.shape, bf16),
+            pltpu.VMEM((count, 8, 128), f32),
+            pltpu.SemaphoreType.DMA((copies,)),
+            pltpu.SemaphoreType.DMA((copies,)),
+            pltpu.SemaphoreType.DMA((1,)),
+        ],
+        compiler_params=pltpu.CompilerParams(
+            collective_id=collective, has_side_effects=True, vmem_limit_bytes=24 << 20
+        ),
+        name="join_heads",
+    )(o, tokens, weight)
+
+
+def part_kernel(
+    elements, resid_grad_ref, proj_ref, tokens_ref, weight_ref, stat_ref, stream_grad_ref, proj_grad_ref,
+    g_out, send, sums, send_sem, recv_sem, local_sem
+):
+    apart, group, inner = groups()
+    cols = g_out.shape[2]
+    sems = (send_sem, recv_sem)
+    greet_ctx(list(range(1, lax.axis_size("ctx"))))
+    mine = lax.axis_index("ctx")
+    sq_proj, cross, sq_tok = stat_ref[0:1, 0:1], stat_ref[1:2, 0:1], stat_ref[2:3, 0:1]
+    rms_scale = lax.rsqrt(sq_proj / elements + 1e-06)
+    stream_sq = (sq_tok + 2.0 * rms_scale * cross + rms_scale * rms_scale * sq_proj) / elements
+    stream_scale = lax.rsqrt(stream_sq + 1e-06)
+    stream = tokens_ref[...].astype(jnp.float32) + proj_ref[...] * rms_scale
+    row = lax.broadcasted_iota(jnp.int32, sums.shape[1:], 0)
+    sums[mine] = jnp.where(
+        row == 0,
+        summed(resid_grad_ref[...] * stream),
+        jnp.where(row == 1, summed(resid_grad_ref[...] * proj_ref[...]), 0.0),
+    )
+    small = exchange_sums(sums, sems, HEAD_GROUPS - 1)
+    for copy in small:
+        copy.wait_recv()
+    total = total_of(sums)
+    mean_gs = total[0:1, 0:1] / elements
+    mean_gp = total[1:2, 0:1] / elements
+    mean_sp = (cross + rms_scale * sq_proj) / elements
+    cubed = stream_scale * stream_scale * stream_scale
+    stream_grad = stream_scale * resid_grad_ref[...] - cubed * mean_gs * stream
+    stream_grad_ref[...] = stream_grad
+    mean_gsp = stream_scale * mean_gp - cubed * mean_gs * mean_sp
+    proj_grad = (
+        rms_scale * stream_grad - rms_scale * rms_scale * rms_scale * mean_gsp * proj_ref[...]
+    ).astype(jnp.bfloat16)
+    proj_grad_ref[...] = proj_grad
+    for other in range(HEAD_GROUPS):
+        send[other] = lax.dot_general(
+            proj_grad,
+            weight_ref[other * cols : (other + 1) * cols, :],
+            (((1,), (1,)), ((), ())),
+            preferred_element_type=jnp.float32,
+        ).astype(jnp.bfloat16)
+    copies = []
+    for gap in range(1, HEAD_GROUPS):
+        other = lax.bitwise_xor(group, gap)
+        copy = remote(send.at[other], g_out.at[group], sems, gap - 1, ctx_partner(gap * apart))
+        copy.start()
+        copies.append(copy)
+    own = pltpu.make_async_copy(send.at[group], g_out.at[group], local_sem.at[0])
+    own.start()
+    own.wait()
+    for copy in copies:
+        copy.wait_recv()
+    for copy in copies + small:
+        copy.wait_send()
+
+
+def part_heads(resid_grad, proj, tokens, weight, stat, elements, collective):
+    rows, width = tokens.shape
+    count = lax.axis_size("ctx")
+    copies = HEAD_GROUPS - 1 + count - 1
+    cols = width // HEAD_GROUPS
+    whole = pl.BlockSpec(memory_space=pltpu.VMEM)
+    f32, bf16 = jnp.float32, jnp.bfloat16
+    return pl.pallas_call(
+        functools.partial(part_kernel, elements),
+        out_shape=(
+            jax.ShapeDtypeStruct((rows, width), f32),
+            jax.ShapeDtypeStruct((rows, width), bf16),
+            jax.ShapeDtypeStruct((HEAD_GROUPS, rows, cols), bf16),
+        ),
+        in_specs=[whole] * 5,
+        out_specs=(whole, whole, pl.BlockSpec(memory_space=pl.ANY)),
+        scratch_shapes=[
+            pltpu.VMEM((HEAD_GROUPS, rows, cols), bf16),
+            pltpu.VMEM((count, 8, 128), f32),
+            pltpu.SemaphoreType.DMA((copies,)),
+            pltpu.SemaphoreType.DMA((copies,)),
+            pltpu.SemaphoreType.DMA((1,)),
+        ],
+        compiler_params=pltpu.CompilerParams(
+            collective_id=collective, has_side_effects=True, vmem_limit_bytes=24 << 20
+        ),
+        name="part_heads",
+    )(resid_grad, proj, tokens, weight, stat)
+
+
+def collect_kernel(dq_ref, dkv_ref, out_ref, near_land, own_s, q_land, kv_land, send_sem, recv_sem, local_sem):
+    apart, group, inner = groups()
+    cols = dq_ref.shape[2]
+    rows = dq_ref.shape[1]
+    width = cols * HEAD_GROUPS
+    sems = (send_sem, recv_sem)
+    gaps = [gap * apart for gap in range(1, HEAD_GROUPS)] + list(range(1, apart))
+    greet_ctx(gaps)
+    number = 0
+    near = []
+    for gap in range(1, apart):
+        other = lax.bitwise_xor(inner, gap)
+        copy = remote(dkv_ref.at[:, other], near_land.at[gap - 1], sems, number, ctx_partner(gap))
+        copy.start()
+        near.append(copy)
+        number = number + 1
+    own = pltpu.make_async_copy(dkv_ref.at[:, inner], own_s, local_sem.at[0])
+    own.start()
+    own_q = pltpu.make_async_copy(dq_ref.at[group], q_land.at[group], local_sem.at[1])
+    own_q.start()
+    far_q = []
+    for gap in range(1, HEAD_GROUPS):
+        other = lax.bitwise_xor(group, gap)
+        copy = remote(dq_ref.at[other], q_land.at[group], sems, number, ctx_partner(gap * apart))
+        copy.start()
+        far_q.append(copy)
+        number = number + 1
+    own.wait()
+    for copy in near:
+        copy.wait_recv()
+    chunk = 32
+
+    def add(position, carry):
+        slot = lax.div(position, rows // chunk)
+        down = pl.ds(pl.multiple_of(lax.rem(position, rows // chunk) * chunk, chunk), chunk)
+        total = own_s[slot, down, :].astype(jnp.float32)
+        for gap in range(1, apart):
+            total = total + near_land[gap - 1, slot, down, :].astype(jnp.float32)
+        own_s[slot, down, :] = total.astype(own_s.dtype)
+        return carry
+
+    lax.fori_loop(0, HEAD_GROUPS * (rows // chunk), add, 0)
+    own_kv = pltpu.make_async_copy(own_s.at[group], kv_land.at[group], local_sem.at[2])
+    own_kv.start()
+    far_kv = []
+    for gap in range(1, HEAD_GROUPS):
+        other = lax.bitwise_xor(group, gap)
+        copy = remote(own_s.at[other], kv_land.at[group], sems, number, ctx_partner(gap * apart))
+        copy.start()
+        far_kv.append(copy)
+        number = number + 1
+    own_q.wait()
+    for copy in far_q:
+        copy.wait_recv()
+    for other in range(HEAD_GROUPS):
+        out_ref[:, other * cols : (other + 1) * cols] = q_land[other]
+    own_kv.wait()
+    for copy in far_kv:
+        copy.wait_recv()
+    for other in range(HEAD_GROUPS):
+        for part in range(2):
+            first = (part + 1) * width + other * cols
+            out_ref[:, first : first + cols] = kv_land[other, :, part * cols : (part + 1) * cols]
+    for copy in near + far_q + far_kv:
+        copy.wait_send()
+
+
+def collect_heads(dq, dkv, collective):
+    slots, rows, cols = dq.shape
+    count = lax.axis_size("ctx")
+    apart = count // HEAD_GROUPS
+    copies = apart - 1 + 2 * (HEAD_GROUPS - 1)
+    hbm = pl.BlockSpec(memory_space=pl.ANY)
+    bf16 = jnp.bfloat16
+    return pl.pallas_call(
+        collect_kernel,
+        out_shape=jax.ShapeDtypeStruct((rows, 3 * cols * HEAD_GROUPS), bf16),
+        in_specs=[hbm, hbm],
+        out_specs=pl.BlockSpec(memory_space=pltpu.VMEM),
+        scratch_shapes=[
+            pltpu.VMEM((max(apart - 1, 1), HEAD_GROUPS, rows, 2 * cols), bf16),
+            pltpu.VMEM((HEAD_GROUPS, rows, 2 * cols), bf16),
+            pltpu.VMEM((HEAD_GROUPS, rows, cols), bf16),
+            pltpu.VMEM((HEAD_GROUPS, rows, 2 * cols), bf16),
+            pltpu.SemaphoreType.DMA((copies,)),
+            pltpu.SemaphoreType.DMA((copies,)),
+            pltpu.SemaphoreType.DMA((3,)),
+        ],
+        compiler_params=pltpu.CompilerParams(
+            collective_id=collective, has_side_effects=True, vmem_limit_bytes=24 << 20
+        ),
+        name="collect_heads",
+    )(dq, dkv.reshape(HEAD_GROUPS, apart, rows, 2 * cols))
+
+
 def scan_kernel(forward_first, a_ref, b_ref, local_ref, cum_ref, total_ref, coef_s, term_s):
     rows, width = a_ref.shape
     segments = 8
@@ -489,30 +1078,6 @@
 
 def gelu_exact(values):
     return jax.nn.gelu(values, approximate=False)
-
-
-def doc_index(positions, starts):
-    return jnp.sum((starts[None, :] <= positions[:, None]).astype(jnp.int32), axis=1) - 1
-
-
-def docs_meet(first_docs, second_docs):
-    return jnp.logical_and(first_docs[0] <= second_docs[-1], second_docs[0] <= first_docs[-1])
-
-
-def score_block(query_blk, key_blk, query_docs, key_docs):
-    scores = jnp.einsum(
-        "qhe,khe->hqk", query_blk, key_blk, preferred_element_type=jnp.float32
-    ) * HEAD_DIM ** (-0.5)
-    allowed = query_docs[None, :, None] == key_docs[None, None, :]
-    return (scores, allowed)
-
-
-def grad_block(query_blk, key_blk, value_blk, grad_blk, query_docs, key_docs, log_total, row_term):
-    scores, allowed = score_block(query_blk, key_blk, query_docs, key_docs)
-    probs = jnp.where(allowed, jnp.exp(scores - log_total[:, :, None]), 0.0)
-    dprobs = jnp.einsum("qhe,khe->hqk", grad_blk, value_blk, preferred_element_type=jnp.float32)
-    dscores = (probs * (dprobs - row_term[:, :, None])).astype(jnp.bfloat16)
-    return (probs, dscores)
 
 
 def body(
@@ -561,16 +1126,12 @@
     char_rows = chars.shape[1]
     half_width = width // 2
     seq_len = tok_rows * lax.axis_size("ctx")
-    key_block = min(seq_len, 512)
-    key_count = seq_len // key_block
-    scale = HEAD_DIM ** (-0.5)
     token_in = tokens[0].astype(f32)
     char_in = chars[0].astype(f32)
     char_map = char_token[0, 0]
     lengths = doc_lengths[0]
     starts = jnp.cumsum(lengths) - lengths
     positions = lax.axis_index("ctx") * tok_rows + jnp.arange(tok_rows, dtype=jnp.int32)
-    query_docs = doc_index(positions, starts)
     doc_first = jnp.any(starts[None, :] == positions[:, None], axis=1)
     doc_last = jnp.any(starts[None, :] == positions[:, None] + 1, axis=1)
     onehot = char_map[None, :] == jnp.arange(tok_rows, dtype=jnp.int32)[:, None]
@@ -586,62 +1147,29 @@
     keep_bwd = 1.0 - (last_char & closes_doc).astype(f32)
     attn_in = normed(token_in, attn_gain_f).astype(bf16)
     qkv = jnp.dot(attn_in, qkv_full, preferred_element_type=f32).astype(bf16)
-    queries = qkv[:, :width]
-    keys = qkv[:, width : 2 * width]
-    values = qkv[:, 2 * width :]
-    keys_all, values_all = gather_all(
-        [keys, values], [((0, 0, width, True), (1, 0, width, False))], False, 2
-    )
-    query_heads = queries.reshape(tok_rows, HEADS, HEAD_DIM)
-    key_blocks = keys_all.reshape(key_count, key_block, HEADS, HEAD_DIM)
-    value_blocks = values_all.reshape(key_count, key_block, HEADS, HEAD_DIM)
-    key_docs = doc_index(jnp.arange(seq_len, dtype=jnp.int32), starts).reshape(key_count, key_block)
-
-    def forward_block(carry, inputs):
-        key_blk, value_blk, docs_blk = inputs
-
-        def forward_used(state):
-            run_max, run_total, run_acc = state
-            scores, allowed = score_block(query_heads, key_blk, query_docs, docs_blk)
-            scores = jnp.where(allowed, scores, masked_score)
-            new_max = jnp.maximum(run_max, jnp.max(scores, axis=2))
-            factor = jnp.exp(run_max - new_max)
-            weights = jnp.where(allowed, jnp.exp(scores - new_max[:, :, None]), 0.0)
-            run_total = run_total * factor + jnp.sum(weights, axis=2)
-            run_acc = run_acc * factor[:, :, None] + jnp.einsum(
-                "hqk,khe->hqe", weights.astype(bf16), value_blk, preferred_element_type=f32
-            )
-            return (new_max, run_total, run_acc)
-
-        def forward_skipped(state):
-            return state
-
-        return (
-            lax.cond(docs_meet(query_docs, docs_blk), forward_used, forward_skipped, carry),
-            None,
-        )
-
-    start_carry = (
-        jnp.full((HEADS, tok_rows), masked_score, f32),
-        jnp.zeros((HEADS, tok_rows), f32),
-        jnp.zeros((HEADS, tok_rows, HEAD_DIM), f32),
-    )
-    (run_max, run_total, run_acc), _ = lax.scan(
-        forward_block, start_carry, (key_blocks, value_blocks, key_docs)
-    )
-    log_total = run_max + jnp.log(run_total)
-    attn_heads = jnp.transpose(run_acc / run_total[:, :, None], (1, 0, 2))
-    attn_out = attn_heads.reshape(tok_rows, width).astype(bf16)
-    proj = jnp.dot(attn_out, out_full, preferred_element_type=f32)
-    sq_proj, cross_sum, sq_tok = lax.psum(
-        (jnp.sum(proj * proj), jnp.sum(token_in * proj), jnp.sum(token_in * token_in)), "ctx"
-    )
     elements = seq_len * width
-    rms_scale = lax.rsqrt(sq_proj / elements + 1e-06)
-    stream_sq = (sq_tok + 2.0 * rms_scale * cross_sum + rms_scale * rms_scale * sq_proj) / elements
-    stream_scale = lax.rsqrt(stream_sq + 1e-06)
-    stream = token_in + proj * rms_scale
-    resid = stream * stream_scale
+    apart = lax.axis_size("ctx") // HEAD_GROUPS
+    slot_blocks = jnp.arange(HEAD_GROUPS, dtype=jnp.int32) * apart + lax.rem(
+        lax.axis_index("ctx"), apart
+    )
+    slot_positions = slot_blocks[:, None] * tok_rows + jnp.arange(tok_rows, dtype=jnp.int32)[None]
+    before = starts[None, None, :] <= slot_positions[:, :, None]
+    doc_begin = jnp.max(jnp.where(before, starts, 0), axis=2)
+    doc_end = jnp.min(jnp.where(before, seq_len, starts), axis=2)
+    spans = jnp.concatenate(
+        [
+            doc_begin[:, None, :],
+            doc_end[:, None, :],
+            jnp.zeros((HEAD_GROUPS, 6, tok_rows), jnp.int32),
+        ],
+        axis=1,
+    )
+    bounds = jnp.stack(
+        [doc_begin[:, 0] // tok_rows, (doc_end[:, -1] + tok_rows - 1) // tok_rows], axis=1
+    )
+    q_heads, kv_heads = spread_heads(qkv, 2)
+    o_heads, exact_heads, log_heads = attend(bounds, q_heads, kv_heads, spans)
+    attn_out, proj, resid, sums = join_heads(o_heads, tokens[0], out_full, elements, 6)
     char_low = normed(char_in, char_gain_f).astype(bf16)
     gates = jnp.dot(char_low, gru_full, preferred_element_type=f32)
     ramp = jnp.arange(half_width, dtype=f32) / (half_width - 1)
@@ -742,74 +1270,14 @@
     _, char_norm_back = jax.vjp(normed, char_in, char_gain_f)
     grad_char_in, grad_char_gain = char_norm_back(grad_char_norm)
     grad_chars_out = (cot_chr_f + grad_char_in).astype(bf16)
-    dot_stream, dot_proj = lax.psum(
-        (jnp.sum(grad_resid * stream), jnp.sum(grad_resid * proj)), "ctx"
-    )
-    mean_gs = dot_stream / elements
-    mean_gp = dot_proj / elements
-    mean_sp = (cross_sum + rms_scale * sq_proj) / elements
-    grad_stream = stream_scale * grad_resid - stream_scale**3 * mean_gs * stream
-    mean_gsp = stream_scale * mean_gp - stream_scale**3 * mean_gs * mean_sp
-    grad_proj = (rms_scale * grad_stream - rms_scale**3 * mean_gsp * proj).astype(bf16)
+    grad_stream, grad_proj, g_heads = part_heads(
+        grad_resid, proj, tokens[0], out_full, sums, elements, 7
+    )
     grad_out_proj = jnp.einsum("tc,te->ce", attn_out, grad_proj, preferred_element_type=f32)
-    grad_attn = jnp.einsum("te,ce->tc", grad_proj, out_full, preferred_element_type=f32).astype(
-        bf16
-    )
-    grad_heads = grad_attn.reshape(tok_rows, HEADS, HEAD_DIM)
-    row_term = jnp.einsum("qhe,qhe->hq", grad_heads.astype(f32), attn_heads)
-
-    def step_block(dq_acc, inputs):
-        key_blk, value_blk, docs_blk = inputs
-
-        def step_used(acc):
-            probs, dscores = grad_block(
-                query_heads,
-                key_blk,
-                value_blk,
-                grad_heads,
-                query_docs,
-                docs_blk,
-                log_total,
-                row_term,
-            )
-            acc = (
-                acc
-                + jnp.einsum("hqk,khe->qhe", dscores, key_blk, preferred_element_type=f32) * scale
-            )
-            dk_blk = (
-                jnp.einsum("hqk,qhe->khe", dscores, query_heads, preferred_element_type=f32) * scale
-            )
-            dv_blk = jnp.einsum(
-                "hqk,qhe->khe", probs.astype(bf16), grad_heads, preferred_element_type=f32
-            )
-            return (acc, (dk_blk, dv_blk))
-
-        def step_skipped(acc):
-            zero_blk = jnp.zeros((key_blk.shape[0], HEADS, HEAD_DIM), f32)
-            return (acc, (zero_blk, zero_blk))
-
-        return lax.cond(docs_meet(query_docs, docs_blk), step_used, step_skipped, dq_acc)
-
-    dq_heads, key_terms = lax.scan(
-        step_block,
-        jnp.zeros((tok_rows, HEADS, HEAD_DIM), f32),
-        (key_blocks, value_blocks, key_docs),
-    )
-    dk_local, dv_local = scatter_sums(
-        [term.reshape(seq_len, width).astype(bf16) for term in key_terms],
-        [((0, 0, width, True), (1, 0, width, False))],
-        False,
-        3,
-        bf16,
-    )
-    grad_qkv_low = jnp.concatenate(
-        [
-            dq_heads.reshape(tok_rows, width).astype(bf16),
-            dk_local,
-            dv_local,
-        ],
-        axis=1,
-    )
+    dq_heads, dkv_heads = attend_back(
+        bounds, q_heads, kv_heads, g_heads, exact_heads, log_heads, spans
+    )
+    grad_qkv_low = collect_heads(dq_heads, dkv_heads, 3)
     grad_qkv = jnp.einsum("tc,tg->cg", attn_in, grad_qkv_low, preferred_element_type=f32)
     grad_attn_in = jnp.einsum("tg,cg->tc", grad_qkv_low, qkv_full, preferred_element_type=f32)
     _, attn_norm_back = jax.vjp(normed, token_in, attn_gain_f)

time: 758 us -> 560 us (0.74)
  local copies, waits for them, and re-layouts: 130 us -> 40 us
  blocking collectives: 58.1 us -> 18.5 us
  matrix products: 80.5 us -> 55.8 us
  loops' own time: 21.2 us -> 0 us
  other arithmetic: 47.2 us -> 38.2 us
  Pallas kernels: 395 us -> 387 us
    pallas_call x0 -> x6, Pallas kernels: none -> 109 us  [the longest x1 21.1 us: collect_heads(): pl.pallas_call(collect_kernel, out_shape=jax.ShapeDtypeStruct((rows, 3 *...]
    pallas_call x3 -> x2, Pallas kernels: 206 us -> 127 us  [scatter_sums(): pl.pallas_call(functools.partial(scatter_kernel, slots, count, over_wsh),...]
    pallas_call x3 -> x2, Pallas kernels: 162 us -> 124 us  [gather_all(): pl.pallas_call(functools.partial(gather_kernel, slots, count, over_wsh),...]
    psum x2 -> x0, blocking collectives: 33.8 us -> none  [the longest x1 21.2 us: body(): lax.psum((jnp.sum(proj * proj), jnp.sum(token_in * proj), jnp.sum(token_i...]
    convert_element_type x6 -> x0, local copies, waits for them, and re-layouts: 31.4 us -> none  [the longest x4 28.4 us: body(): term.reshape(seq_len, width).astype(bf16)]
    another operation x10 -> x0, loops' own time: 21.2 us -> none  [the longest x1 10.5 us: body(): lax.scan(forward_block, start_carry, (key_blocks, value_blocks, key_docs))]
    dot_general x9 -> x0, matrix products: 18.3 us -> none  [the longest x2 4.5 us: score_block(): jnp.einsum('qhe,khe->hqk', query_blk, key_blk, preferred_element_type=jnp...]
    slice x18 -> x0, local copies, waits for them, and re-layouts: 16.1 us -> none  [the longest x8 7.61 us: docs_meet(): first_docs[-1]]
  transfers between devices with their start and end apart: 4 -> 4, of which waited for: 1 -> 0; matrix products, arithmetic and copies ran while one was open for 9% -> 5% of each run, Pallas kernels for 31% -> 39%
where the time goes in v3:
time: 560 us; the launch traced here: 551 us
  Pallas kernels  387 us (69%)
  matrix products  55.8 us (10%)
  local copies, waits for them, and re-layouts  40 us (7%)
  other arithmetic  38.2 us (7%)
  blocking collectives  18.5 us (3%)
  starting transfers between devices  9.01 us (2%)
    pallas_call x2, Pallas kernels, scatter_sums(): pl.pallas_call(functools.partial(scatter_kernel, slots, count, over_wsh),...  127 us
    pallas_call x2, Pallas kernels, gather_all(): pl.pallas_call(functools.partial(gather_kernel, slots, count, over_wsh),...  124 us
    pallas_call x2, Pallas kernels, scan_both(): pl.pallas_call(functools.partial(scan_kernel, forward_first), out_shape=(...  27.3 us
    unnamed x193, local copies, waits for them, and re-layouts  24.3 us
    pallas_call x1, Pallas kernels, collect_heads(): pl.pallas_call(collect_kernel, out_shape=jax.ShapeDtypeStruct((rows, 3 *...  21.1 us
    pallas_call x1, Pallas kernels, attend_back(): pl.pallas_call(attend_back_kernel, out_shape=(jax.ShapeDtypeStruct(q.shap...  19.9 us
    pallas_call x1, Pallas kernels, spread_heads(): pl.pallas_call(spread_kernel, out_shape=(jax.ShapeDtypeStruct((HEAD_GROUP...  19.2 us
    all_gather x2, blocking collectives, carried(): pieces = lax.all_gather(totals[:2], 'ctx')  18.5 us
  transfers between devices with their start and end apart: 4, of which 0 were waited for; matrix products, arithmetic and copies ran while one was open for 5% of the time, Pallas kernels for 39%

profile of v3, /device:TPU:0, one launch (start us, length us, event | category | flops | bytes accessed | tf_op | source)
XLA Modules:
  0.0 550.6 jit_solution(6146380006018555176)
XLA Ops:
  9.0 42.5 %gather_all.2 = (bf16[2,2,2,4,24,1536]{5,4,3,2,1,0:T(8,128)(2,1)S(1)}, bf16[2,2,2,4,24,2432]{5,4,3,2,1,0:T(8,128)(2,1)S(1)}) custom-call(bf16[24,1536]{1,0:T(8,128)(2,1)S(1)} %copy-done.18, bf16[24,2432]{1,0:T(8,128)(2,1)S(1)} %fusion.105.refs_1_), custom_call_target="tpu_custom_call" | custom-call | tf_op jit(solution)/shard_map/gather_all/pallas_call | solution.py:146
  54.6 4.2 fusion.27
  62.0 13.6 %scan_both.2 = (f32[1024,768]{1,0:T(8,128)S(1)}, f32[1024,768]{1,0:T(8,128)S(1)}, f32[8,768]{1,0:T(8,128)S(1)}) custom-call(f32[1024,768]{1,0:T(8,128)S(1)} %pad_maximum_fusion.2.a_ref, f32[1024,768]{1,0:T(8,128)S(1)} %pad_maximum_fusion.3.b_ref), custom_call_target="tpu_custom_call" | custom-call | flops 6291456 | bytes 12582912 | tf_op jit(solution)/shard_map/scan_both/pallas_call | solution.py:1021
  75.7 9.7 %all-gather.2 = f32[8,2,768]{2,1,0:T(2,128)S(1)} all-gather(f32[1,2,768]{2,1,0:T(2,128)S(1)} %slice_bitcast_fusion), channel_id=2, replica_groups=mesh['ctx'=8,'wsh'=4] {'ctx'}, dimensions={0}, use_global_device_ids=true | all-gather | bytes 55296 | tf_op jit(solution)/shard_map/all_gather | solution.py:1037
  90.2 2.8 collective-permute-start
  104.1 19.2 %spread_heads.1 = (bf16[4,256,192]{2,1,0:T(8,128)(2,1)S(1)}, bf16[8,256,384]{2,1,0:T(8,128)(2,1)S(1)}) custom-call(bf16[256,2304]{1,0:T(8,128)(2,1)S(1)} %convolution_convert_fusion.3.qkv_ref), custom_call_target="tpu_custom_call" | custom-call | tf_op jit(solution)/shard_map/spread_heads/pallas_call | solution.py:459
  123.4 81.0 %gather_all.3 = (bf16[2,2,2,4,24,2304]{5,4,3,2,1,0:T(8,128)(2,1)S(1)}, bf16[2,2,2,4,24,768]{5,4,3,2,1,0:T(8,128)(2,1)S(1)}, bf16[2,2,2,4,24,768]{5,4,3,2,1,0:T(8...) custom-call(bf16[24,2304]{1,0:T(8,128)(2,1)S(1)} %copy-done.17, ...), custom_call_target="tpu_custom_call" | custom-call | tf_op jit(solution)/shard_map/gather_all/pallas_call | solution.py:146
  205.4 2.2 copy-done.24
  207.6 2.1 copy-done.25
  213.1 16.9 %attend.1 = (bf16[4,256,192]{2,1,0:T(8,128)(2,1)S(1)}, f32[4,256,192]{2,1,0:T(8,128)S(1)}, f32[4,8,256]{2,1,0:T(8,128)S(1)}) custom-call(s32[4,2]{1,0:T(4,128)S(1)} %pad_add_fusion.bounds, bf16[4,256,192]{2,1,0:T(8,128)(2,1)S(1)} %get-tuple-element.49.q_ref, bf16[8,256,384]{2,1,0:T(8,128)(2,1)S(1)} %get-tuple-element.50.kv_ref, ...), custom_call_target="tpu_custom_call" | custom-call | tf_op jit(solution)/shard_map/attend/pallas_call | solution.py:634
  231.0 17.8 %join_heads.1 = (bf16[256,768]{1,0:T(8,128)(2,1)S(1)}, f32[256,768]{1,0:T(8,128)S(1)}, f32[256,768]{1,0:T(8,128)S(1)}, f32[8,128]{1,0:T(8,128)S(1)}) custom-call(bf16[4,256,192]{2,1,0:T(8,128)(2,1)S(1)} %get-tuple-element.51.o_ref, bf16[256,768]{1,0:T(8,128)(2,1)S(1)} %bitcast.600, bf16[768,768]{1,0:T(8,128)(2,1)S(1)} %bitcast.604), custom_call_target="tpu_custom_call" | custom-call | tf_op jit(solution)/shard_map/join_heads/pallas_call | solution.py:760
  250.9 4.0 select_maximum_fusion.a_ref
  257.4 2.9 multiply_convert_fusion.3
  260.3 9.3 %multiply_convert_fusion = (bf16[256,3072]{1,0:T(8,128)(2,1)S(1)}, f32[256,3072]{1,0:T(8,128)S(1)}, f32[256,3072]{1,0:T(8,128)S(1)}) fusion(bf16[256,768]{1,0:T(8,128)(2,1)S(1)} %get-tuple-element.106, bf16[768,3072]{1,0:T(8,128)(2,1)S(1)} %bitcast.622), kind=kOutput, calls=%fused_computation.42 | convolution fusion | flops 1259077632 | bytes 12976128 | tf_op jit(solution)/shard_map/dot_general | solution.py:1209
  278.7 3.6 convolution_convert_fusion
  284.4 3.7 convolution_convert_fusion.1
  289.5 13.9 %part_heads.1 = (f32[256,768]{1,0:T(8,128)S(1)}, bf16[256,768]{1,0:T(8,128)(2,1)S(1)}, bf16[4,256,192]{2,1,0:T(8,128)(2,1)S(1)}) custom-call(f32[256,768]{1,0:T(8,128)S(1)} %add_add_fusion.3.resid_grad_ref, f32[256,768]{1,0:T(8,128)S(1)} %copy-done.12, bf16[256,768]{1,0:T(8,128)(2,1)S(1)} %bitcast.601, bf16[768,768]{1,0:T(8,128)(2,1)S(1)} %bitcast.605, ...), custom_call_target="tpu_custom_call" | custom-call | tf_op jit(solution)/shard_map/part_heads/pallas_call | solution.py:848
  303.4 19.9 %attend_back.1 = (bf16[4,256,192]{2,1,0:T(8,128)(2,1)S(1)}, bf16[8,256,384]{2,1,0:T(8,128)(2,1)S(1)}) custom-call(s32[4,2]{1,0:T(4,128)S(1)} %pad_add_fusion.bounds, bf16[4,256,192]{2,1,0:T(8,128)(2,1)S(1)} %get-tuple-element.49.q_ref, bf16[8,256,384]{2,1,0:T(8,128)(2,1)S(1)} %get-tuple-element.50.kv_ref, bf16[4,256,192]{2,1,0:T(8,128)(2,1)S(1)} %get-tuple-element.65.g_ref, ...), custom_call_target="tpu_custom_call" | custom-call | tf_op jit(solution)/shard_map/attend_back/pallas_call | solution.py:660
  323.4 21.1 %collect_heads.1 = bf16[256,2304]{1,0:T(8,128)(2,1)S(1)} custom-call(bf16[4,256,192]{2,1,0:T(8,128)(2,1)S(1)} %get-tuple-element.68.dq_ref, bf16[4,2,256,384]{3,2,1,0:T(8,128)(2,1)S(1)} %bitcast.606), custom_call_target="tpu_custom_call" | custom-call | tf_op jit(solution)/shard_map/collect_heads/pallas_call | solution.py:945
  348.9 3.0 collective-permute-start.3
  352.0 2.9 convolution_convert_fusion.2
  362.0 79.4 %scatter_sums.3 = (f32[96,768]{1,0:T(8,128)}, f32[24,3072]{1,0:T(8,128)}, f32[24,768]{1,0:T(8,128)}, f32[24,2304]{1,0:T(8,128)}) custom-call(bf16[2,2,2,4,96,768]{5,4,3,2,1,0:T(8,128)(2,1)} %bitcast.626, bf16[2,2,2,4,24,3072]{5,4,3,2,1,0:T(8,128)(2,1)} %bitcast.627, bf16[2,2,2,4,24,768]{5,4,3,2,1,0:T(8,128)(2,1)} %bitcast.631, ...), custom_call_target="tpu_custom_call" | custom-call | tf_op jit(solution)/shard_map/scatter_sums/pallas_call | solution.py:341
  442.6 5.2 gather_fusion
  447.9 2.4 convert_add_fusion.1.b_ref
  450.7 13.6 %scan_both.3 = (f32[1024,768]{1,0:T(8,128)S(1)}, f32[1024,768]{1,0:T(8,128)S(1)}, f32[8,768]{1,0:T(8,128)S(1)}) custom-call(f32[1024,768]{1,0:T(8,128)S(1)} %copy-done.1, f32[1024,768]{1,0:T(8,128)S(1)} %convert_add_fusion.1.b_ref), custom_call_target="tpu_custom_call" | custom-call | flops 6291456 | bytes 12582912 | tf_op jit(solution)/shard_map/scan_both/pallas_call | solution.py:1021
  464.4 8.8 %all-gather.3 = f32[8,2,768]{2,1,0:T(2,128)S(1)} all-gather(f32[1,2,768]{2,1,0:T(2,128)S(1)} %multiply_bitcast_fusion), channel_id=3, replica_groups=mesh['ctx'=8,'wsh'=4] {'ctx'}, dimensions={0}, use_global_device_ids=true | all-gather | bytes 55296 | tf_op jit(solution)/shard_map/all_gather | solution.py:1037
  476.4 3.0 fusion.44
  479.5 2.9 fusion.12
  482.4 4.4 convolution_convert_fusion.4
  488.8 4.1 pad_maximum_fusion.refs_2_
  493.0 47.7 %scatter_sums.2 = (f32[24,1536]{1,0:T(8,128)}, f32[24,768]{1,0:T(8,128)}, f32[24,2432]{1,0:T(8,128)}) custom-call(bf16[2,2,2,4,24,1536]{5,4,3,2,1,0:T(8,128)(2,1)} %bitcast.636, bf16[2,2,2,4,24,768]{5,4,3,2,1,0:T(8,128)(2,1)} %bitcast.632, bf16[2,2,2,4,24,2432]{5,4,3,2,1,0:T(8,128)(2,1)} %pad_maximum_fusion.refs_2_), custom_call_target="tpu_custom_call" | custom-call | tf_op jit(solution)/shard_map/scatter_sums/pallas_call | solution.py:341
  543.9 2.2 fusion.30
  (300 shorter events, 78.0 us)
Async XLA Ops:
  0.6 53.7 %copy-start.52 = (s32[1,1,1024]{2,1,0:T(1,128)S(1)}, s32[1,1,1024]{2,1,0:T(1,128)}, u32[]{:S(2)}) copy-start(s32[1,1,1024]{2,1,0:T(1,128)} %param.18) | copy-start | bytes 12292
  0.7 8.2 %copy-start.82 = (bf16[24]{0:T(256)(128)(2,1)S(1)}, bf16[24]{0:T(256)(128)(2,1)}, u32[]{:S(2)}) copy-start(bf16[24]{0:T(256)(128)(2,1)} %param.26) | copy-start | bytes 148
  0.7 8.3 %copy-start.54 = (bf16[24,2304]{1,0:T(8,128)(2,1)S(1)}, bf16[24,2304]{1,0:T(8,128)(2,1)}, u32[]{:S(2)}) copy-start(bf16[24,2304]{1,0:T(8,128)(2,1)} %param.21) | copy-start | bytes 331780
  0.7 8.3 %copy-start.18 = (bf16[24,1536]{1,0:T(8,128)(2,1)S(1)}, bf16[24,1536]{1,0:T(8,128)(2,1)}, u32[]{:S(2)}) copy-start(bf16[24,1536]{1,0:T(8,128)(2,1)} %refs_0_.2) | copy-start | bytes 221188
  8.8 44.7 %copy-start.65 = (f32[1024]{0:T(1024)}, f32[1024]{0:T(1024)S(1)}, u32[]{:S(2)}) copy-start(f32[1024]{0:T(1024)S(1)} %fusion.11) | copy-start | bytes 12292
  8.9 49.9 %copy-start.59 = (f32[1024]{0:T(1024)}, f32[1024]{0:T(1024)S(1)}, u32[]{:S(2)}) copy-start(f32[1024]{0:T(1024)S(1)} %fusion.108) | copy-start | bytes 12292
  61.5 36.1 %copy-start.33 = (f32[1024,384]{1,0:T(8,128)}, f32[1024,384]{1,0:T(8,128)S(1)}, u32[]{:S(2)}) copy-start(f32[1024,384]{1,0:T(8,128)S(1)} %get-tuple-element.114) | copy-start | bytes 4718596
  62.0 23.4 %copy-start.28 = (bf16[1,1024,768]{2,1,0:T(8,128)(2,1)S(1)}, bf16[1,1024,768]{2,1,0:T(8,128)(2,1)}, u32[]{:S(2)}) copy-start(bf16[1,1024,768]{2,1,0:T(8,128)(2,1)} %param.17) | copy-start | bytes 4718596
  89.6 8.7 %copy-start.38 = (bf16[256,768]{1,0:T(8,128)(2,1)}, bf16[256,768]{1,0:T(8,128)(2,1)S(1)}, u32[]{:S(2)}) copy-start(bf16[256,768]{1,0:T(8,128)(2,1)S(1)} %fusion.63) | copy-start | bytes 1179652
  90.2 167.1 %collective-permute-start = (bf16[1,768]{1,0:T(2,128)(2,1)}, bf16[1,768]{1,0:T(2,128)(2,1)}, u32[]{:S(2)}, u32[]{:S(2)}) collective-permute-start(bf16[1,768]{1,0:T(2,128)(2,1)} %get-tuple-element.122), channel_id=1, source_target_pairs={{0,4},{4,8},{8,12},{12,16},{16,20},{20,24},{24,28},{1,5},{5,9},{9,... | collective-permute-start | bytes 4616 | tf_op jit(solution)/shard_map/ppermute | solution.py:1063
  93.0 163.0 %collective-permute-start.1 = (bf16[1,768]{1,0:T(2,128)(2,1)}, bf16[1,768]{1,0:T(2,128)(2,1)}, u32[]{:S(2)}, u32[]{:S(2)}) collective-permute-start(bf16[1,768]{1,0:T(2,128)(2,1)} %get-tuple-element.123), channel_id=1, source_target_pairs={{4,0},{8,4},{12,8},{16,12},{20,16},{24,20},{28,24},{5,1},{9,5},{13... | collective-permute-start | bytes 4616 | tf_op jit(solution)/shard_map/ppermute | solution.py:1065
  102.9 20.4 %copy-start.15 = (bf16[24,3072]{1,0:T(8,128)(2,1)S(1)}, bf16[24,3072]{1,0:T(8,128)(2,1)}, u32[]{:S(2)}) copy-start(bf16[24,3072]{1,0:T(8,128)(2,1)} %refs_3_.1) | copy-start | bytes 442372
  102.9 20.4 %copy-start.16 = (bf16[96,768]{1,0:T(8,128)(2,1)S(1)}, bf16[96,768]{1,0:T(8,128)(2,1)}, u32[]{:S(2)}) copy-start(bf16[96,768]{1,0:T(8,128)(2,1)} %refs_4_.1) | copy-start | bytes 442372
  102.9 20.4 %copy-start.17 = (bf16[24,2304]{1,0:T(8,128)(2,1)S(1)}, bf16[24,2304]{1,0:T(8,128)(2,1)}, u32[]{:S(2)}) copy-start(bf16[24,2304]{1,0:T(8,128)(2,1)} %refs_0_.3) | copy-start | bytes 331780
  102.9 20.4 %copy-start.19 = (bf16[24,768]{1,0:T(8,128)(2,1)S(1)}, bf16[24,768]{1,0:T(8,128)(2,1)}, u32[]{:S(2)}) copy-start(bf16[24,768]{1,0:T(8,128)(2,1)} %refs_1_.1) | copy-start | bytes 110596
  102.9 20.4 %copy-start.20 = (bf16[24,768]{1,0:T(8,128)(2,1)S(1)}, bf16[24,768]{1,0:T(8,128)(2,1)}, u32[]{:S(2)}) copy-start(bf16[24,768]{1,0:T(8,128)(2,1)} %refs_2_.1) | copy-start | bytes 110596
  102.9 108.6 %copy-start.39 = (bf16[256,768]{1,0:T(8,128)(2,1)S(1)}, bf16[256,768]{1,0:T(8,128)(2,1)}, u32[]{:S(2)}) copy-start(bf16[256,768]{1,0:T(8,128)(2,1)} %copy-done.38) | copy-start | bytes 1179652
  209.8 39.0 %copy-start.4 = (bf16[2,2,2,4,24,768]{5,4,3,2,1,0:T(8,128)(2,1)}, bf16[2,2,2,4,24,768]{5,4,3,2,1,0:T(8,128)(2,1)S(1)}, u32[]{:S(2)}) copy-start(bf16[2,2,2,4,24,768]{5,4,3,2,1,0:T(8,128)(2,1)S(1)} %get-tuple-element.52) | copy-start | bytes 3538948
  257.4 12.3 %slice-start = ((s8[4718592]{0:T(1024)(128)(4,1)}), s8[4194304]{0:T(1024)(128)(4,1)S(1)}, s32[]{:S(2)}) async-start(s8[4718592]{0:T(1024)(128)(4,1)} %bitcast.616), calls=%async_computation | async-start | bytes 8388608
  260.3 9.4 %slice-start.1 = ((s8[4718592]{0:T(1024)(128)(4,1)}), s8[524288]{0:T(1024)(128)(4,1)S(1)}, s32[]{:S(2)}) async-start(s8[4718592]{0:T(1024)(128)(4,1)} %bitcast.616), calls=%async_computation.1 | async-start | bytes 1048576
  260.3 9.4 %copy-start.46 = (bf16[1,256,768]{2,1,0:T(8,128)(2,1)S(1)}, bf16[1,256,768]{2,1,0:T(8,128)(2,1)}, u32[]{:S(2)}) copy-start(bf16[1,256,768]{2,1,0:T(8,128)(2,1)} %param.30) | copy-start | bytes 1179652
  288.4 15.0 %copy-start.10 = (f32[4,256,192]{2,1,0:T(8,128)S(1)}, f32[4,256,192]{2,1,0:T(8,128)}, u32[]{:S(2)}) copy-start(f32[4,256,192]{2,1,0:T(8,128)} %copy-done.9) | copy-start | bytes 2359300
  303.4 41.1 %copy-start.23 = (bf16[2,2,2,4,24,2432]{5,4,3,2,1,0:T(8,128)(2,1)S(1)}, bf16[2,2,2,4,24,2432]{5,4,3,2,1,0:T(8,128)(2,1)}, u32[]{:S(2)}) copy-start(bf16[2,2,2,4,24,2432]{5,4,3,2,1,0:T(8,128)(2,1)} %copy-done.21) | copy-start | bytes 11206660
  347.5 94.5 %collective-permute-start.2 = (bf16[1,768]{1,0:T(2,128)(2,1)S(1)}, bf16[1,768]{1,0:T(2,128)(2,1)S(1)}, u32[]{:S(2)}, u32[]{:S(2)}) collective-permute-start(bf16[1,768]{1,0:T(2,128)(2,1)S(1)} %get-tuple-element.120), channel_id=1, source_target_pairs={{4,0},{8,4},{12,8},{16,12},{20,16},{24,20},{28,24},{5,1},{9,5},{13... | collective-permute-start | bytes 4616 | tf_op jit(solution)/shard_map/ppermute | solution.py:1065
  348.9 92.6 %collective-permute-start.3 = (bf16[1,768]{1,0:T(2,128)(2,1)S(1)}, bf16[1,768]{1,0:T(2,128)(2,1)S(1)}, u32[]{:S(2)}, u32[]{:S(2)}) collective-permute-start(bf16[1,768]{1,0:T(2,128)(2,1)S(1)} %get-tuple-element.121), channel_id=1, source_target_pairs={{0,4},{4,8},{8,12},{12,16},{16,20},{20,24},{24,28},{1,5},{5,9},{9,... | collective-permute-start | bytes 4616 | tf_op jit(solution)/shard_map/ppermute | solution.py:1063
  362.0 79.5 %copy-start.8 = (bf16[2,2,2,4,24,2304]{5,4,3,2,1,0:T(8,128)(2,1)S(1)}, bf16[2,2,2,4,24,2304]{5,4,3,2,1,0:T(8,128)(2,1)}, u32[]{:S(2)}) copy-start(bf16[2,2,2,4,24,2304]{5,4,3,2,1,0:T(8,128)(2,1)} %copy-done.6) | copy-start | bytes 10616836
  362.0 80.0 %copy-start.47 = (f32[256,768]{1,0:T(8,128)S(1)}, f32[256,768]{1,0:T(8,128)}, u32[]{:S(2)}) copy-start(f32[256,768]{1,0:T(8,128)} %fusion.74) | copy-start | bytes 2359300
  362.0 80.0 %copy-start.81 = (f32[256]{0:T(256)S(1)}, f32[256]{0:T(256)}, u32[]{:S(2)}) copy-start(f32[256]{0:T(256)} %sqrt.7) | copy-start | bytes 3076
  450.7 13.6 %copy-start.71 = (f32[768]{0:T(1024)S(1)}, f32[768]{0:T(1024)}, u32[]{:S(2)}) copy-start(f32[768]{0:T(1024)} %pad_maximum_fusion.18) | copy-start | bytes 9220
  450.7 23.0 %slice-start.4 = ((s8[6291456]{0:T(1024)(128)(4,1)}), s8[2097152]{0:T(1024)(128)(4,1)S(1)}, s32[]{:S(2)}) async-start(s8[6291456]{0:T(1024)(128)(4,1)} %bitcast.628), calls=%async_computation.4 | async-start | bytes 4194304
  493.0 50.9 %copy-start.35 = (f32[1024,768]{1,0:T(8,128)S(1)}, f32[1024,768]{1,0:T(8,128)}, u32[]{:S(2)}) copy-start(f32[1024,768]{1,0:T(8,128)} %copy-done.34) | copy-start | bytes 9437188
  493.0 50.9 %copy-start.63 = (f32[768]{0:T(1024)S(1)}, f32[768]{0:T(1024)}, u32[]{:S(2)}) copy-start(f32[768]{0:T(1024)} %copy-done.61) | copy-start | bytes 9220
  (64 other events, 215.3 us)

commit v4 on v3

--- a/solution.py
+++ b/solution.py
@@ -69,14 +69,39 @@
     )
 
 
-def gather_kernel(slots, count, over_wsh, *refs):
-    shards, outs = refs[:count], refs[count : 2 * count]
-    sems, local_sems = refs[2 * count : 2 * count + 2], refs[2 * count + 2]
+LAG = 2
+FRONT_SHARE = 0.75
+BACK_SHARE = 0.85
+SLOT_ELEMENTS = 24 * 512
+
+
+def wavefront(slots, steps, move):
+    moves = []
+    for tick in range(1, len(slots) + steps * LAG):
+        for number in range(len(slots) - 1, -1, -1):
+            step, off = divmod(tick - number - 1, LAG)
+            if off == 0 and 0 <= step < steps:
+                moves.append(functools.partial(move, slots[number], step + 1))
+    return moves
+
+
+def weave(ticks, pieces, share):
+    ticks = list(ticks)
+    total = len(ticks)
+    ticks.pop(0)()
+    for number, piece in enumerate(pieces):
+        piece()
+        while total - len(ticks) < share * total * (number + 1) / len(pieces) and ticks:
+            ticks.pop(0)()
+    for tick in ticks:
+        tick()
+
+
+def gather_ticks(slots, shards, outs, sems, local_sems, over_wsh):
     width_w = lax.axis_size("wsh") if over_wsh else 1
     mine_w = lax.axis_index("wsh") if over_wsh else 0
     bits = len(masks_of("ctx"))
     per_stream = width_w - 1 + bits
-    greet(over_wsh)
     streams = [stream for slot in slots for stream in slot]
     number_of = {stream: position for position, stream in enumerate(streams)}
     started = {}
@@ -123,39 +148,61 @@
             else:
                 copy.wait_recv()
 
-    for tick in range(len(slots) + bits + 1):
-        for number, slot in reversed(list(enumerate(slots))):
-            step = tick - number
-            for stream in slot:
-                if 1 <= step <= bits + 1:
-                    finish(stream, step - 1)
-                if 0 <= step <= bits:
-                    start(stream, step)
-    for (stream, step), copies in started.items():
-        for copy in copies[1:] if step == 0 else copies:
-            copy.wait_send()
-
-
-def gather_all(arrays, slots, over_wsh, collective):
+    def first():
+        for stream in streams:
+            start(stream, 0)
+
+    def move(slot, step):
+        for stream in slot:
+            finish(stream, step - 1)
+            if step <= bits:
+                start(stream, step)
+
+    def drain():
+        for (stream, step), copies in started.items():
+            for copy in copies[1:] if step == 0 else copies:
+                copy.wait_send()
+
+    return [first] + wavefront(slots, bits + 1, move) + [drain]
+
+
+def gather_sems(slots, over_wsh):
     bits = len(masks_of("ctx"))
     width_w = lax.axis_size("wsh") if over_wsh else 1
-    count = len(arrays)
     streams = sum(len(slot) for slot in slots)
     copies = streams * (width_w - 1 + bits)
+    return [
+        pltpu.SemaphoreType.DMA((copies,)),
+        pltpu.SemaphoreType.DMA((copies,)),
+        pltpu.SemaphoreType.DMA((streams,)),
+    ]
+
+
+def gather_shapes(arrays, over_wsh):
+    bits = len(masks_of("ctx"))
+    width_w = lax.axis_size("wsh") if over_wsh else 1
+    return tuple(
+        jax.ShapeDtypeStruct((2,) * bits + (width_w,) + array.shape, array.dtype)
+        for array in arrays
+    )
+
+
+def gather_kernel(slots, count, over_wsh, *refs):
+    greet(over_wsh)
+    shards, outs, sems = refs[:count], refs[count : 2 * count], refs[2 * count :]
+    for tick in gather_ticks(slots, shards, outs, sems[:2], sems[2], over_wsh):
+        tick()
+
+
+def gather_all(arrays, slots, over_wsh, collective):
+    count = len(arrays)
     hbm = pl.BlockSpec(memory_space=pl.ANY)
     outs = pl.pallas_call(
         functools.partial(gather_kernel, slots, count, over_wsh),
-        out_shape=tuple(
-            jax.ShapeDtypeStruct((2,) * bits + (width_w,) + array.shape, array.dtype)
-            for array in arrays
-        ),
+        out_shape=gather_shapes(arrays, over_wsh),
         in_specs=[hbm] * count,
         out_specs=(hbm,) * count,
-        scratch_shapes=[
-            pltpu.SemaphoreType.DMA((copies,)),
-            pltpu.SemaphoreType.DMA((copies,)),
-            pltpu.SemaphoreType.DMA((streams,)),
-        ],
+        scratch_shapes=gather_sems(slots, over_wsh),
         compiler_params=pltpu.CompilerParams(
             collective_id=collective, has_side_effects=True, vmem_limit_bytes=4 << 20
         ),
@@ -189,12 +236,10 @@
     lax.fori_loop(0, steps, step, 0)
 
 
-def scatter_kernel(slots, count, over_wsh, *refs):
+def scatter_ticks(slots, grads, outs, scratch, over_wsh):
     streams = [stream for slot in slots for stream in slot]
-    grads, outs = refs[:count], refs[count : 2 * count]
     bits = len(masks_of("ctx"))
-    held = refs[2 * count : 3 * count]
-    rest = refs[3 * count :]
+    held, rest = scratch[: len(grads)], scratch[len(grads) :]
     per_stream_bufs = bits + (1 if over_wsh else 0)
     landing = {}
     for number, stream in enumerate(streams):
@@ -208,7 +253,6 @@
     every = {mask: ctx_bit(mask) for mask in masks_of("ctx")}
     low = masks_of("ctx")[0]
     started = {}
-    greet(over_wsh)
 
     def start(stream, step):
         array, first, cols, upward = stream
@@ -301,29 +345,40 @@
                 outs[array][down, span] = total.astype(outs[array].dtype)
 
     steps = bits + (1 if over_wsh else 0)
-    for tick in range(len(slots) + steps):
-        for number, slot in reversed(list(enumerate(slots))):
-            step = tick - number
-            for stream in slot:
-                if 1 <= step <= steps:
-                    finish(stream, step - 1)
-                if 0 <= step < steps:
-                    start(stream, step)
-    for (stream, step), copies in started.items():
-        for copy in copies[1:] if step == 0 else copies:
-            copy.wait_send()
-
-
-def scatter_sums(arrays, slots, over_wsh, collective, dtype):
+
+    def first():
+        for stream in streams:
+            start(stream, 0)
+
+    def move(slot, step):
+        for stream in slot:
+            finish(stream, step - 1)
+            if step < steps:
+                start(stream, step)
+
+    def drain():
+        for (stream, step), copies in started.items():
+            for copy in copies[1:] if step == 0 else copies:
+                copy.wait_send()
+
+    return [first] + wavefront(slots, steps, move) + [drain]
+
+
+def scatter_shapes(arrays, over_wsh):
     bits = len(masks_of("ctx"))
     width_w = lax.axis_size("wsh") if over_wsh else 1
-    count = len(arrays)
-    parts = width_w << bits
-    rows = [array.shape[0] // parts for array in arrays]
+    rows = [array.shape[0] // (width_w << bits) for array in arrays]
     shaped = [
         array.reshape((2,) * bits + (width_w, row, array.shape[1]))
         for array, row in zip(arrays, rows)
     ]
+    return shaped, rows
+
+
+def scatter_scratch(arrays, slots, over_wsh):
+    bits = len(masks_of("ctx"))
+    width_w = lax.axis_size("wsh") if over_wsh else 1
+    rows = [array.shape[0] // (width_w << bits) for array in arrays]
     streams = [stream for slot in slots for stream in slot]
     copies = len(streams) * (width_w - 1 + bits)
     buffers = [
@@ -338,6 +393,23 @@
             )
         if over_wsh:
             buffers.append(pltpu.VMEM((width_w - 1, rows[array], cols), kind))
+    return buffers + [
+        pltpu.SemaphoreType.DMA((copies,)),
+        pltpu.SemaphoreType.DMA((copies,)),
+        pltpu.SemaphoreType.DMA((len(streams),)),
+    ]
+
+
+def scatter_kernel(slots, count, over_wsh, *refs):
+    greet(over_wsh)
+    grads, outs, scratch = refs[:count], refs[count : 2 * count], refs[2 * count :]
+    for tick in scatter_ticks(slots, grads, outs, scratch, over_wsh):
+        tick()
+
+
+def scatter_sums(arrays, slots, over_wsh, collective, dtype):
+    count = len(arrays)
+    shaped, rows = scatter_shapes(arrays, over_wsh)
     return pl.pallas_call(
         functools.partial(scatter_kernel, slots, count, over_wsh),
         out_shape=tuple(
@@ -345,12 +417,7 @@
         ),
         in_specs=[pl.BlockSpec(memory_space=pl.ANY)] * count,
         out_specs=(pl.BlockSpec(memory_space=pltpu.VMEM),) * count,
-        scratch_shapes=buffers
-        + [
-            pltpu.SemaphoreType.DMA((copies,)),
-            pltpu.SemaphoreType.DMA((copies,)),
-            pltpu.SemaphoreType.DMA((len(streams),)),
-        ],
+        scratch_shapes=scatter_scratch(arrays, slots, over_wsh),
         compiler_params=pltpu.CompilerParams(
             collective_id=collective, has_side_effects=True, vmem_limit_bytes=56 << 20
         ),
@@ -358,8 +425,10 @@
     )(*shaped)
 
 
-def halves(number, cols):
-    pieces = 2 if cols < 2304 else 4
+def halves(number, rows, cols):
+    pieces = 2 * max(1, rows * cols // SLOT_ELEMENTS)
+    while cols // pieces < 128:
+        pieces = pieces - 2
     cuts = [cols * piece // pieces // 128 * 128 for piece in range(pieces)] + [cols]
     streams = [
         (number, cuts[piece], cuts[piece + 1] - cuts[piece], piece % 2 == 0)
@@ -368,10 +437,14 @@
     return [tuple(streams[piece : piece + 2]) for piece in range(0, pieces, 2)]
 
 
-def slots_of(arrays):
-    return [
-        slot for number, part in enumerate(arrays) for slot in halves(number, part.shape[1])
-    ]
+def slots_of(arrays, shards):
+    slots = []
+    for number, part in enumerate(arrays):
+        rows = part.shape[0]
+        if not shards:
+            rows = rows // (lax.axis_size("ctx") * lax.axis_size("wsh"))
+        slots = slots + halves(number, rows, part.shape[1])
+    return slots
 
 
 HEAD_GROUPS = 4
@@ -396,86 +469,72 @@
     pl.semaphore_wait(barrier, len(gaps))
 
 
-def spread_kernel(qkv_ref, q_out, kv_out, send_q, send_kv, send_sem, recv_sem, local_sem):
+def spread_ticks(qkv_ref, q_out, kv_out, send_q, send_kv, send_sem, recv_sem, local_sem):
     apart, group, inner = groups()
     width = qkv_ref.shape[1] // 3
     cols = width // HEAD_GROUPS
     mine = lax.axis_index("ctx")
     sems = (send_sem, recv_sem)
-    gaps = [gap * apart for gap in range(1, HEAD_GROUPS)] + list(range(1, apart))
-    for other in range(HEAD_GROUPS):
-        send_q[other] = qkv_ref[:, other * cols : (other + 1) * cols]
-        for part in range(2):
-            first = (part + 1) * width + other * cols
-            send_kv[other, :, part * cols : (part + 1) * cols] = qkv_ref[:, first : first + cols]
-    greet_ctx(gaps)
-    kv_copies, q_copies = [], []
-    for gap in range(1, HEAD_GROUPS):
-        other = lax.bitwise_xor(group, gap)
-        partner = ctx_partner(gap * apart)
-        copy = remote(send_kv.at[other], kv_out.at[mine], sems, gap - 1, partner)
-        copy.start()
-        kv_copies.append(copy)
-    for gap in range(1, HEAD_GROUPS):
-        other = lax.bitwise_xor(group, gap)
-        partner = ctx_partner(gap * apart)
-        copy = remote(send_q.at[other], q_out.at[group], sems, HEAD_GROUPS - 2 + gap, partner)
-        copy.start()
-        q_copies.append(copy)
-    own = [
-        pltpu.make_async_copy(send_kv.at[group], kv_out.at[mine], local_sem.at[0]),
-        pltpu.make_async_copy(send_q.at[group], q_out.at[group], local_sem.at[1]),
+    kv_copies, q_copies, own, passed = [], [], [], []
+
+    def send():
+        for other in range(HEAD_GROUPS):
+            send_q[other] = qkv_ref[:, other * cols : (other + 1) * cols]
+            for part in range(2):
+                first = (part + 1) * width + other * cols
+                send_kv[other, :, part * cols : (part + 1) * cols] = qkv_ref[
+                    :, first : first + cols
+                ]
+        for gap in range(1, HEAD_GROUPS):
+            other = lax.bitwise_xor(group, gap)
+            partner = ctx_partner(gap * apart)
+            kv_copies.append(
+                remote(send_kv.at[other], kv_out.at[mine], sems, gap - 1, partner)
+            )
+        for gap in range(1, HEAD_GROUPS):
+            other = lax.bitwise_xor(group, gap)
+            partner = ctx_partner(gap * apart)
+            q_copies.append(
+                remote(send_q.at[other], q_out.at[group], sems, HEAD_GROUPS - 2 + gap, partner)
+            )
+        own.append(pltpu.make_async_copy(send_kv.at[group], kv_out.at[mine], local_sem.at[0]))
+        own.append(pltpu.make_async_copy(send_q.at[group], q_out.at[group], local_sem.at[1]))
+        for copy in own + kv_copies + q_copies:
+            copy.start()
+
+    def pass_on():
+        own[0].wait()
+        number = 2 * (HEAD_GROUPS - 1)
+        for gap in range(HEAD_GROUPS):
+            if gap:
+                kv_copies[gap - 1].wait_recv()
+            slot = lax.bitwise_xor(mine, gap * apart)
+            for near in range(1, apart):
+                copy = remote(kv_out.at[slot], kv_out.at[slot], sems, number, ctx_partner(near))
+                copy.start()
+                passed.append(copy)
+                number = number + 1
+
+    def wait():
+        own[1].wait()
+        for copy in q_copies + passed:
+            copy.wait_recv()
+        for copy in kv_copies + q_copies + passed:
+            copy.wait_send()
+
+    return send, pass_on, wait
+
+
+def spread_scratch(rows, cols, dtype):
+    apart = lax.axis_size("ctx") // HEAD_GROUPS
+    copies = 2 * (HEAD_GROUPS - 1) + HEAD_GROUPS * (apart - 1)
+    return [
+        pltpu.VMEM((HEAD_GROUPS, rows, cols), dtype),
+        pltpu.VMEM((HEAD_GROUPS, rows, 2 * cols), dtype),
+        pltpu.SemaphoreType.DMA((copies,)),
+        pltpu.SemaphoreType.DMA((copies,)),
+        pltpu.SemaphoreType.DMA((2,)),
     ]
-    for copy in own:
-        copy.start()
-    own[0].wait()
-    number = 2 * (HEAD_GROUPS - 1)
-    passed = []
-    for gap in range(HEAD_GROUPS):
-        if gap:
-            kv_copies[gap - 1].wait_recv()
-        slot = lax.bitwise_xor(mine, gap * apart)
-        for near in range(1, apart):
-            copy = remote(kv_out.at[slot], kv_out.at[slot], sems, number, ctx_partner(near))
-            copy.start()
-            passed.append(copy)
-            number = number + 1
-    own[1].wait()
-    for copy in q_copies:
-        copy.wait_recv()
-    for copy in passed:
-        copy.wait_recv()
-    for copy in kv_copies + q_copies + passed:
-        copy.wait_send()
-
-
-def spread_heads(qkv, collective):
-    rows = qkv.shape[0]
-    count = lax.axis_size("ctx")
-    apart = count // HEAD_GROUPS
-    cols = qkv.shape[1] // 3 // HEAD_GROUPS
-    copies = 2 * (HEAD_GROUPS - 1) + HEAD_GROUPS * (apart - 1)
-    hbm = pl.BlockSpec(memory_space=pl.ANY)
-    return pl.pallas_call(
-        spread_kernel,
-        out_shape=(
-            jax.ShapeDtypeStruct((HEAD_GROUPS, rows, cols), qkv.dtype),
-            jax.ShapeDtypeStruct((count, rows, 2 * cols), qkv.dtype),
-        ),
-        in_specs=[pl.BlockSpec(memory_space=pltpu.VMEM)],
-        out_specs=(hbm, hbm),
-        scratch_shapes=[
-            pltpu.VMEM((HEAD_GROUPS, rows, cols), qkv.dtype),
-            pltpu.VMEM((HEAD_GROUPS, rows, 2 * cols), qkv.dtype),
-            pltpu.SemaphoreType.DMA((copies,)),
-            pltpu.SemaphoreType.DMA((copies,)),
-            pltpu.SemaphoreType.DMA((2,)),
-        ],
-        compiler_params=pltpu.CompilerParams(
-            collective_id=collective, has_side_effects=True, vmem_limit_bytes=16 << 20
-        ),
-        name="spread_heads",
-    )(qkv)
 
 
 def head_rows(value, head):
@@ -781,14 +840,16 @@
     )(o, tokens, weight)
 
 
-def part_kernel(
-    elements, resid_grad_ref, proj_ref, tokens_ref, weight_ref, stat_ref, stream_grad_ref, proj_grad_ref,
-    g_out, send, sums, send_sem, recv_sem, local_sem
-):
+def part_kernel(elements, slots, *refs):
+    grad_ref, resid_grad_ref, proj_ref, tokens_ref, weight_ref, stat_ref = refs[:6]
+    shard_ref, stream_grad_ref, proj_grad_ref, g_out = refs[6:10]
+    send, sums, send_sem, recv_sem, local_sem = refs[10:15]
     apart, group, inner = groups()
     cols = g_out.shape[2]
     sems = (send_sem, recv_sem)
-    greet_ctx(list(range(1, lax.axis_size("ctx"))))
+    ticks = scatter_ticks(slots, [grad_ref], [shard_ref], refs[15:], True)
+    greet_all()
+    ticks.pop(0)()
     mine = lax.axis_index("ctx")
     sq_proj, cross, sq_tok = stat_ref[0:1, 0:1], stat_ref[1:2, 0:1], stat_ref[2:3, 0:1]
     rms_scale = lax.rsqrt(sq_proj / elements + 1e-06)
@@ -802,6 +863,7 @@
         jnp.where(row == 1, summed(resid_grad_ref[...] * proj_ref[...]), 0.0),
     )
     small = exchange_sums(sums, sems, HEAD_GROUPS - 1)
+    ticks.pop(0)()
     for copy in small:
         copy.wait_recv()
     total = total_of(sums)
@@ -831,6 +893,8 @@
         copies.append(copy)
     own = pltpu.make_async_copy(send.at[group], g_out.at[group], local_sem.at[0])
     own.start()
+    for tick in ticks:
+        tick()
     own.wait()
     for copy in copies:
         copy.wait_recv()
@@ -838,235 +902,651 @@
         copy.wait_send()
 
 
-def part_heads(resid_grad, proj, tokens, weight, stat, elements, collective):
+def part_heads(grad, resid_grad, proj, tokens, weight, stat, elements, collective):
     rows, width = tokens.shape
     count = lax.axis_size("ctx")
     copies = HEAD_GROUPS - 1 + count - 1
     cols = width // HEAD_GROUPS
     whole = pl.BlockSpec(memory_space=pltpu.VMEM)
     f32, bf16 = jnp.float32, jnp.bfloat16
+    slots = slots_of([grad], False)
+    shaped, shard_rows = scatter_shapes([grad], True)
     return pl.pallas_call(
-        functools.partial(part_kernel, elements),
+        functools.partial(part_kernel, elements, slots),
         out_shape=(
+            jax.ShapeDtypeStruct((shard_rows[0], grad.shape[1]), f32),
             jax.ShapeDtypeStruct((rows, width), f32),
             jax.ShapeDtypeStruct((rows, width), bf16),
             jax.ShapeDtypeStruct((HEAD_GROUPS, rows, cols), bf16),
         ),
-        in_specs=[whole] * 5,
-        out_specs=(whole, whole, pl.BlockSpec(memory_space=pl.ANY)),
+        in_specs=[pl.BlockSpec(memory_space=pl.ANY)] + [whole] * 5,
+        out_specs=(whole, whole, whole, pl.BlockSpec(memory_space=pl.ANY)),
         scratch_shapes=[
             pltpu.VMEM((HEAD_GROUPS, rows, cols), bf16),
             pltpu.VMEM((count, 8, 128), f32),
             pltpu.SemaphoreType.DMA((copies,)),
             pltpu.SemaphoreType.DMA((copies,)),
             pltpu.SemaphoreType.DMA((1,)),
-        ],
+        ]
+        + scatter_scratch([grad], slots, True),
         compiler_params=pltpu.CompilerParams(
-            collective_id=collective, has_side_effects=True, vmem_limit_bytes=24 << 20
+            collective_id=collective, has_side_effects=True, vmem_limit_bytes=32 << 20
         ),
         name="part_heads",
-    )(resid_grad, proj, tokens, weight, stat)
-
-
-def collect_kernel(dq_ref, dkv_ref, out_ref, near_land, own_s, q_land, kv_land, send_sem, recv_sem, local_sem):
+    )(shaped[0], resid_grad, proj, tokens, weight, stat)
+
+
+def collect_ticks(dq_ref, dkv_ref, out_ref, scratch):
+    near_land, own_s, q_land, kv_land, send_sem, recv_sem, local_sem = scratch
     apart, group, inner = groups()
     cols = dq_ref.shape[2]
     rows = dq_ref.shape[1]
     width = cols * HEAD_GROUPS
     sems = (send_sem, recv_sem)
-    gaps = [gap * apart for gap in range(1, HEAD_GROUPS)] + list(range(1, apart))
-    greet_ctx(gaps)
-    number = 0
-    near = []
-    for gap in range(1, apart):
-        other = lax.bitwise_xor(inner, gap)
-        copy = remote(dkv_ref.at[:, other], near_land.at[gap - 1], sems, number, ctx_partner(gap))
-        copy.start()
-        near.append(copy)
-        number = number + 1
-    own = pltpu.make_async_copy(dkv_ref.at[:, inner], own_s, local_sem.at[0])
-    own.start()
-    own_q = pltpu.make_async_copy(dq_ref.at[group], q_land.at[group], local_sem.at[1])
-    own_q.start()
-    far_q = []
-    for gap in range(1, HEAD_GROUPS):
-        other = lax.bitwise_xor(group, gap)
-        copy = remote(dq_ref.at[other], q_land.at[group], sems, number, ctx_partner(gap * apart))
-        copy.start()
-        far_q.append(copy)
-        number = number + 1
-    own.wait()
-    for copy in near:
-        copy.wait_recv()
-    chunk = 32
-
-    def add(position, carry):
-        slot = lax.div(position, rows // chunk)
-        down = pl.ds(pl.multiple_of(lax.rem(position, rows // chunk) * chunk, chunk), chunk)
-        total = own_s[slot, down, :].astype(jnp.float32)
+    near, far_q, far_kv, own = [], [], [], []
+
+    def send():
+        number = 0
         for gap in range(1, apart):
-            total = total + near_land[gap - 1, slot, down, :].astype(jnp.float32)
-        own_s[slot, down, :] = total.astype(own_s.dtype)
-        return carry
-
-    lax.fori_loop(0, HEAD_GROUPS * (rows // chunk), add, 0)
-    own_kv = pltpu.make_async_copy(own_s.at[group], kv_land.at[group], local_sem.at[2])
-    own_kv.start()
-    far_kv = []
-    for gap in range(1, HEAD_GROUPS):
-        other = lax.bitwise_xor(group, gap)
-        copy = remote(own_s.at[other], kv_land.at[group], sems, number, ctx_partner(gap * apart))
-        copy.start()
-        far_kv.append(copy)
-        number = number + 1
-    own_q.wait()
-    for copy in far_q:
-        copy.wait_recv()
-    for other in range(HEAD_GROUPS):
-        out_ref[:, other * cols : (other + 1) * cols] = q_land[other]
-    own_kv.wait()
-    for copy in far_kv:
-        copy.wait_recv()
-    for other in range(HEAD_GROUPS):
-        for part in range(2):
-            first = (part + 1) * width + other * cols
-            out_ref[:, first : first + cols] = kv_land[other, :, part * cols : (part + 1) * cols]
-    for copy in near + far_q + far_kv:
-        copy.wait_send()
-
-
-def collect_heads(dq, dkv, collective):
-    slots, rows, cols = dq.shape
-    count = lax.axis_size("ctx")
-    apart = count // HEAD_GROUPS
+            other = lax.bitwise_xor(inner, gap)
+            near.append(
+                remote(dkv_ref.at[:, other], near_land.at[gap - 1], sems, number, ctx_partner(gap))
+            )
+            number = number + 1
+        own.append(pltpu.make_async_copy(dkv_ref.at[:, inner], own_s, local_sem.at[0]))
+        own.append(pltpu.make_async_copy(dq_ref.at[group], q_land.at[group], local_sem.at[1]))
+        for gap in range(1, HEAD_GROUPS):
+            other = lax.bitwise_xor(group, gap)
+            far_q.append(
+                remote(
+                    dq_ref.at[other], q_land.at[group], sems, number, ctx_partner(gap * apart)
+                )
+            )
+            number = number + 1
+        for copy in near + own + far_q:
+            copy.start()
+
+    def add_near():
+        own[0].wait()
+        for copy in near:
+            copy.wait_recv()
+        chunk = 32
+
+        def add(position, carry):
+            slot = lax.div(position, rows // chunk)
+            down = pl.ds(pl.multiple_of(lax.rem(position, rows // chunk) * chunk, chunk), chunk)
+            total = own_s[slot, down, :].astype(jnp.float32)
+            for gap in range(1, apart):
+                total = total + near_land[gap - 1, slot, down, :].astype(jnp.float32)
+            own_s[slot, down, :] = total.astype(own_s.dtype)
+            return carry
+
+        lax.fori_loop(0, HEAD_GROUPS * (rows // chunk), add, 0)
+        number = apart - 1 + HEAD_GROUPS - 1
+        own.append(pltpu.make_async_copy(own_s.at[group], kv_land.at[group], local_sem.at[2]))
+        own[2].start()
+        for gap in range(1, HEAD_GROUPS):
+            other = lax.bitwise_xor(group, gap)
+            copy = remote(
+                own_s.at[other], kv_land.at[group], sems, number, ctx_partner(gap * apart)
+            )
+            copy.start()
+            far_kv.append(copy)
+            number = number + 1
+
+    def write():
+        own[1].wait()
+        for copy in far_q:
+            copy.wait_recv()
+        for other in range(HEAD_GROUPS):
+            out_ref[:, other * cols : (other + 1) * cols] = q_land[other]
+        own[2].wait()
+        for copy in far_kv:
+            copy.wait_recv()
+        for other in range(HEAD_GROUPS):
+            for part in range(2):
+                first = (part + 1) * width + other * cols
+                out_ref[:, first : first + cols] = kv_land[
+                    other, :, part * cols : (part + 1) * cols
+                ]
+        for copy in near + far_q + far_kv:
+            copy.wait_send()
+
+    return send, add_near, write
+
+
+def collect_scratch(rows, cols, dtype):
+    apart = lax.axis_size("ctx") // HEAD_GROUPS
     copies = apart - 1 + 2 * (HEAD_GROUPS - 1)
-    hbm = pl.BlockSpec(memory_space=pl.ANY)
-    bf16 = jnp.bfloat16
-    return pl.pallas_call(
-        collect_kernel,
-        out_shape=jax.ShapeDtypeStruct((rows, 3 * cols * HEAD_GROUPS), bf16),
-        in_specs=[hbm, hbm],
-        out_specs=pl.BlockSpec(memory_space=pltpu.VMEM),
-        scratch_shapes=[
-            pltpu.VMEM((max(apart - 1, 1), HEAD_GROUPS, rows, 2 * cols), bf16),
-            pltpu.VMEM((HEAD_GROUPS, rows, 2 * cols), bf16),
-            pltpu.VMEM((HEAD_GROUPS, rows, cols), bf16),
-            pltpu.VMEM((HEAD_GROUPS, rows, 2 * cols), bf16),
-            pltpu.SemaphoreType.DMA((copies,)),
-            pltpu.SemaphoreType.DMA((copies,)),
-            pltpu.SemaphoreType.DMA((3,)),
-        ],
-        compiler_params=pltpu.CompilerParams(
-            collective_id=collective, has_side_effects=True, vmem_limit_bytes=24 << 20
-        ),
-        name="collect_heads",
-    )(dq, dkv.reshape(HEAD_GROUPS, apart, rows, 2 * cols))
-
-
-def scan_kernel(forward_first, a_ref, b_ref, local_ref, cum_ref, total_ref, coef_s, term_s):
-    rows, width = a_ref.shape
-    segments = 8
-    length = rows // segments
-    lanes = 128
-    chunks = width // lanes
-    half = chunks // 2
-    ahead = [(chunk < half) == forward_first for chunk in range(chunks)]
-    for chunk in range(chunks):
-        span = pl.ds(chunk * rows, rows)
-        coef_s[span, :] = a_ref[:, pl.ds(chunk * lanes, lanes)]
-        term_s[span, :] = b_ref[:, pl.ds(chunk * lanes, lanes)]
+    return [
+        pltpu.VMEM((max(apart - 1, 1), HEAD_GROUPS, rows, 2 * cols), dtype),
+        pltpu.VMEM((HEAD_GROUPS, rows, 2 * cols), dtype),
+        pltpu.VMEM((HEAD_GROUPS, rows, cols), dtype),
+        pltpu.VMEM((HEAD_GROUPS, rows, 2 * cols), dtype),
+        pltpu.SemaphoreType.DMA((copies,)),
+        pltpu.SemaphoreType.DMA((copies,)),
+        pltpu.SemaphoreType.DMA((3,)),
+    ]
+
+
+LANES = 128
+SEGMENTS = 8
+PAD = 8
+
+
+def gate_cols(chunk, half):
+    direction, inside = chunk // half, (chunk % half) * LANES
+    first = direction * 2 * half * LANES + inside
+    return first, first + half * LANES, inside
+
+
+def read_gate(gates_ref, curve_ref, down, chunk, half):
+    gate, cand, inside = gate_cols(chunk, half)
+    zeta = jax.nn.sigmoid(
+        gates_ref[down, pl.ds(gate, LANES)] - curve_ref[0:1, pl.ds(inside, LANES)]
+    )
+    return zeta, gates_ref[down, pl.ds(cand, LANES)] * curve_ref[1:2, pl.ds(inside, LANES)]
+
+
+def scan_chunks(coef_s, term_s, rows, chunks, ahead, shifts, found):
+    length = rows // SEGMENTS
+    pitch = rows + 2 * PAD
+    parts = 4
 
     def step(j, carry):
         states, prods = carry
         new_states, new_prods = [], []
         for chunk in range(chunks):
             place = j if ahead[chunk] else length - 1 - j
-            where = (pl.ds(chunk * rows + place, segments, stride=length), slice(None))
-            coef = coef_s[where]
-            state = coef * states[chunk] + term_s[where]
+            base = chunk * pitch + PAD + place
+            coef_at = pl.ds(base + shifts[chunk], SEGMENTS, stride=length)
+            term_at = pl.ds(base, SEGMENTS, stride=length)
+            coef = coef_s[coef_at, :]
+            state = coef * states[chunk] + term_s[term_at, :]
             prod = coef * prods[chunk]
-            term_s[where] = state
-            coef_s[where] = prod
+            term_s[term_at, :] = state
+            coef_s[coef_at, :] = prod
             new_states.append(state)
             new_prods.append(prod)
         return (tuple(new_states), tuple(new_prods))
 
-    zero = jnp.zeros((segments, lanes), jnp.float32)
-    one = jnp.ones((segments, lanes), jnp.float32)
-    states, prods = lax.fori_loop(
-        0, length, step, ((zero,) * chunks, (one,) * chunks), unroll=4
-    )
-    for chunk in range(chunks):
-        cols = pl.ds(chunk * lanes, lanes)
-        carry = jnp.zeros((1, lanes), jnp.float32)
-        prod = jnp.ones((1, lanes), jnp.float32)
-        order = range(segments) if ahead[chunk] else range(segments - 1, -1, -1)
-        for segment in order:
-            span = (pl.ds(segment * length, length), cols)
-            held = pl.ds(chunk * rows + segment * length, length)
-            cum = coef_s[held, :]
-            local_ref[span] = term_s[held, :] + cum * carry
-            cum_ref[span] = cum * prod
-            end_prod = prods[chunk][segment : segment + 1]
-            carry = end_prod * carry + states[chunk][segment : segment + 1]
-            prod = end_prod * prod
-        total_ref[0:1, cols] = prod
-        total_ref[1:2, cols] = carry
-
-
-def scan_both(coefs, terms, forward_first):
-    rows, width = coefs.shape
-    full = jax.ShapeDtypeStruct((rows, width), jnp.float32)
-    whole = pl.BlockSpec(memory_space=pltpu.VMEM)
-    return pl.pallas_call(
-        functools.partial(scan_kernel, forward_first),
-        out_shape=(full, full, jax.ShapeDtypeStruct((8, width), jnp.float32)),
-        in_specs=[whole, whole],
-        out_specs=(whole, whole, whole),
-        scratch_shapes=[pltpu.VMEM((rows * width // 128, 128), jnp.float32)] * 2,
-        compiler_params=pltpu.CompilerParams(vmem_limit_bytes=32 << 20),
-        cost_estimate=pl.CostEstimate(
-            flops=8 * rows * width, bytes_accessed=16 * rows * width, transcendentals=0
-        ),
-        name="scan_both",
-    )(coefs, terms)
-
-
-def carried(totals, forward_first):
-    count, mine = lax.axis_size("ctx"), lax.axis_index("ctx")
-    pieces = lax.all_gather(totals[:2], "ctx")
-    half = totals.shape[1] // 2
+    zero = jnp.zeros((SEGMENTS, LANES), jnp.float32)
+    one = jnp.ones((SEGMENTS, LANES), jnp.float32)
+    found.append(((zero,) * chunks, (one,) * chunks))
+
+    def part(number):
+        span = length // parts
+        found[0] = lax.fori_loop(number * span, (number + 1) * span, step, found[0], unroll=4)
+
+    return [functools.partial(part, number) for number in range(parts)]
+
+
+def block_totals(states, prods, chunk, ahead):
+    carry = jnp.zeros((1, LANES), jnp.float32)
+    prod = jnp.ones((1, LANES), jnp.float32)
+    for segment in range(SEGMENTS) if ahead[chunk] else range(SEGMENTS - 1, -1, -1):
+        row = slice(segment, segment + 1)
+        carry = prods[chunk][row] * carry + states[chunk][row]
+        prod = prods[chunk][row] * prod
+    return prod, carry
+
+
+def carry_of(totals_ref, forward_first):
+    count = totals_ref.shape[0]
+    mine = lax.axis_index("ctx")
+    half = totals_ref.shape[2] // 2
     low = jnp.zeros((1, half), jnp.float32)
     high = jnp.zeros((1, half), jnp.float32)
     for position in range(count - 1):
         back = count - 1 - position
         first, second = (position, back) if forward_first else (back, position)
-        ahead_ok = (first < mine) if forward_first else (first > mine)
-        behind_ok = (second > mine) if forward_first else (second < mine)
+        low_ok = (first < mine) if forward_first else (first > mine)
+        high_ok = (second > mine) if forward_first else (second < mine)
         low = jnp.where(
-            ahead_ok, pieces[first, 0:1, :half] * low + pieces[first, 1:2, :half], low
+            low_ok, totals_ref[first, 0:1, :half] * low + totals_ref[first, 1:2, :half], low
         )
         high = jnp.where(
-            behind_ok, pieces[second, 0:1, half:] * high + pieces[second, 1:2, half:], high
+            high_ok, totals_ref[second, 0:1, half:] * high + totals_ref[second, 1:2, half:], high
         )
     return jnp.concatenate([low, high], axis=1)
 
 
-def padded_2(cells, sides, width):
-    for axis, dim in sides:
-        count = lax.axis_size(axis)
-        ends = count - 1
-        head = lax.slice_in_dim(cells, 0, width, axis=dim)
-        tail = lax.slice_in_dim(cells, cells.shape[dim] - width, cells.shape[dim], axis=dim)
-        cells = jnp.concatenate(
-            [
-                lax.ppermute(tail, axis, [(i, (i + 1) % count) for i in range(ends)]),
-                cells,
-                lax.ppermute(head, axis, [((i + 1) % count, i) for i in range(ends)]),
-            ],
-            axis=dim,
+def segment_carries(states, prods, chunk, ahead, entering):
+    carry = entering[:, chunk * LANES : (chunk + 1) * LANES]
+    carries = {}
+    for segment in range(SEGMENTS) if ahead[chunk] else range(SEGMENTS - 1, -1, -1):
+        row = slice(segment, segment + 1)
+        carries[segment] = carry
+        carry = prods[chunk][row] * carry + states[chunk][row]
+    return carries
+
+
+def ring_partner(step):
+    count = lax.axis_size("ctx")
+    return place_of("ctx", lax.rem(lax.axis_index("ctx") + count + step, count))
+
+
+def greet_all():
+    barrier = pltpu.get_barrier_semaphore()
+    partners = [ctx_partner(gap) for gap in range(1, lax.axis_size("ctx"))] + [
+        place_of("wsh", lax.bitwise_xor(lax.axis_index("wsh"), gap))
+        for gap in range(1, lax.axis_size("wsh"))
+    ]
+    for partner in partners:
+        pl.semaphore_signal(
+            barrier, inc=1, device_id=partner, device_id_type=pl.DeviceIdType.MESH
         )
-    return cells
+    pl.semaphore_wait(barrier, len(partners))
+
+
+def front_kernel(slots, count, *refs):
+    shards = refs[:count]
+    qkv_ref, gates_ref, chars_ref, curve_ref, keep_ref, map_ref = refs[count : count + 6]
+    refs = refs[count + 6 :]
+    outs = refs[:count]
+    q_out, kv_out, states_ref, chars_out, pooled_ref, edge_ref, root_ref = refs[count : count + 7]
+    refs = refs[count + 7 :]
+    gather_scratch, spread_refs, refs = refs[:3], refs[3:8], refs[8:]
+    coef_s, term_s, mixed_s, totals_s, land_edge, send_sem, recv_sem = refs
+    sems = (send_sem, recv_sem)
+    rows, width = chars_ref.shape
+    chunks = width // LANES
+    half = chunks // 2
+    length = rows // SEGMENTS
+    pitch = rows + 2 * PAD
+    ahead = [chunk < half for chunk in range(chunks)]
+    mine = lax.axis_index("ctx")
+    others = lax.axis_size("ctx") - 1
+    toks = pooled_ref.shape[0]
+    tail = edge_ref.shape[1]
+    send, pass_on, wait = spread_ticks(qkv_ref, q_out, kv_out, *spread_refs)
+    found, small, edges, kept = [], [], [], {}
+
+    def prepare(chunk):
+        direction = chunk // half
+
+        def one(position, carry):
+            down = pl.ds(pl.multiple_of(position * length, length), length)
+            zeta, cand = read_gate(gates_ref, curve_ref, down, chunk, half)
+            held = pl.ds(pl.multiple_of(chunk * pitch + PAD + position * length, 8), length)
+            coef_s[held, :] = (1.0 - zeta) * keep_ref[down, direction : direction + 1]
+            term_s[held, :] = zeta * cand
+            return carry
+
+        lax.fori_loop(0, SEGMENTS, one, 0)
+
+    def send_totals():
+        states, prods = found[0]
+        for chunk in range(chunks):
+            prod, carry = block_totals(states, prods, chunk, ahead)
+            cols = pl.ds(chunk * LANES, LANES)
+            totals_s[mine, 0:1, cols] = prod
+            totals_s[mine, 1:2, cols] = carry
+        small.extend(exchange_sums(totals_s, sems, 0))
+
+    def count_chars():
+        hits = lax.broadcasted_iota(jnp.int32, (toks, rows), 0) == map_ref[0:1, :]
+        counts = jnp.sum(hits.astype(jnp.float32), axis=1, keepdims=True)
+        root_ref[...] = jnp.broadcast_to(jnp.sqrt(counts), root_ref.shape)
+
+    def enter():
+        for copy in small:
+            copy.wait_recv()
+        entering = carry_of(totals_s, True)
+        states_ref[PAD - 1 : PAD, :] = entering
+        states_ref[PAD + rows : PAD + rows + 1, :] = entering
+        kept["entering"] = entering
+
+    def settle(chunk):
+        states, prods = found[0]
+        carries = segment_carries(states, prods, chunk, ahead, kept["entering"])
+        cols = pl.ds(chunk * LANES, LANES)
+        for segment in range(SEGMENTS):
+            held = pl.ds(chunk * pitch + PAD + segment * length, length)
+            down = pl.ds(segment * length, length)
+            state = term_s[held, :] + coef_s[held, :] * carries[segment]
+            states_ref[pl.ds(PAD + segment * length, length), cols] = state
+            mixed = state.astype(jnp.bfloat16)
+            mixed_s[down, cols] = mixed
+            chars_out[down, cols] = (
+                chars_ref[down, cols].astype(jnp.float32) + mixed.astype(jnp.float32)
+            ).astype(jnp.bfloat16)
+
+    def pool():
+        hits = lax.broadcasted_iota(jnp.int32, (toks, rows), 0) == map_ref[0:1, :]
+        pooled_ref[...] = (
+            dot32(hits.astype(jnp.bfloat16), mixed_s[...]) / root_ref[:, 0:1]
+        ).astype(jnp.bfloat16)
+        last = pooled_ref.at[pl.ds(toks - tail, tail)]
+        edges.append(remote(last, land_edge.at[0], sems, others, ring_partner(1)))
+        head = pooled_ref.at[pl.ds(0, tail)]
+        edges.append(remote(head, land_edge.at[1], sems, others + 1, ring_partner(-1)))
+        for copy in edges:
+            copy.start()
+
+    def close():
+        for copy in edges:
+            copy.wait_recv()
+        edge_ref[...] = land_edge[...]
+        for copy in small + edges:
+            copy.wait_send()
+
+    pieces = [functools.partial(prepare, chunk) for chunk in range(chunks)]
+    pieces.insert(chunks // 2, pass_on)
+    pieces = pieces + scan_chunks(
+        coef_s, term_s, rows, chunks, ahead, [0] * chunks, found
+    )
+    pieces = pieces + [send_totals, count_chars, wait, enter]
+    pieces = pieces + [functools.partial(settle, chunk) for chunk in range(chunks)]
+    pieces = pieces + [pool, close]
+    greet_all()
+    send()
+    weave(
+        gather_ticks(slots, shards, outs, gather_scratch[:2], gather_scratch[2], True), pieces, FRONT_SHARE
+    )
+
+
+def front(arrays, slots, qkv, gates, chars, curve, keep, char_map, collective):
+    count = len(arrays)
+    rows, width = chars.shape
+    toks = qkv.shape[0]
+    cols = width // HEAD_GROUPS
+    ctx = lax.axis_size("ctx")
+    f32, bf16 = jnp.float32, jnp.bfloat16
+    hbm = pl.BlockSpec(memory_space=pl.ANY)
+    whole = pl.BlockSpec(memory_space=pltpu.VMEM)
+    held = pltpu.VMEM((width // LANES * (rows + 2 * PAD), LANES), f32)
+    outs = pl.pallas_call(
+        functools.partial(front_kernel, slots, count),
+        out_shape=gather_shapes(arrays, True)
+        + (
+            jax.ShapeDtypeStruct((HEAD_GROUPS, toks, cols), bf16),
+            jax.ShapeDtypeStruct((ctx, toks, 2 * cols), bf16),
+            jax.ShapeDtypeStruct((rows + 2 * PAD, width), f32),
+            jax.ShapeDtypeStruct((rows, width), bf16),
+            jax.ShapeDtypeStruct((toks, width), bf16),
+            jax.ShapeDtypeStruct((2, 16, width), bf16),
+            jax.ShapeDtypeStruct((toks, LANES), f32),
+        ),
+        in_specs=[hbm] * count + [whole] * 6,
+        out_specs=(hbm,) * (count + 2) + (whole,) * 5,
+        scratch_shapes=gather_sems(slots, True)
+        + spread_scratch(toks, cols, bf16)
+        + [
+            held,
+            held,
+            pltpu.VMEM((rows, width), bf16),
+            pltpu.VMEM((ctx, 8, width), f32),
+            pltpu.VMEM((2, 16, width), bf16),
+            pltpu.SemaphoreType.DMA((ctx + 1,)),
+            pltpu.SemaphoreType.DMA((ctx + 1,)),
+        ],
+        compiler_params=pltpu.CompilerParams(
+            collective_id=collective, has_side_effects=True, vmem_limit_bytes=48 << 20
+        ),
+        name="front",
+    )(*arrays, qkv, gates, chars, curve, keep, char_map)
+    return [out.reshape((-1, out.shape[-1])) for out in outs[:count]], outs[count:]
+
+
+def back_kernel(slots, late_slots, count, *refs):
+    grads = refs[:count]
+    dq_ref, dkv_ref, gates_ref, states_ref, cot_ref, taps_ref, curve_ref, keep_ref, root_ref, in_ref = refs[
+        count : count + 10
+    ]
+    refs = refs[count + 10 :]
+    outs, late_out = refs[:count], refs[count]
+    heads_out, gates_out, late_grad = refs[count + 1 : count + 4]
+    refs = refs[count + 4 :]
+    collect_refs, refs = refs[:7], refs[7:]
+    coef_s, term_s, edge_s, high_s, low_s, totals_s, stage_s = refs[:7]
+    send_sem, recv_sem, stage_sem = refs[7:10]
+    late_size = 3 + 1 + len([stream for slot in late_slots for stream in slot]) * (
+        len(masks_of("ctx")) + 1
+    )
+    ticks = scatter_ticks(slots, grads, outs, refs[10 + late_size :], True)
+    late_ticks = scatter_ticks(
+        late_slots, [late_grad], [late_out], refs[10 : 10 + late_size], True
+    )
+    sems = (send_sem, recv_sem)
+    rows, width = cot_ref.shape
+    toks = root_ref.shape[0]
+    chunks = width // LANES
+    half = chunks // 2
+    length = rows // SEGMENTS
+    pitch = rows + 2 * PAD
+    ahead = [chunk >= half for chunk in range(chunks)]
+    shifts = [1 if chunk < half else -1 for chunk in range(chunks)]
+    ctx = lax.axis_size("ctx")
+    mine = lax.axis_index("ctx")
+    others = ctx - 1
+    bf16 = jnp.bfloat16
+    send, add_near, write = collect_ticks(dq_ref, dkv_ref, heads_out, collect_refs)
+    found, small, edges, kept = [], [], [], {}
+
+    def open_edges():
+        head = taps_ref.at[0, pl.ds(0, PAD)]
+        edges.append(remote(head, edge_s.at[0], sems, others, ring_partner(-1)))
+        last = taps_ref.at[2, pl.ds(toks - PAD, PAD)]
+        edges.append(remote(last, edge_s.at[1], sems, others + 1, ring_partner(1)))
+        for copy in edges:
+            copy.start()
+
+    def prepare(chunk):
+        direction = chunk // half
+        gate, _, inside = gate_cols(chunk, half)
+
+        def one(position, carry):
+            down = pl.ds(pl.multiple_of(position * length, length), length)
+            zeta = jax.nn.sigmoid(
+                gates_ref[down, pl.ds(gate, LANES)] - curve_ref[0:1, pl.ds(inside, LANES)]
+            )
+            held = pl.ds(pl.multiple_of(chunk * pitch + PAD + position * length, 8), length)
+            coef_s[held, :] = (1.0 - zeta) * keep_ref[down, direction : direction + 1]
+            return carry
+
+        lax.fori_loop(0, SEGMENTS, one, 0)
+        outside = chunk * pitch + (PAD + rows if chunk < half else 0)
+        coef_s[pl.ds(outside, PAD), :] = jnp.ones((PAD, LANES), jnp.float32)
+
+    def join_taps():
+        for copy in edges:
+            copy.wait_recv()
+        token = lax.broadcasted_iota(jnp.int32, (toks, width), 0)
+        outer = jnp.where(mine == ctx - 1, 0.0, edge_s[0, 0:1, :])
+        after = jnp.where(token == toks - 1, outer, pltpu.roll(taps_ref[0], toks - 1, 0))
+        outer = jnp.where(mine == 0, 0.0, edge_s[1, PAD - 1 : PAD, :])
+        before = jnp.where(token == 0, outer, pltpu.roll(taps_ref[2], 1, 0))
+        pooled_grad = (after + taps_ref[1] + before) / root_ref[:, 0:1]
+        high = pooled_grad.astype(bf16)
+        high_s[...] = high
+        low_s[...] = (pooled_grad - high.astype(jnp.float32)).astype(bf16)
+
+    def mix(first, last):
+        def one(position, carry):
+            down = pl.ds(pl.multiple_of(position * length, length), length)
+            tokens = lax.broadcasted_iota(jnp.int32, (length, toks), 1).astype(jnp.float32)
+            hits = (tokens == keep_ref[down, 2:3]).astype(bf16)
+            mixed = cot_ref[down, :].astype(jnp.float32) + (
+                dot32(hits, high_s[...]) + dot32(hits, low_s[...])
+            )
+            for chunk in range(chunks):
+                held = pl.ds(pl.multiple_of(chunk * pitch + PAD + position * length, 8), length)
+                term_s[held, :] = mixed[:, chunk * LANES : (chunk + 1) * LANES]
+            return carry
+
+        lax.fori_loop(first, last, one, 0)
+
+    def send_totals():
+        states, prods = found[0]
+        for chunk in range(chunks):
+            prod, carry = block_totals(states, prods, chunk, ahead)
+            edge = chunk * pitch + PAD + (0 if chunk < half else rows - 1)
+            own = coef_s[pl.ds(edge, 1), :]
+            cols = pl.ds(chunk * LANES, LANES)
+            totals_s[mine, 0:1, cols] = own * prod
+            totals_s[mine, 1:2, cols] = own * carry
+        small.extend(exchange_sums(totals_s, sems, 0))
+
+    block = 3 * LANES
+    group_rows = late_grad.shape[-2]
+    groups_in = block // group_rows
+
+    def weigh(down, across):
+        cols = pl.ds(across * width, width)
+        product = lax.dot_general(
+            in_ref[:, down * block : (down + 1) * block],
+            heads_out[:, across * width : (across + 1) * width],
+            (((0,), (0,)), ((), ())),
+            preferred_element_type=jnp.float32,
+        ).astype(bf16)
+        slot = (down * 3 + across) % 2
+        if down * 3 + across >= 2:
+            kept["stage", slot].wait()
+        lead = stage_s.shape[1:-2]
+        for group in range(groups_in):
+            place, rest = [], group
+            for size in reversed(lead):
+                place.append(rest % size)
+                rest = rest // size
+            stage_s[(slot,) + tuple(place[::-1])] = product[
+                group * group_rows : (group + 1) * group_rows
+            ]
+        copy = pltpu.make_async_copy(
+            stage_s.at[slot],
+            late_grad.at[(down,) + (slice(None),) * len(lead) + (slice(None), cols)],
+            stage_sem.at[slot],
+        )
+        copy.start()
+        kept["stage", slot] = copy
+
+    def open_late():
+        for slot in range(2):
+            kept["stage", slot].wait()
+        late_ticks.pop(0)()
+
+    def enter():
+        for copy in small:
+            copy.wait_recv()
+        kept["entering"] = carry_of(totals_s, False)
+
+    def settle(chunk):
+        states, prods = found[0]
+        carries = segment_carries(states, prods, chunk, ahead, kept["entering"])
+        gate, cand_at, inside = gate_cols(chunk, half)
+        direction = chunk // half
+        behind = -1 if chunk < half else 1
+        cols = pl.ds(chunk * LANES, LANES)
+        lift = curve_ref[1:2, pl.ds(inside, LANES)]
+        for segment in range(SEGMENTS):
+            base = chunk * pitch + PAD + segment * length
+            down = pl.ds(segment * length, length)
+            slope = (
+                term_s[pl.ds(base, length), :]
+                + coef_s[pl.ds(base + shifts[chunk], length), :] * carries[segment]
+            )
+            zeta, cand = read_gate(gates_ref, curve_ref, down, chunk, half)
+            past = states_ref[pl.ds(PAD + segment * length + behind, length), cols]
+            keep = keep_ref[down, direction : direction + 1]
+            lifted = slope * zeta
+            gates_out[down, pl.ds(gate, LANES)] = (
+                lifted * (cand - keep * past) * (1.0 - zeta)
+            ).astype(bf16)
+            gates_out[down, pl.ds(cand_at, LANES)] = (lifted * lift).astype(bf16)
+
+    def close():
+        for copy in small + edges:
+            copy.wait_send()
+
+    prepares = [functools.partial(prepare, chunk) for chunk in range(chunks)]
+    pieces = prepares[:half] + [add_near] + prepares[half:] + [join_taps]
+    pieces = pieces + [functools.partial(mix, 0, 4), functools.partial(mix, 4, SEGMENTS), write]
+    weighs = [
+        functools.partial(weigh, down, across) for down in range(width // block) for across in range(3)
+    ]
+    scans = scan_chunks(coef_s, term_s, rows, chunks, ahead, shifts, found)
+    pieces = pieces + weighs + [open_late] + scans + [send_totals, enter]
+    pieces = pieces + [functools.partial(settle, chunk) for chunk in range(chunks)] + [close]
+    greet_all()
+    open_edges()
+    send()
+    total = len(ticks) + len(late_ticks) - 1
+    ticks.pop(0)()
+    done = 1
+    for number, piece in enumerate(pieces):
+        piece()
+        while done < BACK_SHARE * total * (number + 1) / len(pieces) and len(ticks) > 4:
+            ticks.pop(0)()
+            done = done + 1
+    while ticks or late_ticks:
+        if late_ticks:
+            late_ticks.pop(0)()
+        if ticks:
+            ticks.pop(0)()
+
+
+def back(arrays, slots, dq, dkv, gates, states, cot, taps, curve, keep, roots, attn_in, collective):
+    count = len(arrays)
+    rows, width = cot.shape
+    toks, cols = dq.shape[1:]
+    ctx, wsh = lax.axis_size("ctx"), lax.axis_size("wsh")
+    bits = len(masks_of("ctx"))
+    apart = ctx // HEAD_GROUPS
+    f32, bf16 = jnp.float32, jnp.bfloat16
+    hbm = pl.BlockSpec(memory_space=pl.ANY)
+    whole = pl.BlockSpec(memory_space=pltpu.VMEM)
+    held = pltpu.VMEM((width // LANES * (rows + 2 * PAD), LANES), f32)
+    shaped, shard_rows = scatter_shapes(arrays, True)
+    late = jax.ShapeDtypeStruct((width, 3 * width), bf16)
+    late_rows = width // (ctx * wsh)
+    late_slots = slots_of([late], False)
+    outs = pl.pallas_call(
+        functools.partial(back_kernel, slots, late_slots, count),
+        out_shape=tuple(
+            jax.ShapeDtypeStruct((row, array.shape[1]), f32)
+            for array, row in zip(arrays, shard_rows)
+        )
+        + (
+            jax.ShapeDtypeStruct((late_rows, 3 * width), f32),
+            jax.ShapeDtypeStruct((toks, 3 * width), bf16),
+            jax.ShapeDtypeStruct(gates.shape, bf16),
+            jax.ShapeDtypeStruct((2,) * bits + (wsh, late_rows, 3 * width), bf16),
+        ),
+        in_specs=[hbm] * (count + 2) + [whole] * 8,
+        out_specs=(whole,) * (count + 3) + (hbm,),
+        scratch_shapes=collect_scratch(toks, cols, bf16)
+        + [
+            held,
+            held,
+            pltpu.VMEM((2, PAD, width), f32),
+            pltpu.VMEM((toks, width), bf16),
+            pltpu.VMEM((toks, width), bf16),
+            pltpu.VMEM((ctx, 8, width), f32),
+            pltpu.VMEM((2,) + (2,) * (bits - 1) + (wsh, late_rows, width), bf16),
+            pltpu.SemaphoreType.DMA((ctx + 1,)),
+            pltpu.SemaphoreType.DMA((ctx + 1,)),
+            pltpu.SemaphoreType.DMA((2,)),
+        ]
+        + scatter_scratch([late], late_slots, True)
+        + scatter_scratch(arrays, slots, True),
+        compiler_params=pltpu.CompilerParams(
+            collective_id=collective, has_side_effects=True, vmem_limit_bytes=60 << 20
+        ),
+        name="back",
+    )(
+        *shaped,
+        dq,
+        dkv.reshape(HEAD_GROUPS, apart, toks, 2 * cols),
+        gates,
+        states,
+        cot,
+        taps,
+        curve,
+        keep,
+        roots,
+        attn_in,
+    )
+    return outs[:count], outs[count : count + 3]
 
 
 def normed(values, scales):
@@ -1100,7 +1580,6 @@
 ):
     f32 = jnp.float32
     bf16 = jnp.bfloat16
-    every = ("ctx", "wsh")
     width = tokens.shape[2]
     lane = 128
     gain_block = jnp.stack([gain_attn, gain_char, gain_merge], axis=1)
@@ -1108,20 +1587,13 @@
     first_needed = [gru_weight, jnp.concatenate([qkv_weight, gain_block], axis=1)]
     gru_full, gains_and_qkv = gather_all(
         first_needed,
-        slots_of(first_needed),
+        slots_of(first_needed, True),
         True,
         0,
     )
     qkv_full = gains_and_qkv[:, : 3 * width]
     gains = jnp.transpose(gains_and_qkv[:, 3 * width :].astype(f32))
     attn_gain_f, char_gain_f, merge_gain_f = gains[0], gains[1], gains[2]
-    later = [conv_weight, out_weight, merge_weight, up_weight, down_weight]
-    conv_full, out_full, merge_full, up_full, down_full = gather_all(
-        later,
-        slots_of(later),
-        True,
-        1,
-    )
     tok_rows = tokens.shape[1]
     char_rows = chars.shape[1]
     half_width = width // 2
@@ -1135,9 +1607,6 @@
     doc_first = jnp.any(starts[None, :] == positions[:, None], axis=1)
     doc_last = jnp.any(starts[None, :] == positions[:, None] + 1, axis=1)
     onehot = char_map[None, :] == jnp.arange(tok_rows, dtype=jnp.int32)[:, None]
-    onehot_low = onehot.astype(bf16)
-    counts = jnp.sum(onehot.astype(f32), axis=1)
-    root_counts = jnp.sqrt(counts)
     boundary = char_map[1:] != char_map[:-1]
     first_char = jnp.concatenate([jnp.ones((1,), bool), boundary])
     last_char = jnp.concatenate([boundary, jnp.ones((1,), bool)])
@@ -1167,35 +1636,31 @@
     bounds = jnp.stack(
         [doc_begin[:, 0] // tok_rows, (doc_end[:, -1] + tok_rows - 1) // tok_rows], axis=1
     )
-    q_heads, kv_heads = spread_heads(qkv, 2)
-    o_heads, exact_heads, log_heads = attend(bounds, q_heads, kv_heads, spans)
-    attn_out, proj, resid, sums = join_heads(o_heads, tokens[0], out_full, elements, 6)
     char_low = normed(char_in, char_gain_f).astype(bf16)
     gates = jnp.dot(char_low, gru_full, preferred_element_type=f32)
     ramp = jnp.arange(half_width, dtype=f32) / (half_width - 1)
     shift = (1.0 + math.log(char_rows * lax.axis_size("ctx"))) * ramp
-    lift = jnp.exp(0.5 * shift)
-    zeta_f = jax.nn.sigmoid(gates[:, :half_width] - shift)
-    cand_f = gates[:, half_width : 2 * half_width] * lift
-    zeta_b = jax.nn.sigmoid(gates[:, 2 * half_width : 3 * half_width] - shift)
-    cand_b = gates[:, 3 * half_width :] * lift
-    coef_f = (1.0 - zeta_f) * keep_fwd[:, None]
-    coef_b = (1.0 - zeta_b) * keep_bwd[:, None]
-    coefs = jnp.concatenate([coef_f, coef_b], axis=1)
-    terms = jnp.concatenate([zeta_f * cand_f, zeta_b * cand_b], axis=1)
-    local_state, cum_state, totals = scan_both(coefs, terms, True)
-    carry_in = carried(totals, True)
-    states = local_state + cum_state * carry_in
-    state_f = states[:, :half_width]
-    state_b = states[:, half_width:]
-    carry_in_f = carry_in[0, :half_width]
-    carry_in_b = carry_in[0, half_width:]
-    mixed = states.astype(bf16)
-    out_chars = (char_in + mixed.astype(f32)).astype(bf16)
-    pooled = (jnp.dot(onehot_low, mixed, preferred_element_type=f32) / root_counts[:, None]).astype(
-        bf16
-    )
-    padded = padded_2(pooled, (("ctx", 0),), 1)
+    curve = jnp.pad(jnp.stack([shift, jnp.exp(0.5 * shift)]), ((0, 6), (0, 0)))
+    keep = jnp.stack([keep_fwd, keep_bwd, char_map.astype(f32)], axis=1)
+    keep = jnp.pad(keep, ((0, 0), (0, lane - 3)))
+    later = [conv_weight, out_weight, merge_weight, up_weight, down_weight]
+    gathered, fronts = front(
+        later, slots_of(later, True), qkv, gates, chars[0], curve, keep, char_map[None, :], 1
+    )
+    conv_full, out_full, merge_full, up_full, down_full = gathered
+    q_heads, kv_heads, states, out_chars, pooled, edges, roots = fronts
+    o_heads, exact_heads, log_heads = attend(bounds, q_heads, kv_heads, spans)
+    attn_out, proj, resid, sums = join_heads(o_heads, tokens[0], out_full, elements, 6)
+    mine = lax.axis_index("ctx")
+    edge_rows = edges.shape[1]
+    padded = jnp.concatenate(
+        [
+            jnp.where(mine == 0, 0.0, edges[0, edge_rows - 1 :]).astype(bf16),
+            pooled,
+            jnp.where(mine == lax.axis_size("ctx") - 1, 0.0, edges[1, :1]).astype(bf16),
+        ],
+        axis=0,
+    )
     conv_out = jnp.zeros((tok_rows, width), f32)
     for kernel in range(3):
         conv_out = conv_out + jnp.dot(
@@ -1234,82 +1699,66 @@
         ],
         axis=1,
     )
-    grad_padded = padded_2(grad_pre, (("ctx", 0),), 1)
-    grad_pooled = jnp.zeros((tok_rows, width), f32)
-    for kernel in range(3):
-        grad_pooled = grad_pooled + jnp.einsum(
-            "te,ce->tc",
-            grad_padded[2 - kernel : 2 - kernel + tok_rows],
-            conv_full[:, kernel * width : (kernel + 1) * width],
-            preferred_element_type=f32,
-        )
+    grad_taps = jnp.stack(
+        [
+            jnp.einsum(
+                "te,ce->tc",
+                grad_pre,
+                conv_full[:, kernel * width : (kernel + 1) * width],
+                preferred_element_type=f32,
+            )
+            for kernel in range(3)
+        ]
+    )
     _, merge_norm_back = jax.vjp(normed, resid, merge_gain_f)
     grad_resid_norm, grad_merge_gain = merge_norm_back(grad_merge_in)
     grad_resid = cot_tok_f + grad_resid_norm
-    grad_mixed = cot_chr_f + jnp.take(grad_pooled / root_counts[:, None], char_map, axis=0)
-    shifted_f = jnp.concatenate([coef_f[1:], jnp.ones((1, half_width), f32)], axis=0)
-    shifted_b = jnp.concatenate([jnp.ones((1, half_width), f32), coef_b[:-1]], axis=0)
-    local_lam, cum_lam, lam_totals = scan_both(
-        jnp.concatenate([shifted_f, shifted_b], axis=1), grad_mixed, False
-    )
-    edge = jnp.concatenate([coef_f[0], coef_b[-1]])[None, :]
-    lams = local_lam + cum_lam * carried(lam_totals[:2] * edge, False)
-    lam_f = lams[:, :half_width]
-    lam_b = lams[:, half_width:]
-    prev_f = jnp.concatenate([carry_in_f[None, :], state_f[:-1]], axis=0)
-    grad_zeta_f = lam_f * (cand_f - keep_fwd[:, None] * prev_f) * zeta_f * (1.0 - zeta_f)
-    grad_cand_f = lam_f * zeta_f * lift
-    next_b = jnp.concatenate([state_b[1:], carry_in_b[None, :]], axis=0)
-    grad_zeta_b = lam_b * (cand_b - keep_bwd[:, None] * next_b) * zeta_b * (1.0 - zeta_b)
-    grad_cand_b = lam_b * zeta_b * lift
-    grad_gates = jnp.concatenate(
-        [grad_zeta_f, grad_cand_f, grad_zeta_b, grad_cand_b], axis=1
-    ).astype(bf16)
+    down_shard, grad_stream, grad_proj, g_heads = part_heads(
+        grad_down.astype(bf16), grad_resid, proj, tokens[0], out_full, sums, elements, 7
+    )
+    grad_out_proj = jnp.einsum("tc,te->ce", attn_out, grad_proj, preferred_element_type=f32)
+    dq_heads, dkv_heads = attend_back(
+        bounds, q_heads, kv_heads, g_heads, exact_heads, log_heads, spans
+    )
+    early = [grad_up, grad_conv, grad_out_proj, grad_merge]
+    early = [part.astype(bf16) for part in early]
+    early_shards, backs = back(
+        early,
+        slots_of(early, False),
+        dq_heads,
+        dkv_heads,
+        gates,
+        states,
+        cot_chars[0],
+        grad_taps,
+        curve,
+        keep,
+        roots,
+        attn_in,
+        4,
+    )
+    up_shard, conv_shard, out_shard, merge_shard = early_shards
+    qkv_shard, grad_qkv_low, grad_gates = backs
     grad_gru = jnp.einsum("tc,tg->cg", char_low, grad_gates, preferred_element_type=f32)
     grad_char_norm = jnp.einsum("tg,cg->tc", grad_gates, gru_full, preferred_element_type=f32)
     _, char_norm_back = jax.vjp(normed, char_in, char_gain_f)
     grad_char_in, grad_char_gain = char_norm_back(grad_char_norm)
     grad_chars_out = (cot_chr_f + grad_char_in).astype(bf16)
-    grad_stream, grad_proj, g_heads = part_heads(
-        grad_resid, proj, tokens[0], out_full, sums, elements, 7
-    )
-    grad_out_proj = jnp.einsum("tc,te->ce", attn_out, grad_proj, preferred_element_type=f32)
-    dq_heads, dkv_heads = attend_back(
-        bounds, q_heads, kv_heads, g_heads, exact_heads, log_heads, spans
-    )
-    grad_qkv_low = collect_heads(dq_heads, dkv_heads, 3)
-    grad_qkv = jnp.einsum("tc,tg->cg", attn_in, grad_qkv_low, preferred_element_type=f32)
     grad_attn_in = jnp.einsum("tg,cg->tc", grad_qkv_low, qkv_full, preferred_element_type=f32)
     _, attn_norm_back = jax.vjp(normed, token_in, attn_gain_f)
     grad_token_in, grad_attn_gain = attn_norm_back(grad_attn_in)
     grad_tokens_out = (grad_stream + grad_token_in).astype(bf16)
     gain_grads = jnp.stack([grad_attn_gain, grad_char_gain, grad_merge_gain], axis=1)
     gain_grads = jnp.pad(gain_grads, ((0, 0), (0, lane - 3)))
-    early = [grad_down, grad_up, grad_merge, grad_conv]
-    early = [part.astype(bf16) for part in early]
-    down_shard, up_shard, merge_shard, conv_shard = scatter_sums(
-        early,
-        slots_of(early),
-        True,
-        4,
-        f32,
-    )
-    late = [grad_gru, grad_out_proj, jnp.concatenate([grad_qkv, gain_grads], axis=1)]
-    late = [part.astype(bf16) for part in late]
-    gru_shard, out_shard, qkv_shard = scatter_sums(
-        late,
-        slots_of(late),
-        True,
-        5,
-        f32,
-    )
-    gain_shard = qkv_shard[:, 3 * width :]
+    late = [jnp.concatenate([grad_gru, gain_grads], axis=1).astype(bf16)]
+    gru_shard = scatter_sums(late, slots_of(late, False), True, 5, f32)[0]
+    gain_shard = gru_shard[:, 2 * width :]
     shards = (
         gain_shard[:, 0],
-        qkv_shard[:, : 3 * width],
+        qkv_shard,
         out_shard,
         gain_shard[:, 1],
-        gru_shard,
+        gru_shard[:, : 2 * width],
         conv_shard,
         gain_shard[:, 2],
         merge_shard,

time: 560 us -> 484 us (0.86)
  local copies, waits for them, and re-layouts: 40 us -> 19.8 us
  blocking collectives: 18.5 us -> 0 us
  Pallas kernels: 387 us -> 370 us
  other arithmetic: 38.2 us -> 25.9 us
  starting transfers between devices: 9.01 us -> 0 us
    pallas_call x5 -> x3, Pallas kernels: 81.5 us -> 246 us  [the longest x1 103 us: back(): pl.pallas_call(functools.partial(back_kernel, slots, late_slots, count),...]
    pallas_call x2 -> x1, Pallas kernels: 127 us -> 24.4 us  [scatter_sums(): pl.pallas_call(functools.partial(scatter_kernel, slots, count, over_wsh),...]
    pallas_call x2 -> x1, Pallas kernels: 124 us -> 40.9 us  [gather_all(): pl.pallas_call(functools.partial(gather_kernel, slots, count, over_wsh),...]
    all_gather x2 -> x0, blocking collectives: 18.5 us -> none  [carried(): pieces = lax.all_gather(totals[:2], 'ctx')]
    unnamed x193 -> x145, local copies, waits for them, and re-layouts: 24.3 us -> 14.3 us
    ppermute x4 -> x0, starting transfers between devices: 9.01 us -> none  [the longest x2 5.84 us: padded_2(): lax.ppermute(tail, axis, [(i, (i + 1) % count) for i in range(ends)])]
    concatenate x7 -> x2, other arithmetic: 9.23 us -> 2.56 us  [the longest x1 1.72 us: body(): late = [jnp.concatenate([grad_gru, gain_grads], axis=1).astype(bf16)]]
  transfers between devices with their start and end apart: 4 -> 0, of which waited for: 0 -> 0; matrix products, arithmetic and copies ran while one was open for 5% -> 0% of each run, Pallas kernels for 39% -> 0%
where the time goes in v4:
time: 484 us; the launch traced here: 475 us
  Pallas kernels  370 us (76%)
  matrix products  57 us (12%)
  other arithmetic  25.9 us (5%)
  local copies, waits for them, and re-layouts  19.8 us (4%)
    pallas_call x1, Pallas kernels, back(): pl.pallas_call(functools.partial(back_kernel, slots, late_slots, count),...  103 us
    pallas_call x1, Pallas kernels, front(): pl.pallas_call(functools.partial(front_kernel, slots, count), out_shape=g...  98.7 us
    pallas_call x1, Pallas kernels, part_heads(): pl.pallas_call(functools.partial(part_kernel, elements, slots), out_shape...  44.7 us
    pallas_call x1, Pallas kernels, gather_all(): pl.pallas_call(functools.partial(gather_kernel, slots, count, over_wsh),...  40.9 us
    pallas_call x1, Pallas kernels, scatter_sums(): pl.pallas_call(functools.partial(scatter_kernel, slots, count, over_wsh),...  24.4 us
    pallas_call x1, Pallas kernels, attend_back(): pl.pallas_call(attend_back_kernel, out_shape=(jax.ShapeDtypeStruct(q.shap...  24.2 us
    pallas_call x1, Pallas kernels, attend(): pl.pallas_call(attend_kernel, out_shape=(jax.ShapeDtypeStruct(q.shape, bf...  20.9 us
    unnamed x145, local copies, waits for them, and re-layouts  14.3 us

profile of v4, /device:TPU:0, one launch (start us, length us, event | category | flops | bytes accessed | tf_op | source)
XLA Modules:
  0.0 475.1 jit_solution(13845529638544890134)
XLA Ops:
  9.3 1.7 convert_reduce_fusion
  12.2 40.9 %gather_all.1 = (bf16[2,2,2,4,24,1536]{5,4,3,2,1,0:T(8,128)(2,1)S(1)}, bf16[2,2,2,4,24,2432]{5,4,3,2,1,0:T(8,128)(2,1)S(1)}) custom-call(bf16[24,1536]{1,0:T(8,128)(2,1)S(1)} %copy-done.23, bf16[24,2432]{1,0:T(8,128)(2,1)S(1)} %fusion.62.refs_1_), custom_call_target="tpu_custom_call" | custom-call | tf_op jit(solution)/shard_map/gather_all/pallas_call | solution.py:200
  54.5 1.8 copy-done.28
  57.6 3.2 convolution_convert_fusion.2.refs_5_
  61.0 4.9 %fusion.21.refs_6_ = f32[1024,1536]{1,0:T(8,128)} fusion(bf16[768,1536]{1,0:T(8,128)(2,1)S(1)} %bitcast.143, bf16[1,1024,768]{2,1,0:T(8,128)(2,1)S(1)} %copy-done.33, f32[768]{0:T(1024)S(1)} %get-tuple-element.89, f32[1024]{0:T(1024)S(1)} %fusion.69, f32[1024]{0:T(1024)S(1)} %broadcast_multiply_fusion), kind=kOutput, calls=%fused_computation.45 | convolution fusion | flops 2419851264 | bytes 10234880 | tf_op jit(solution)/shard_map/dot_general | solution.py:1640
  65.9 98.7 %front.1 = (bf16[2,2,2,4,24,2304]{5,4,3,2,1,0:T(8,128)(2,1)}, bf16[2,2,2,4,24,768]{5,4,3,2,1,0:T(8,128)(2,1)S(1)}, bf16[2,2,2,4,24,768]{5,4,3,2,1,0:T(8,128)(2,1...) custom-call(bf16[24,2304]{1,0:T(8,128)(2,1)S(1)} %copy-done.20, ...), custom_call_target="tpu_custom_call" | custom-call | tf_op jit(solution)/shard_map/front/pallas_call | solution.py:1259
  165.8 2.7 fusion.40
  168.5 2.7 convolution_add_fusion.1
  171.2 20.9 %attend.1 = (bf16[4,256,192]{2,1,0:T(8,128)(2,1)S(1)}, f32[4,256,192]{2,1,0:T(8,128)S(1)}, f32[4,8,256]{2,1,0:T(8,128)S(1)}) custom-call(s32[4,2]{1,0:T(4,128)S(1)} %pad_add_fusion.bounds, bf16[4,256,192]{2,1,0:T(8,128)(2,1)S(1)} %get-tuple-element.50.q_ref, bf16[8,256,384]{2,1,0:T(8,128)(2,1)S(1)} %copy-done.1, s32[4,8,256]{2,1,0:T(8,128)S(1)} %add_add_fusion.4.spans_ref), custom_call_target="tpu_custom_call" | custom-call | tf_op jit(solution)/shard_map/attend/pallas_call | solution.py:693
  193.1 13.9 %join_heads.1 = (bf16[256,768]{1,0:T(8,128)(2,1)S(1)}, f32[256,768]{1,0:T(8,128)S(1)}, f32[256,768]{1,0:T(8,128)S(1)}, f32[8,128]{1,0:T(8,128)S(1)}) custom-call(bf16[4,256,192]{2,1,0:T(8,128)(2,1)S(1)} %get-tuple-element.52.o_ref, bf16[256,768]{1,0:T(8,128)(2,1)S(1)} %bitcast.131, bf16[768,768]{1,0:T(8,128)(2,1)S(1)} %bitcast.133), custom_call_target="tpu_custom_call" | custom-call | tf_op jit(solution)/shard_map/join_heads/pallas_call | solution.py:819
  209.7 2.0 fusion.84
  211.7 3.3 multiply_convert_fusion.2
  215.0 9.1 %multiply_convert_fusion = (bf16[256,3072]{1,0:T(8,128)(2,1)S(1)}, f32[256,3072]{1,0:T(8,128)S(1)}, f32[256,3072]{1,0:T(8,128)S(1)}) fusion(bf16[256,768]{1,0:T(8,128)(2,1)S(1)} %get-tuple-element.104, bf16[768,3072]{1,0:T(8,128)(2,1)S(1)} %bitcast.171), kind=kOutput, calls=%fused_computation.24 | convolution fusion | flops 1259077632 | bytes 12976128 | tf_op jit(solution)/shard_map/dot_general | solution.py:1674
  224.2 2.0 add_convert_fusion.1
  226.2 1.6 add_convert_fusion.3
  227.9 2.2 fusion.30
  231.3 1.7 convolution_convert_fusion.4
  237.6 2.2 pad_maximum_fusion.refs_1_
  239.8 3.6 convolution_convert_fusion
  244.9 44.7 %part_heads.1 = (f32[96,768]{1,0:T(8,128)S(1)}, f32[256,768]{1,0:T(8,128)S(1)}, bf16[256,768]{1,0:T(8,128)(2,1)S(1)}, bf16[4,256,192]{2,1,0:T(8,128)(2,1)S(1)}) custom-call(bf16[2,2,2,4,96,768]{5,4,3,2,1,0:T(8,128)(2,1)S(1)} %bitcast.130, f32[256,768]{1,0:T(8,128)S(1)} %add_add_fusion.3.refs_1_, f32[256,768]{1,0:T(8,128)S(1)} %copy-done.13, ...), custom_call_target="tpu_custom_call" | custom-call | tf_op jit(solution)/shard_map/part_heads/pallas_call | solution.py:914
  289.7 24.2 %attend_back.1 = (bf16[4,256,192]{2,1,0:T(8,128)(2,1)S(1)}, bf16[8,256,384]{2,1,0:T(8,128)(2,1)S(1)}) custom-call(s32[4,2]{1,0:T(4,128)S(1)} %pad_add_fusion.bounds, bf16[4,256,192]{2,1,0:T(8,128)(2,1)S(1)} %copy-done.8, bf16[8,256,384]{2,1,0:T(8,128)(2,1)S(1)} %copy-done.1, bf16[4,256,192]{2,1,0:T(8,128)(2,1)S(1)} %get-tuple-element.67.g_ref, ...), custom_call_target="tpu_custom_call" | custom-call | tf_op jit(solution)/shard_map/attend_back/pallas_call | solution.py:719
  317.4 102.7 %back.1 = (f32[24,3072]{1,0:T(8,128)}, f32[24,2304]{1,0:T(8,128)}, f32[24,768]{1,0:T(8,128)}, f32[24,768]{1,0:T(8,128)}, f32[24,2304]{1,0:T(8,128)}, /*index=5*/...) custom-call(bf16[2,2,2,4,24,3072]{5,4,3,2,1,0:T(8,128)(2,1)} %bitcast.146, ...), custom_call_target="tpu_custom_call" | custom-call | tf_op jit(solution)/shard_map/back/pallas_call | solution.py:1503
  420.2 3.7 fusion.51
  425.6 2.9 fusion.9
  428.5 2.7 fusion.7
  431.3 2.3 fusion.23
  433.8 1.7 copy.67
  435.5 4.7 convolution_convert_fusion.3
  440.3 1.7 pad_maximum_fusion.1.refs_0_
  442.0 24.4 %scatter_sums.1 = f32[24,1664]{1,0:T(8,128)} custom-call(bf16[2,2,2,4,24,1664]{5,4,3,2,1,0:T(8,128)(2,1)} %pad_maximum_fusion.1.refs_0_), custom_call_target="tpu_custom_call" | custom-call | tf_op jit(solution)/shard_map/scatter_sums/pallas_call | solution.py:413
  466.4 1.6 slice_reduce_fusion
  468.0 1.6 slice.91
  (214 shorter events, 35.0 us)
Async XLA Ops:
  0.6 10.4 %copy-start.32 = (bf16[1,1024,768]{2,1,0:T(8,128)(2,1)S(1)}, bf16[1,1024,768]{2,1,0:T(8,128)(2,1)}, u32[]{:S(2)}) copy-start(bf16[1,1024,768]{2,1,0:T(8,128)(2,1)} %param.17) | copy-start | bytes 4718596
  0.7 11.5 %copy-start.23 = (bf16[24,1536]{1,0:T(8,128)(2,1)S(1)}, bf16[24,1536]{1,0:T(8,128)(2,1)}, u32[]{:S(2)}) copy-start(bf16[24,1536]{1,0:T(8,128)(2,1)} %refs_0_.2) | copy-start | bytes 221188
  0.7 11.2 %copy-start.43 = (bf16[24,2304]{1,0:T(8,128)(2,1)S(1)}, bf16[24,2304]{1,0:T(8,128)(2,1)}, u32[]{:S(2)}) copy-start(bf16[24,2304]{1,0:T(8,128)(2,1)} %param.21) | copy-start | bytes 331780
  4.9 51.7 %copy-start.54 = (f32[256]{0:T(256)}, f32[256]{0:T(256)S(1)}, u32[]{:S(2)}) copy-start(f32[256]{0:T(256)S(1)} %broadcast_multiply_fusion.2) | copy-start | bytes 3076
  6.2 50.5 %copy-start.56 = (f32[256]{0:T(256)}, f32[256]{0:T(256)S(1)}, u32[]{:S(2)}) copy-start(f32[256]{0:T(256)S(1)} %fusion.76) | copy-start | bytes 3076
  9.3 47.4 %copy-start = (bf16[1,256,768]{2,1,0:T(8,128)(2,1)S(1)}, bf16[1,256,768]{2,1,0:T(8,128)(2,1)}, u32[]{:S(2)}) copy-start(bf16[1,256,768]{2,1,0:T(8,128)(2,1)} %param.16) | copy-start | bytes 1179652
  11.6 44.9 %copy-start.52 = (f32[1024]{0:T(1024)}, f32[1024]{0:T(1024)S(1)}, u32[]{:S(2)}) copy-start(f32[1024]{0:T(1024)S(1)} %fusion.8) | copy-start | bytes 12292
  11.7 49.2 %copy-start.48 = (f32[1024]{0:T(1024)}, f32[1024]{0:T(1024)S(1)}, u32[]{:S(2)}) copy-start(f32[1024]{0:T(1024)S(1)} %fusion.69) | copy-start | bytes 12292
  11.8 54.1 %copy-start.21 = (f32[8,384]{1,0:T(8,128)}, f32[8,384]{1,0:T(8,128)S(1)}, u32[]{:S(2)}) copy-start(f32[8,384]{1,0:T(8,128)S(1)} %select_maximum_fusion.refs_8_.refs_10_) | copy-start | bytes 36868
  11.9 159.3 %copy-start.15 = (s32[4,8,256]{2,1,0:T(8,128)}, s32[4,8,256]{2,1,0:T(8,128)S(1)}, u32[]{:S(2)}) copy-start(s32[4,8,256]{2,1,0:T(8,128)S(1)} %add_add_fusion.4.spans_ref) | copy-start | bytes 98308
  12.2 53.7 %copy-start.4 = (f32[1024,128]{1,0:T(8,128)}, f32[1024,128]{1,0:T(8,128)S(1)}, u32[]{:S(2)}) copy-start(f32[1024,128]{1,0:T(8,128)S(1)} %pad.19.refs_9_.refs_11_) | copy-start | bytes 1572868
  165.2 26.9 %copy-start.5 = (bf16[2,2,2,4,24,768]{5,4,3,2,1,0:T(8,128)(2,1)}, bf16[2,2,2,4,24,768]{5,4,3,2,1,0:T(8,128)(2,1)S(1)}, u32[]{:S(2)}) copy-start(bf16[2,2,2,4,24,768]{5,4,3,2,1,0:T(8,128)(2,1)S(1)} %get-tuple-element.55) | copy-start | bytes 3538948
  165.2 26.9 %copy-start.7 = (bf16[4,256,192]{2,1,0:T(8,128)(2,1)}, bf16[4,256,192]{2,1,0:T(8,128)(2,1)S(1)}, u32[]{:S(2)}) copy-start(bf16[4,256,192]{2,1,0:T(8,128)(2,1)S(1)} %get-tuple-element.50.q_ref) | copy-start | bytes 1179652
  165.2 27.9 %copy-start.2 = (bf16[2,2,2,4,24,768]{5,4,3,2,1,0:T(8,128)(2,1)}, bf16[2,2,2,4,24,768]{5,4,3,2,1,0:T(8,128)(2,1)S(1)}, u32[]{:S(2)}) copy-start(bf16[2,2,2,4,24,768]{5,4,3,2,1,0:T(8,128)(2,1)S(1)} %get-tuple-element.53) | copy-start | bytes 3538948
  165.2 5.9 %copy-start.1 = (bf16[8,256,384]{2,1,0:T(8,128)(2,1)S(1)}, bf16[8,256,384]{2,1,0:T(8,128)(2,1)}, u32[]{:S(2)}) copy-start(bf16[8,256,384]{2,1,0:T(8,128)(2,1)} %get-tuple-element.51.kv_ref) | copy-start | bytes 4718596
  165.8 26.3 %copy-start.58 = (bf16[1,768]{1,0:T(2,128)(2,1)}, bf16[1,768]{1,0:T(2,128)(2,1)S(1)}, u32[]{:S(2)}) copy-start(bf16[1,768]{1,0:T(2,128)(2,1)S(1)} %get-tuple-element.108) | copy-start | bytes 4612
  193.1 13.9 %copy-start.26 = (f32[4,8,256]{2,1,0:T(8,128)}, f32[4,8,256]{2,1,0:T(8,128)S(1)}, u32[]{:S(2)}) copy-start(f32[4,8,256]{2,1,0:T(8,128)S(1)} %get-tuple-element.69.log_ref) | copy-start | bytes 98308
  211.6 12.5 %slice-start = ((s8[4718592]{0:T(1024)(128)(4,1)}), s8[4194304]{0:T(1024)(128)(4,1)S(1)}, s32[]{:S(2)}) async-start(s8[4718592]{0:T(1024)(128)(4,1)} %bitcast.165), calls=%async_computation | async-start | bytes 8388608
  215.0 9.2 %copy-start.37 = (bf16[1,256,768]{2,1,0:T(8,128)(2,1)S(1)}, bf16[1,256,768]{2,1,0:T(8,128)(2,1)}, u32[]{:S(2)}) copy-start(bf16[1,256,768]{2,1,0:T(8,128)(2,1)} %param.30) | copy-start | bytes 1179652
  215.0 9.2 %slice-start.1 = ((s8[4718592]{0:T(1024)(128)(4,1)}), s8[524288]{0:T(1024)(128)(4,1)S(1)}, s32[]{:S(2)}) async-start(s8[4718592]{0:T(1024)(128)(4,1)} %bitcast.165), calls=%async_computation.1 | async-start | bytes 1048576
  244.9 44.7 %copy-start.8 = (bf16[4,256,192]{2,1,0:T(8,128)(2,1)S(1)}, bf16[4,256,192]{2,1,0:T(8,128)(2,1)}, u32[]{:S(2)}) copy-start(bf16[4,256,192]{2,1,0:T(8,128)(2,1)} %copy-done.7) | copy-start | bytes 1179652
  244.9 44.7 %copy-start.11 = (f32[4,256,192]{2,1,0:T(8,128)S(1)}, f32[4,256,192]{2,1,0:T(8,128)}, u32[]{:S(2)}) copy-start(f32[4,256,192]{2,1,0:T(8,128)} %copy-done.10) | copy-start | bytes 2359300
  244.9 44.7 %copy-start.16 = (s32[4,8,256]{2,1,0:T(8,128)S(1)}, s32[4,8,256]{2,1,0:T(8,128)}, u32[]{:S(2)}) copy-start(s32[4,8,256]{2,1,0:T(8,128)} %copy-done.15) | copy-start | bytes 98308
  244.9 44.7 %copy-start.27 = (f32[4,8,256]{2,1,0:T(8,128)S(1)}, f32[4,8,256]{2,1,0:T(8,128)}, u32[]{:S(2)}) copy-start(f32[4,8,256]{2,1,0:T(8,128)} %copy-done.26) | copy-start | bytes 98308
  317.4 102.7 %copy-start.47 = (f32[768]{0:T(1024)S(1)}, f32[768]{0:T(1024)}, u32[]{:S(2)}) copy-start(f32[768]{0:T(1024)} %copy-done.46) | copy-start | bytes 9220
  317.4 102.7 %copy-start.55 = (f32[256]{0:T(256)S(1)}, f32[256]{0:T(256)}, u32[]{:S(2)}) copy-start(f32[256]{0:T(256)} %copy-done.54) | copy-start | bytes 3076
  440.2 29.3 %copy-start.38 = (bf16[1024,768]{1,0:T(8,128)(2,1)S(1)}, bf16[1024,768]{1,0:T(8,128)(2,1)}, u32[]{:S(2)}) copy-start(bf16[1024,768]{1,0:T(8,128)(2,1)} %get-tuple-element.61) | copy-start | bytes 4718596
  442.0 28.7 %copy-start.42 = (f32[24,2304]{1,0:T(8,128)S(1)}, f32[24,2304]{1,0:T(8,128)}, u32[]{:S(2)}) copy-start(f32[24,2304]{1,0:T(8,128)} %get-tuple-element.143) | copy-start | bytes 663556
  442.0 29.4 %copy-start.45 = (f32[24,768]{1,0:T(8,128)S(1)}, f32[24,768]{1,0:T(8,128)}, u32[]{:S(2)}) copy-start(f32[24,768]{1,0:T(8,128)} %get-tuple-element.144) | copy-start | bytes 221188
  442.0 30.0 %copy-start.41 = (f32[24,2304]{1,0:T(8,128)S(1)}, f32[24,2304]{1,0:T(8,128)}, u32[]{:S(2)}) copy-start(f32[24,2304]{1,0:T(8,128)} %get-tuple-element.147) | copy-start | bytes 663556
  442.0 30.7 %copy-start.44 = (f32[24,768]{1,0:T(8,128)S(1)}, f32[24,768]{1,0:T(8,128)}, u32[]{:S(2)}) copy-start(f32[24,768]{1,0:T(8,128)} %get-tuple-element.149) | copy-start | bytes 221188
  442.0 31.3 %copy-start.40 = (f32[24,3072]{1,0:T(8,128)S(1)}, f32[24,3072]{1,0:T(8,128)}, u32[]{:S(2)}) copy-start(f32[24,3072]{1,0:T(8,128)} %get-tuple-element.150) | copy-start | bytes 884740
  (36 other events, 106.5 us)
